TPU v7x, 512 devices: a whole 4x8x8 slice. The times are simulated.
512 devices in a mesh: ctx: 128 (over z_hi, x, y), fsdp: 4 (over z_lo, core).
Axes of the slice: x: 4, y: 8, z: 8 (z_hi: 4, z_lo: 2; z = z_hi * 2 + z_lo), core: 2. Of those that a mesh axis runs over, the one named last changes fastest.
Arguments:
- query_in: bfloat16 [4, 16384, 2048], P('fsdp', 'ctx'), may hold values from -6 to 6
- key_in: bfloat16 [4, 16384, 2048], P('fsdp', 'ctx'), may hold values from -6 to 6
- value_in: bfloat16 [4, 16384, 2048], P('fsdp', 'ctx'), may hold values from -6 to 6
- feature_taps: float32 [3, 3, 2048], replicated, may hold values from -3 to 3
- decay_rate: float32 [128, 16], replicated, as said below
- residues: float32 [128, 16], replicated, may hold values from -3 to 3
- skip_gain: float32 [2048], replicated, may hold values from 0.5 to 1.5
- out_weight: bfloat16 [2048, 2048], P('fsdp'), may hold values from -0.1875 to 0.1875
Outputs:
- block_out: bfloat16 [4, 16384, 2048], P('fsdp', 'ctx')
Inputs may be any that keep to these rules, and one draw needn't show every extreme that they name: `decay_rate`: every rate is positive.
All inputs are finite; a program needn't handle non-finite values.
Results may differ from a plain program's by a relative error of at most 0.0062.
Values may be sent and summed in bfloat16 or wider, within the bound.
A program may use at most 128 MiB of HBM per device.

v0:
```python
import math

import jax
import jax.numpy as jnp
from jax import lax
from jax.sharding import PartitionSpec as P

GROUP = 16
FEAT = 3


exact_precision = lax.Precision.HIGHEST
split_precision = lax.Precision.HIGH


def shifted(shard, axis, by):
    count = lax.axis_size(axis)
    pairs = [(i, i + by) for i in range(count) if 0 <= i + by < count]
    return lax.ppermute(shard, axis, pairs)


def featurize(rows, tail, taps_one):
    values = jnp.concatenate([tail, rows], axis=0).astype(jnp.float32)
    count = rows.shape[0]
    total = taps_one[0] * values[FEAT - 1 :]
    for offset in range(1, FEAT):
        total = total + taps_one[offset] * values[FEAT - 1 - offset : FEAT - 1 - offset + count]
    return total


def mode_tables(rate_rows, residue_rows, width):
    positions = jnp.arange(width).astype(jnp.float32)
    scale = residue_rows * jnp.sqrt(-jnp.expm1(-2.0 * rate_rows))
    powers = jnp.exp(-rate_rows[:, :, None] * positions)
    kernel = jnp.einsum("gm,gmt->gt", scale, powers, precision=exact_precision)
    lagged = jnp.exp(-rate_rows[:, :, None] * (positions + 1.0)) * scale[:, :, None]
    closing = jnp.exp(-rate_rows[:, :, None] * (width - 1.0 - positions))
    return (kernel, lagged, closing)


def lower_toeplitz(kernel):
    groups_here, width = kernel.shape
    extended = jnp.concatenate([jnp.zeros((groups_here, width), jnp.float32), kernel], axis=1)
    reversed_ext = extended[:, ::-1]
    tiled = jnp.tile(reversed_ext, (1, width))[:, : width * (2 * width - 1)]
    framed = tiled.reshape(groups_here, width, 2 * width - 1)
    return framed[:, :, width - 1 : 2 * width - 1]


def block_terms(operands):
    signal, kernel, closing = operands
    toeplitz = lower_toeplitz(kernel)
    inner = jnp.einsum("gij,gcbj->gcbi", toeplitz, signal, precision=split_precision)
    ending = jnp.einsum("gcbj,gmj->gcbm", signal, closing, precision=split_precision)
    return (inner, ending)


def spanned_terms(signal, kernel, closing):
    groups_here = signal.shape[0]
    width = signal.shape[-1]
    per_span = math.gcd(groups_here, max(1, (1 << 20) // (width * width)))
    outer = groups_here // per_span

    def reshape_front(array):
        return array.reshape((outer, per_span) + array.shape[1:])

    inner, ending = lax.map(
        block_terms, (reshape_front(signal), reshape_front(kernel), reshape_front(closing))
    )
    return (inner.reshape(signal.shape), ending.reshape((groups_here,) + ending.shape[2:]))


def channel_conv(signal, rate_rows, residue_rows):
    chans_here, length = signal.shape
    width = min(128, length)
    blocks = length // width
    groups_here = chans_here // GROUP
    values = signal.astype(jnp.float32).reshape(groups_here, GROUP, blocks, width)
    kernel, lagged, closing = mode_tables(rate_rows, residue_rows, width)
    inner, ending = spanned_terms(values, kernel, closing)
    factor = jnp.broadcast_to(jnp.exp(-rate_rows * width)[:, None, None, :], ending.shape)

    def combine(earlier, later):
        return (earlier[0] * later[0], earlier[1] * later[0] + later[1])

    through = lax.associative_scan(combine, (factor, ending), axis=2)[1]
    entering = jnp.concatenate([jnp.zeros_like(through[:, :, :1]), through[:, :, :-1]], axis=2)
    crossing = jnp.einsum("gcbm,gmi->gcbi", entering, lagged, precision=split_precision)
    return (inner + crossing).reshape(chans_here, length)


def local(query_in, key_in, value_in, feature_taps, decay_rate, residues, skip_gain, out_weight):
    query_rows = query_in[0]
    key_rows = key_in[0]
    value_rows = value_in[0]
    rows_here = query_rows.shape[0]
    keep = FEAT - 1
    tails = shifted(
        (
            query_rows[rows_here - keep :],
            key_rows[rows_here - keep :],
            value_rows[rows_here - keep :],
        ),
        "ctx",
        1,
    )
    featured_q = featurize(query_rows, tails[0], feature_taps[0])
    featured_k = featurize(key_rows, tails[1], feature_taps[1])
    featured_v = featurize(value_rows, tails[2], feature_taps[2])
    kv_round = lax.optimization_barrier((featured_k * featured_v).astype(jnp.bfloat16))
    spread = lax.all_to_all(jnp.transpose(kv_round), "ctx", split_axis=0, concat_axis=1, tiled=True)
    groups_here = spread.shape[0] // GROUP
    first_group = lax.axis_index("ctx") * groups_here
    rate_rows = lax.dynamic_slice_in_dim(decay_rate, first_group, groups_here, 0)
    residue_rows = lax.dynamic_slice_in_dim(residues, first_group, groups_here, 0)
    filtered = channel_conv(spread, rate_rows, residue_rows).astype(jnp.bfloat16)
    convolved = jnp.transpose(
        lax.all_to_all(filtered, "ctx", split_axis=1, concat_axis=0, tiled=True)
    )
    convolved = lax.optimization_barrier(convolved)
    gated = (
        featured_q * (convolved.astype(jnp.float32) + skip_gain * kv_round.astype(jnp.float32))
    ).astype(jnp.bfloat16)
    block_out = jnp.dot(
        gated,
        lax.all_gather(out_weight, "fsdp", axis=0, tiled=True),
        preferred_element_type=jnp.float32,
    ).astype(jnp.bfloat16)
    return block_out[None]


def solution(mesh):
    return jax.shard_map(
        local,
        mesh=mesh,
        in_specs=(
            P("fsdp", "ctx", None),
            P("fsdp", "ctx", None),
            P("fsdp", "ctx", None),
            P(),
            P(),
            P(),
            P(),
            P("fsdp", None),
        ),
        out_specs=P("fsdp", "ctx", None),
        check_vma=False,
    )
```

profile of v0, /device:TPU:199, one launch (start us, length us, event | category | flops | bytes accessed | tf_op | source)
XLA Modules:
  0.0 188.2 jit_solution(14850674802791064342)
XLA Ops:
  6.5 0.7 all-gather.2.cloned.1.call-update
  8.1 3.2 %collective-permute-start.1 = (bf16[2,2048]{0,1:T(8,128)(2,1)S(1)}, bf16[2,2048]{0,1:T(8,128)(2,1)S(1)}, u32[]{:S(2)}, u32[]{:S(2)}) collective-permute-start(bf16[2,2048]{0,1:T(8,128)(2,1)S(1)} %slice_bitcast_fusion.1), channel_id=1, source_target_pairs={{0,4},{4,8},{8,12},{12,16},{16,20},{20,24},{24,28},{28,32},{32,36}... | collective-permute-start | bytes 24584 | tf_op jit(solution)/shard_map/ppermute | solution.py:19
  11.8 3.2 %collective-permute-start.2 = (bf16[2,2048]{0,1:T(8,128)(2,1)S(1)}, bf16[2,2048]{0,1:T(8,128)(2,1)S(1)}, u32[]{:S(2)}, u32[]{:S(2)}) collective-permute-start(bf16[2,2048]{0,1:T(8,128)(2,1)S(1)} %slice_bitcast_fusion), channel_id=1, source_target_pairs={{0,4},{4,8},{8,12},{12,16},{16,20},{20,24},{24,28},{28,32},{32,36}... | collective-permute-start | bytes 24584 | tf_op jit(solution)/shard_map/ppermute | solution.py:19
  15.3 9.5 %collective-permute-done.1 = bf16[2,2048]{0,1:T(8,128)(2,1)S(1)} collective-permute-done((bf16[2,2048]{0,1:T(8,128)(2,1)S(1)}, bf16[2,2048]{0,1:T(8,128)(2,1)S(1)}, u32[]{:S(2)}, u32[]{:S(2)}) %collective-permute-start.1) | collective-permute-done | bytes 8224 | tf_op jit(solution)/shard_map/ppermute | solution.py:19
  24.9 0.4 maximum_convert_fusion.1
  25.3 10.8 %collective-permute-done.2 = bf16[2,2048]{0,1:T(8,128)(2,1)S(1)} collective-permute-done((bf16[2,2048]{0,1:T(8,128)(2,1)S(1)}, bf16[2,2048]{0,1:T(8,128)(2,1)S(1)}, u32[]{:S(2)}, u32[]{:S(2)}) %collective-permute-start.2) | collective-permute-done | bytes 8224 | tf_op jit(solution)/shard_map/ppermute | solution.py:19
  36.1 0.4 maximum_convert_fusion.2
  36.5 3.7 %fusion.4 = bf16[128,2048]{0,1:T(8,128)(2,1)} fusion(f32[130,2048]{0,1:T(8,128)S(1)} %maximum_convert_fusion.2, f32[130,2048]{0,1:T(8,128)S(1)} %maximum_convert_fusion.1, f32[2048]{0:T(1024)S(1)} %bitcast.73, f32[2048]{0:T(1024)S(1)} %bitcast.74, f32[2048]{0:T(1024)S(1)} %bitcast.69, f32[2048]{0:T(1024)S(1)} %bitcast.70, f32[2048]{0:T(1024)S(1)} %bitcast.71, ...), kind=kLoop, calls=%fused_computation.7 | loop fusion | flops 3145728 | bytes 6864896 | tf_op jit(solution)/shard_map/convert_element_type | solution.py:110
  40.2 33.8 %all-to-all-start = ((bf16[128,16,128]{2,1,0:T(8,128)(2,1)}), bf16[128,16,128]{2,1,0:T(8,128)(2,1)S(1)}, u32[]{:S(2)}, u32[]{:S(2)}) async-start(bf16[128,16,128]{2,1,0:T(8,128)(2,1)} %bitcast.16), calls=%async_computation | async-start | bytes 1048576 | tf_op jit(solution)/shard_map/all_to_all | solution.py:111
  75.3 14.3 %all-to-all-done = bf16[128,16,128]{2,1,0:T(8,128)(2,1)S(1)} async-done(((bf16[128,16,128]{2,1,0:T(8,128)(2,1)}), bf16[128,16,128]{2,1,0:T(8,128)(2,1)S(1)}, u32[]{:S(2)}, u32[]{:S(2)}) %all-to-all-start) | async-done | bytes 524320 | tf_op jit(solution)/shard_map/all_to_all | solution.py:111
  89.7 0.4 fusion.14
  90.1 0.5 copy.66
  92.4 20.0 %pad.110 = f32[1,16,128,16]{3,1,2,0:T(8,128)} pad(f32[1,16,64,16]{3,1,2,0:T(8,128)S(1)} %add.157, f32[]{:T(128)} %constant.16.clone.1), padding=0_0_0x0_0_0x1_0_1x0_0_0 | pad | bytes 196612
  112.6 0.5 pad.78
  113.1 0.7 copy-done
  114.1 0.5 fusion.16
  114.6 0.9 fusion.1
  115.5 1.1 copy.64
  116.7 13.3 %all-to-all-start.1 = ((bf16[16,128,128]{2,0,1:T(8,128)(2,1)}), bf16[16,128,128]{2,0,1:T(8,128)(2,1)S(1)}, u32[]{:S(2)}, u32[]{:S(2)}) async-start(bf16[16,128,128]{2,0,1:T(8,128)(2,1)} %copy.64), calls=%async_computation.1 | async-start | bytes 1048576 | tf_op jit(solution)/shard_map/all_to_all | solution.py:118
  130.4 3.1 %collective-permute-start = (bf16[2,2048]{0,1:T(8,128)(2,1)S(1)}, bf16[2,2048]{0,1:T(8,128)(2,1)S(1)}, u32[]{:S(2)}, u32[]{:S(2)}) collective-permute-start(bf16[2,2048]{0,1:T(8,128)(2,1)S(1)} %slice_bitcast_fusion.2), channel_id=1, source_target_pairs={{0,4},{4,8},{8,12},{12,16},{16,20},{20,24},{24,28},{28,32},{32,36}... | collective-permute-start | bytes 24584 | tf_op jit(solution)/shard_map/ppermute | solution.py:19
  133.5 21.2 %collective-permute-done = bf16[2,2048]{0,1:T(8,128)(2,1)S(1)} collective-permute-done((bf16[2,2048]{0,1:T(8,128)(2,1)S(1)}, bf16[2,2048]{0,1:T(8,128)(2,1)S(1)}, u32[]{:S(2)}, u32[]{:S(2)}) %collective-permute-start) | collective-permute-done | bytes 8224 | tf_op jit(solution)/shard_map/ppermute | solution.py:19
  154.7 0.4 maximum_convert_fusion
  155.2 19.1 %all-gather.2.cloned.1.call-done = bf16[2048,2048]{1,0:T(8,128)(2,1)} async-done(((bf16[512,2048]{1,0:T(8,128)(2,1)}), bf16[2048,2048]{1,0:T(8,128)(2,1)}) %all-gather.2.cloned.1.call-update) | async-done | bytes 8388624 | tf_op jit(solution)/shard_map/all_gather | solution.py:126
  174.3 7.1 %fusion = bf16[1,128,2048]{2,1,0:T(8,128)(2,1)} fusion(bf16[2048,2048]{1,0:T(8,128)(2,1)} %all-gather.2.cloned.1.call-done, f32[130,2048]{0,1:T(8,128)S(1)} %maximum_convert_fusion, bf16[128,2048]{0,1:T(8,128)(2,1)} %fusion.4, bf16[128,2048]{0,1:T(8,128)(2,1)S(1)} %bitcast.67, f32[2048]{0:T(1024)S(1)} %copy-done.7, f32[2048]{0:T(1024)S(1)} %bitcast.76, ...), kind=kOutput, calls=%fused_computation.1 | convolution fusion | flops 1076887552 | bytes 13139968 | tf_op jit(solution)/shard_map/dot_general | solution.py:124
  (79 shorter events, 5.2 us)
Async XLA Ops:
  6.5 1.0 copy-start.1
  6.5 4.7 %copy-start.2 = (bf16[1,128,2048]{2,1,0:T(8,128)(2,1)S(1)}, bf16[1,128,2048]{2,1,0:T(8,128)(2,1)}, u32[]{:S(2)}) copy-start(bf16[1,128,2048]{2,1,0:T(8,128)(2,1)} %param.10) | copy-start | bytes 1572868
  6.5 167.7 %all-gather.2.cloned.1.call-start = ((), (), s32[]{:S(2)}) async-start(), calls=%async_computation.2 | async-start | bytes 10485760 | tf_op jit(solution)/shard_map/all_gather | solution.py:126
  7.6 7.4 %copy-start.4 = (f32[3,3,2048]{2,1,0:T(4,128)S(1)}, f32[3,3,2048]{2,1,0:T(4,128)}, u32[]{:S(2)}) copy-start(f32[3,3,2048]{2,1,0:T(4,128)} %param.11) | copy-start | bytes 221188
  7.6 7.5 %copy-start.5 = (f32[128,16]{0,1:T(8,128)S(1)}, f32[128,16]{0,1:T(8,128)}, u32[]{:S(2)}) copy-start(f32[128,16]{0,1:T(8,128)} %param.12) | copy-start | bytes 24580
  7.6 7.5 %copy-start.6 = (f32[128,16]{0,1:T(8,128)S(1)}, f32[128,16]{0,1:T(8,128)}, u32[]{:S(2)}) copy-start(f32[128,16]{0,1:T(8,128)} %param.13) | copy-start | bytes 24580
  8.1 16.8 %collective-permute-start.1 = (bf16[2,2048]{0,1:T(8,128)(2,1)S(1)}, bf16[2,2048]{0,1:T(8,128)(2,1)S(1)}, u32[]{:S(2)}, u32[]{:S(2)}) collective-permute-start(bf16[2,2048]{0,1:T(8,128)(2,1)S(1)} %slice_bitcast_fusion.1), channel_id=1, source_target_pairs={{0,4},{4,8},{8,12},{12,16},{16,20},{20,24},{24,28},{28,32},{32,36}... | collective-permute-start | bytes 24584 | tf_op jit(solution)/shard_map/ppermute | solution.py:19
  11.8 24.3 %collective-permute-start.2 = (bf16[2,2048]{0,1:T(8,128)(2,1)S(1)}, bf16[2,2048]{0,1:T(8,128)(2,1)S(1)}, u32[]{:S(2)}, u32[]{:S(2)}) collective-permute-start(bf16[2,2048]{0,1:T(8,128)(2,1)S(1)} %slice_bitcast_fusion), channel_id=1, source_target_pairs={{0,4},{4,8},{8,12},{12,16},{16,20},{20,24},{24,28},{28,32},{32,36}... | collective-permute-start | bytes 24584 | tf_op jit(solution)/shard_map/ppermute | solution.py:19
  40.2 49.5 %all-to-all-start = ((bf16[128,16,128]{2,1,0:T(8,128)(2,1)}), bf16[128,16,128]{2,1,0:T(8,128)(2,1)S(1)}, u32[]{:S(2)}, u32[]{:S(2)}) async-start(bf16[128,16,128]{2,1,0:T(8,128)(2,1)} %bitcast.16), calls=%async_computation | async-start | bytes 1048576 | tf_op jit(solution)/shard_map/all_to_all | solution.py:111
  112.6 1.3 copy-start
  114.6 15.3 %copy-start.3 = (bf16[1,128,2048]{2,1,0:T(8,128)(2,1)S(1)}, bf16[1,128,2048]{2,1,0:T(8,128)(2,1)}, u32[]{:S(2)}) copy-start(bf16[1,128,2048]{2,1,0:T(8,128)(2,1)} %param.8) | copy-start | bytes 1572868
  116.7 38.5 %all-to-all-start.1 = ((bf16[16,128,128]{2,0,1:T(8,128)(2,1)}), bf16[16,128,128]{2,0,1:T(8,128)(2,1)S(1)}, u32[]{:S(2)}, u32[]{:S(2)}) async-start(bf16[16,128,128]{2,0,1:T(8,128)(2,1)} %copy.64), calls=%async_computation.1 | async-start | bytes 1048576 | tf_op jit(solution)/shard_map/all_to_all | solution.py:118
  130.2 44.0 %copy-start.7 = (f32[2048]{0:T(1024)S(1)}, f32[2048]{0:T(1024)}, u32[]{:S(2)}) copy-start(f32[2048]{0:T(1024)} %param.14) | copy-start | bytes 24580
  130.4 24.3 %collective-permute-start = (bf16[2,2048]{0,1:T(8,128)(2,1)S(1)}, bf16[2,2048]{0,1:T(8,128)(2,1)S(1)}, u32[]{:S(2)}, u32[]{:S(2)}) collective-permute-start(bf16[2,2048]{0,1:T(8,128)(2,1)S(1)} %slice_bitcast_fusion.2), channel_id=1, source_target_pairs={{0,4},{4,8},{8,12},{12,16},{16,20},{20,24},{24,28},{28,32},{32,36}... | collective-permute-start | bytes 24584 | tf_op jit(solution)/shard_map/ppermute | solution.py:19
Sparse Core Ops, SparseCore 0:
  9.5 164.7 all-gather.1
where the time goes:
time: 189 us; the launch traced here: 188 us
  waiting for transfers between devices  75.7 us (40%)
  starting transfers between devices  56.6 us (30%)
  local copies, waits for them, and re-layouts  26.9 us (14%)
  between operations  14 us (7%)
  matrix products  9.12 us (5%)
  other arithmetic  5.98 us (3%)
    ppermute x3, waiting for transfers between devices, shifted(): return lax.ppermute(shard, axis, pairs)  41.6 us
    all_to_all x1, starting transfers between devices, local(): lax.all_to_all(jnp.transpose(kv_round), 'ctx', split_axis=0, concat_axis=...  33.8 us
    unnamed x22, local copies, waits for them, and re-layouts  22.1 us
    all_gather x1, waiting for transfers between devices, local(): lax.all_gather(out_weight, 'fsdp', axis=0, tiled=True)  19.1 us
    all_to_all x1, waiting for transfers between devices, local(): lax.all_to_all(jnp.transpose(kv_round), 'ctx', split_axis=0, concat_axis=...  14.3 us
    all_to_all x1, starting transfers between devices, local(): lax.all_to_all(filtered, 'ctx', split_axis=1, concat_axis=0, tiled=True)  13.3 us
    ppermute x3, starting transfers between devices, shifted(): return lax.ppermute(shard, axis, pairs)  9.51 us
    dot_general x1, matrix products, local(): jnp.dot(gated, lax.all_gather(out_weight, 'fsdp', axis=0, tiled=True), pr...  7.12 us
  transfers between devices with their start and end apart: 6, of which 5 were waited for; matrix products, arithmetic and copies ran while one was open for 18% of the time, Pallas kernels for 0%

commit v1 on v0

v1 whole, which is shorter than its diff:
```python
import jax
import jax.numpy as jnp
from jax import lax
from jax.sharding import PartitionSpec as P

GROUP = 16
FEAT = 3

exact_precision = lax.Precision.HIGHEST


def shifted(shard, axis, by):
    count = lax.axis_size(axis)
    pairs = [(i, i + by) for i in range(count) if 0 <= i + by < count]
    return lax.ppermute(shard, axis, pairs)


def featurize(rows, tail, taps_one):
    values = jnp.concatenate([tail, rows], axis=0).astype(jnp.float32)
    count = rows.shape[0]
    total = taps_one[0] * values[FEAT - 1 :]
    for offset in range(1, FEAT):
        total = total + taps_one[offset] * values[FEAT - 1 - offset : FEAT - 1 - offset + count]
    return total


def split_bf16(values):
    high = values.astype(jnp.bfloat16)
    low = (values - high.astype(jnp.float32)).astype(jnp.bfloat16)
    return high, low


def two_pass(spec, table, signal):
    high, low = split_bf16(table)
    first = jnp.einsum(spec, high, signal, preferred_element_type=jnp.float32)
    return first + jnp.einsum(spec, low, signal, preferred_element_type=jnp.float32)


def toeplitz(kernel):
    width = kernel.shape[1]
    lag = lax.optimization_barrier(jnp.arange(width, dtype=jnp.int32))
    diff = lag[:, None] - lag[None, :]
    onehot = (lag[:, None, None] == diff[None, :, :]).astype(jnp.bfloat16)
    high, low = split_bf16(kernel)
    first = jnp.einsum("gs,sij->gij", high, onehot, preferred_element_type=jnp.float32)
    return first + jnp.einsum("gs,sij->gij", low, onehot, preferred_element_type=jnp.float32)


def local(query_in, key_in, value_in, feature_taps, decay_rate, residues, skip_gain, out_weight):
    query_rows = query_in[0]
    key_rows = key_in[0]
    value_rows = value_in[0]
    rows_here, chans = query_rows.shape
    keep = FEAT - 1
    tails = shifted(
        jnp.concatenate(
            [query_rows[rows_here - keep :], key_rows[rows_here - keep :], value_rows[rows_here - keep :]],
            axis=0,
        ),
        "ctx",
        1,
    )
    featured_q = featurize(query_rows, tails[0:keep], feature_taps[0])
    featured_k = featurize(key_rows, tails[keep : 2 * keep], feature_taps[1])
    featured_v = featurize(value_rows, tails[2 * keep :], feature_taps[2])
    kv_round = (featured_k * featured_v).astype(jnp.bfloat16)

    groups = chans // GROUP
    width = rows_here
    kv_grouped = kv_round.reshape(width, groups, GROUP)

    positions = jnp.arange(width, dtype=jnp.float32)
    scale = residues * jnp.sqrt(-jnp.expm1(-2.0 * decay_rate))
    powers = jnp.exp(-decay_rate[:, :, None] * positions)
    kernel = jnp.einsum("gm,gmt->gt", scale, powers, precision=exact_precision)
    closing = jnp.exp(-decay_rate[:, :, None] * (width - 1.0 - positions))
    lagged = jnp.exp(-decay_rate[:, :, None] * (positions + 1.0)) * scale[:, :, None]

    inner = two_pass("gij,jgc->igc", toeplitz(kernel), kv_grouped)
    ending = two_pass("gnj,jgc->gnc", closing, kv_grouped)

    count = lax.axis_size("ctx")
    entering = shifted(ending, "ctx", 1)
    if count > 2:
        step_decay = jnp.exp(-decay_rate * float(width))[:, :, None]
        entering = entering + step_decay * shifted(ending, "ctx", 2)
        span = 2
        while span < count:
            decay = jnp.exp(-decay_rate * float(width * span))[:, :, None]
            entering = entering + decay * shifted(entering, "ctx", span)
            span *= 2
    crossing = jnp.einsum("gni,gnc->igc", lagged, entering, precision=exact_precision)
    convolved = (inner + crossing).reshape(width, chans).astype(jnp.bfloat16)

    gated = (
        featured_q * (convolved.astype(jnp.float32) + skip_gain * kv_round.astype(jnp.float32))
    ).astype(jnp.bfloat16)
    block_out = jnp.dot(
        gated,
        lax.all_gather(out_weight, "fsdp", axis=0, tiled=True),
        preferred_element_type=jnp.float32,
    ).astype(jnp.bfloat16)
    return block_out[None]


def solution(mesh):
    return jax.shard_map(
        local,
        mesh=mesh,
        in_specs=(
            P("fsdp", "ctx", None),
            P("fsdp", "ctx", None),
            P("fsdp", "ctx", None),
            P(),
            P(),
            P(),
            P(),
            P("fsdp", None),
        ),
        out_specs=P("fsdp", "ctx", None),
        check_vma=False,
    )
```

time: 189 us -> 172 us (0.910)
  the two profiles are of different devices: /device:TPU:199 before, /device:TPU:8 now
where the time goes in v1:
time: 172 us; the launch traced here: 171 us
  starting transfers between devices  97.2 us (57%)
  matrix products  27.6 us (16%)
  waiting for transfers between devices  17.4 us (10%)
  between operations  13.7 us (8%)
  local copies, waits for them, and re-layouts  8.02 us (5%)
  other arithmetic  7.26 us (4%)
    ppermute x9, starting transfers between devices, shifted(): return lax.ppermute(shard, axis, pairs)  97.2 us
    ppermute x9, waiting for transfers between devices, shifted(): return lax.ppermute(shard, axis, pairs)  16.7 us
    dot_general x2, matrix products, two_pass(): jnp.einsum(spec, low, signal, preferred_element_type=jnp.float32)  6.17 us
    dot_general x1, matrix products, local(): jnp.dot(gated, lax.all_gather(out_weight, 'fsdp', axis=0, tiled=True), pr...  5.46 us
    dot_general x1, matrix products, toeplitz(): jnp.einsum('gs,sij->gij', high, onehot, preferred_element_type=jnp.float32)  5.25 us
    dot_general x2, matrix products, two_pass(): first = jnp.einsum(spec, high, signal, preferred_element_type=jnp.float32)  5.12 us
  transfers between devices with their start and end apart: 10, of which 5 were waited for; matrix products, arithmetic and copies ran while one was open for 22% of the time, Pallas kernels for 0%

profile of v1, /device:TPU:8, one launch (start us, length us, event | category | flops | bytes accessed | tf_op | source)
XLA Modules:
  0.0 171.2 jit_solution(876113990603138598)
XLA Ops:
  9.2 3.5 %collective-permute-start = (bf16[6,2048]{0,1:T(8,128)(2,1)S(1)}, bf16[6,2048]{0,1:T(8,128)(2,1)S(1)}, u32[]{:S(2)}, u32[]{:S(2)}) collective-permute-start(bf16[6,2048]{0,1:T(8,128)(2,1)S(1)} %copy.44), channel_id=1, source_target_pairs={{0,4},{4,8},{8,12},{12,16},{16,20},{20,24},{24,28},{28,32},{32,36}... | collective-permute-start | bytes 73736 | tf_op jit(solution)/shard_map/ppermute | solution.py:15
  14.5 1.3 copy.46
  16.3 8.4 %collective-permute-done = bf16[6,2048]{0,1:T(8,128)(2,1)S(1)} collective-permute-done((bf16[6,2048]{0,1:T(8,128)(2,1)S(1)}, bf16[6,2048]{0,1:T(8,128)(2,1)S(1)}, u32[]{:S(2)}, u32[]{:S(2)}) %collective-permute-start) | collective-permute-done | bytes 24608 | tf_op jit(solution)/shard_map/ppermute | solution.py:15
  26.7 3.0 %fusion.20 = bf16[128,2048]{0,1:T(8,128)(2,1)S(1)} fusion(f32[130,2048]{0,1:T(8,128)S(1)} %maximum_convert_fusion.2, f32[130,2048]{0,1:T(8,128)S(1)} %maximum_convert_fusion.1, f32[2048]{0:T(1024)S(1)} %bitcast.63, f32[2048]{0:T(1024)S(1)} %bitcast.64, f32[2048]{0:T(1024)S(1)} %bitcast.59, f32[2048]{0:T(1024)S(1)} %bitcast.60, f32[2048]{0:T(1024)S(1)} %bitcast.61, ...), kind=kLoop, calls=%fused_computation.24 | loop fusion | flops 3145728 | bytes 6864896 | tf_op jit(solution)/shard_map/convert_element_type | solution.py:66
  31.2 3.5 %collective-permute-start.1 = (f32[128,16,16]{0,2,1:T(8,128)S(1)}, f32[128,16,16]{0,2,1:T(8,128)S(1)}, u32[]{:S(2)}, u32[]{:S(2)}) collective-permute-start(f32[128,16,16]{0,2,1:T(8,128)S(1)} %copy.51), channel_id=1, source_target_pairs={{0,4},{4,8},{8,12},{12,16},{16,20},{20,24},{24,28},{28,32},{32,36}... | collective-permute-start | bytes 393224 | tf_op jit(solution)/shard_map/ppermute | solution.py:15
  34.7 6.9 %collective-permute-start.2 = (f32[128,16,16]{0,2,1:T(8,128)S(1)}, f32[128,16,16]{0,2,1:T(8,128)S(1)}, u32[]{:S(2)}, u32[]{:S(2)}) collective-permute-start(f32[128,16,16]{0,2,1:T(8,128)S(1)} %copy.51), channel_id=1, source_target_pairs={{0,8},{4,12},{8,16},{12,20},{16,24},{20,28},{24,32},{28,36},{32,40... | collective-permute-start | bytes 393224 | tf_op jit(solution)/shard_map/ppermute | solution.py:15
  41.6 1.1 fusion.32
  42.8 1.9 %collective-permute-done.2 = f32[128,16,16]{0,2,1:T(8,128)S(1)} collective-permute-done((f32[128,16,16]{0,2,1:T(8,128)S(1)}, f32[128,16,16]{0,2,1:T(8,128)S(1)}, u32[]{:S(2)}, u32[]{:S(2)}) %collective-permute-start.2) | collective-permute-done | bytes 131104 | tf_op jit(solution)/shard_map/ppermute | solution.py:15
  44.6 5.3 %collective-permute-start.3 = (f32[128,16,16]{0,2,1:T(8,128)S(1)}, f32[128,16,16]{0,2,1:T(8,128)S(1)}, u32[]{:S(2)}, u32[]{:S(2)}) collective-permute-start(f32[128,16,16]{0,2,1:T(8,128)S(1)} %multiply_add_fusion.6), channel_id=1, source_target_pairs={{0,8},{4,12},{8,16},{12,20},{16,24},{20,28},{24,32},{28,36},{32,40... | collective-permute-start | bytes 393224 | tf_op jit(solution)/shard_map/ppermute | solution.py:15
  50.1 3.3 %collective-permute-done.3 = f32[128,16,16]{0,2,1:T(8,128)S(1)} collective-permute-done((f32[128,16,16]{0,2,1:T(8,128)S(1)}, f32[128,16,16]{0,2,1:T(8,128)S(1)}, u32[]{:S(2)}, u32[]{:S(2)}) %collective-permute-start.3) | collective-permute-done | bytes 131104 | tf_op jit(solution)/shard_map/ppermute | solution.py:15
  53.4 12.2 %collective-permute-start.4 = (f32[128,16,16]{0,2,1:T(8,128)S(1)}, f32[128,16,16]{0,2,1:T(8,128)S(1)}, u32[]{:S(2)}, u32[]{:S(2)}) collective-permute-start(f32[128,16,16]{0,2,1:T(8,128)S(1)} %multiply_add_fusion.5), channel_id=1, source_target_pairs={{0,16},{4,20},{8,24},{12,28},{16,32},{20,36},{24,40},{28,44},{32,4... | collective-permute-start | bytes 393224 | tf_op jit(solution)/shard_map/ppermute | solution.py:15
  65.6 1.5 fusion
  68.2 6.8 %collective-permute-start.5 = (f32[128,16,16]{0,2,1:T(8,128)S(1)}, f32[128,16,16]{0,2,1:T(8,128)S(1)}, u32[]{:S(2)}, u32[]{:S(2)}) collective-permute-start(f32[128,16,16]{0,2,1:T(8,128)S(1)} %multiply_add_fusion.4), channel_id=1, source_target_pairs={{0,32},{4,36},{8,40},{12,44},{16,48},{20,52},{24,56},{28,60},{32,6... | collective-permute-start | bytes 393224 | tf_op jit(solution)/shard_map/ppermute | solution.py:15
  75.0 5.3 %add_convert_fusion = (bf16[128,128,128]{2,0,1:T(8,128)(2,1)}, bf16[128,128,128]{2,0,1:T(8,128)(2,1)}) fusion(f32[128,128,128]{2,0,1:T(8,128)S(1)} %fusion, s32[128,128]{1,0:T(8,128)S(1)} %broadcast_subtract_fusion, s32[128]{0:T(128)S(1)} %iota.15, f32[128,128]{1,0:T(8,128)S(1)} %bitcast.54), kind=kOutput, calls=%fused_computation.13 | convolution fusion | flops 549470208 | bytes 16908800 | tf_op jit(solution)/shard_map/gs,sij->gij/dot_general | solution.py:45
  80.7 12.3 %collective-permute-start.6 = (f32[128,16,16]{0,2,1:T(8,128)S(1)}, f32[128,16,16]{0,2,1:T(8,128)S(1)}, u32[]{:S(2)}, u32[]{:S(2)}) collective-permute-start(f32[128,16,16]{0,2,1:T(8,128)S(1)} %multiply_add_fusion.3), channel_id=1, source_target_pairs={{0,64},{4,68},{8,72},{12,76},{16,80},{20,84},{24,88},{28,92},{32,9... | collective-permute-start | bytes 393224 | tf_op jit(solution)/shard_map/ppermute | solution.py:15
  93.0 5.7 %fusion.4 = f32[128,16,128]{2,1,0:T(8,128)S(1)} fusion(bf16[128,128,16]{0,2,1:T(8,128)(2,1)S(1)} %bitcast.48, bf16[128,128,128]{2,0,1:T(8,128)(2,1)} %get-tuple-element.6), kind=kOutput, calls=%fused_computation.5 | convolution fusion | flops 67108864 | bytes 5767168 | tf_op jit(solution)/shard_map/gij,jgc->igc/dot_general | solution.py:36
  98.7 26.2 %collective-permute-start.7 = (f32[128,16,16]{0,2,1:T(8,128)S(1)}, f32[128,16,16]{0,2,1:T(8,128)S(1)}, u32[]{:S(2)}, u32[]{:S(2)}) collective-permute-start(f32[128,16,16]{0,2,1:T(8,128)S(1)} %multiply_add_fusion.2), channel_id=1, source_target_pairs={{0,128},{4,132},{8,136},{12,140},{16,144},{20,148},{24,152},{28,15... | collective-permute-start | bytes 393224 | tf_op jit(solution)/shard_map/ppermute | solution.py:15
  124.9 4.6 %fusion.13 = f32[128,16,128]{2,1,0:T(8,128)} fusion(f32[128,16,128]{2,1,0:T(8,128)S(1)} %fusion.4, bf16[128,128,16]{0,2,1:T(8,128)(2,1)S(1)} %bitcast.49, bf16[128,128,128]{2,0,1:T(8,128)(2,1)S(1)} %copy-done), kind=kOutput, calls=%fused_computation.16 | convolution fusion | flops 67371008 | bytes 6815744 | tf_op jit(solution)/shard_map/gij,jgc->igc/dot_general | solution.py:35
  129.5 20.5 %collective-permute-start.8 = (f32[128,16,16]{0,2,1:T(8,128)S(1)}, f32[128,16,16]{0,2,1:T(8,128)S(1)}, u32[]{:S(2)}, u32[]{:S(2)}) collective-permute-start(f32[128,16,16]{0,2,1:T(8,128)S(1)} %multiply_add_fusion.1), channel_id=1, source_target_pairs={{0,256},{4,260},{8,264},{12,268},{16,272},{20,276},{24,280},{28,28... | collective-permute-start | bytes 393224 | tf_op jit(solution)/shard_map/ppermute | solution.py:15
  150.5 2.1 %collective-permute-done.8 = f32[128,16,16]{0,2,1:T(8,128)S(1)} collective-permute-done((f32[128,16,16]{0,2,1:T(8,128)S(1)}, f32[128,16,16]{0,2,1:T(8,128)S(1)}, u32[]{:S(2)}, u32[]{:S(2)}) %collective-permute-start.8) | collective-permute-done | bytes 131104 | tf_op jit(solution)/shard_map/ppermute | solution.py:15
  152.6 1.4 copy.54
  154.0 3.0 %fusion.17 = f32[128,16,128]{2,1,0:T(8,128)S(1)} fusion(f32[128,16,128]{2,1,0:T(8,128)} %fusion.13, f32[128,16,16]{1,2,0:T(8,128)} %copy.54, f32[128,16]{1,0:T(8,128)S(1)} %copy.53, f32[128]{0:T(128)S(1)} %iota_add_fusion, f32[128,16]{1,0:T(8,128)S(1)} %copy.48), kind=kOutput, calls=%fused_computation.20 | convolution fusion | flops 51642368 | bytes 2245120 | tf_op jit(solution)/shard_map/gni,gnc->igc/dot_general | solution.py:92
  156.9 1.9 %fusion.26 = bf16[128,2048]{0,1:T(8,128)(2,1)S(1)} fusion(f32[130,2048]{0,1:T(8,128)S(1)} %maximum_convert_fusion, f32[128,16,128]{2,1,0:T(8,128)S(1)} %fusion.17, bf16[128,2048]{0,1:T(8,128)(2,1)S(1)} %fusion.20, f32[2048]{0:T(1024)S(1)} %copy-done.4, f32[2048]{0:T(1024)S(1)} %bitcast.57, f32[2048]{0:T(1024)S(1)} %bitcast.58, f32[2048]{0:T(1024)S(1)} %bitcast.56), kind=kLoop, calls=%fused_computation.36 | loop fusion | flops 2621440 | bytes 5275648 | tf_op jit(solution)/shard_map/convert_element_type | solution.py:97
  158.9 5.5 %fusion.12 = bf16[1,128,2048]{2,1,0:T(8,128)(2,1)} fusion(bf16[128,2048]{0,1:T(8,128)(2,1)S(1)} %fusion.26, bf16[2048,2048]{1,0:T(8,128)(2,1)} %all-gather.2.cloned.1.call-done), kind=kOutput, calls=%fused_computation.15 | convolution fusion | flops 1074003968 | bytes 9437184 | tf_op jit(solution)/shard_map/dot_general | solution.py:98
  (47 shorter events, 10.4 us)
Async XLA Ops:
  6.5 9.3 %copy-start.2 = (bf16[1,128,2048]{2,1,0:T(8,128)(2,1)S(1)}, bf16[1,128,2048]{2,1,0:T(8,128)(2,1)}, u32[]{:S(2)}) copy-start(bf16[1,128,2048]{2,1,0:T(8,128)(2,1)} %param.10) | copy-start | bytes 1572868
  6.5 152.4 %all-gather.2.cloned.1.call-start = ((), (), s32[]{:S(2)}) async-start(), calls=%async_computation | async-start | bytes 10485760 | tf_op jit(solution)/shard_map/all_gather | solution.py:100
  9.2 15.6 %collective-permute-start = (bf16[6,2048]{0,1:T(8,128)(2,1)S(1)}, bf16[6,2048]{0,1:T(8,128)(2,1)S(1)}, u32[]{:S(2)}, u32[]{:S(2)}) collective-permute-start(bf16[6,2048]{0,1:T(8,128)(2,1)S(1)} %copy.44), channel_id=1, source_target_pairs={{0,4},{4,8},{8,12},{12,16},{16,20},{20,24},{24,28},{28,32},{32,36}... | collective-permute-start | bytes 73736 | tf_op jit(solution)/shard_map/ppermute | solution.py:15
  31.2 11.6 %collective-permute-start.1 = (f32[128,16,16]{0,2,1:T(8,128)S(1)}, f32[128,16,16]{0,2,1:T(8,128)S(1)}, u32[]{:S(2)}, u32[]{:S(2)}) collective-permute-start(f32[128,16,16]{0,2,1:T(8,128)S(1)} %copy.51), channel_id=1, source_target_pairs={{0,4},{4,8},{8,12},{12,16},{16,20},{20,24},{24,28},{28,32},{32,36}... | collective-permute-start | bytes 393224 | tf_op jit(solution)/shard_map/ppermute | solution.py:15
  34.7 10.0 %collective-permute-start.2 = (f32[128,16,16]{0,2,1:T(8,128)S(1)}, f32[128,16,16]{0,2,1:T(8,128)S(1)}, u32[]{:S(2)}, u32[]{:S(2)}) collective-permute-start(f32[128,16,16]{0,2,1:T(8,128)S(1)} %copy.51), channel_id=1, source_target_pairs={{0,8},{4,12},{8,16},{12,20},{16,24},{20,28},{24,32},{28,36},{32,40... | collective-permute-start | bytes 393224 | tf_op jit(solution)/shard_map/ppermute | solution.py:15
  44.6 8.8 %collective-permute-start.3 = (f32[128,16,16]{0,2,1:T(8,128)S(1)}, f32[128,16,16]{0,2,1:T(8,128)S(1)}, u32[]{:S(2)}, u32[]{:S(2)}) collective-permute-start(f32[128,16,16]{0,2,1:T(8,128)S(1)} %multiply_add_fusion.6), channel_id=1, source_target_pairs={{0,8},{4,12},{8,16},{12,20},{16,24},{20,28},{24,32},{28,36},{32,40... | collective-permute-start | bytes 393224 | tf_op jit(solution)/shard_map/ppermute | solution.py:15
  53.4 14.7 %collective-permute-start.4 = (f32[128,16,16]{0,2,1:T(8,128)S(1)}, f32[128,16,16]{0,2,1:T(8,128)S(1)}, u32[]{:S(2)}, u32[]{:S(2)}) collective-permute-start(f32[128,16,16]{0,2,1:T(8,128)S(1)} %multiply_add_fusion.5), channel_id=1, source_target_pairs={{0,16},{4,20},{8,24},{12,28},{16,32},{20,36},{24,40},{28,44},{32,4... | collective-permute-start | bytes 393224 | tf_op jit(solution)/shard_map/ppermute | solution.py:15
  68.1 12.2 %copy-start.3 = (bf16[1,128,2048]{2,1,0:T(8,128)(2,1)S(1)}, bf16[1,128,2048]{2,1,0:T(8,128)(2,1)}, u32[]{:S(2)}) copy-start(bf16[1,128,2048]{2,1,0:T(8,128)(2,1)} %param.8) | copy-start | bytes 1572868
  68.2 12.5 %collective-permute-start.5 = (f32[128,16,16]{0,2,1:T(8,128)S(1)}, f32[128,16,16]{0,2,1:T(8,128)S(1)}, u32[]{:S(2)}, u32[]{:S(2)}) collective-permute-start(f32[128,16,16]{0,2,1:T(8,128)S(1)} %multiply_add_fusion.4), channel_id=1, source_target_pairs={{0,32},{4,36},{8,40},{12,44},{16,48},{20,52},{24,56},{28,60},{32,6... | collective-permute-start | bytes 393224 | tf_op jit(solution)/shard_map/ppermute | solution.py:15
  80.6 44.2 %copy-start = (bf16[128,128,128]{2,0,1:T(8,128)(2,1)S(1)}, bf16[128,128,128]{2,0,1:T(8,128)(2,1)}, u32[]{:S(2)}) copy-start(bf16[128,128,128]{2,0,1:T(8,128)(2,1)} %get-tuple-element.5) | copy-start | bytes 12582916
  80.7 18.0 %collective-permute-start.6 = (f32[128,16,16]{0,2,1:T(8,128)S(1)}, f32[128,16,16]{0,2,1:T(8,128)S(1)}, u32[]{:S(2)}, u32[]{:S(2)}) collective-permute-start(f32[128,16,16]{0,2,1:T(8,128)S(1)} %multiply_add_fusion.3), channel_id=1, source_target_pairs={{0,64},{4,68},{8,72},{12,76},{16,80},{20,84},{24,88},{28,92},{32,9... | collective-permute-start | bytes 393224 | tf_op jit(solution)/shard_map/ppermute | solution.py:15
  98.7 51.4 %copy-start.1 = (bf16[2,2048]{0,1:T(8,128)(2,1)S(1)}, bf16[2,2048]{0,1:T(8,128)(2,1)}, u32[]{:S(2)}) copy-start(bf16[2,2048]{0,1:T(8,128)(2,1)} %get-tuple-element.9) | copy-start | bytes 24580
  98.7 30.8 %collective-permute-start.7 = (f32[128,16,16]{0,2,1:T(8,128)S(1)}, f32[128,16,16]{0,2,1:T(8,128)S(1)}, u32[]{:S(2)}, u32[]{:S(2)}) collective-permute-start(f32[128,16,16]{0,2,1:T(8,128)S(1)} %multiply_add_fusion.2), channel_id=1, source_target_pairs={{0,128},{4,132},{8,136},{12,140},{16,144},{20,148},{24,152},{28,15... | collective-permute-start | bytes 393224 | tf_op jit(solution)/shard_map/ppermute | solution.py:15
  129.5 27.4 %copy-start.4 = (f32[2048]{0:T(1024)S(1)}, f32[2048]{0:T(1024)}, u32[]{:S(2)}) copy-start(f32[2048]{0:T(1024)} %param.14) | copy-start | bytes 24580
  129.5 23.0 %collective-permute-start.8 = (f32[128,16,16]{0,2,1:T(8,128)S(1)}, f32[128,16,16]{0,2,1:T(8,128)S(1)}, u32[]{:S(2)}, u32[]{:S(2)}) collective-permute-start(f32[128,16,16]{0,2,1:T(8,128)S(1)} %multiply_add_fusion.1), channel_id=1, source_target_pairs={{0,256},{4,260},{8,264},{12,268},{16,272},{20,276},{24,280},{28,28... | collective-permute-start | bytes 393224 | tf_op jit(solution)/shard_map/ppermute | solution.py:15
Sparse Core Ops, SparseCore 0:
  9.5 90.2 all-gather.1

commit v2 on v1

--- a/solution.py
+++ b/solution.py
@@ -25,9 +25,8 @@
 
 
 def split_bf16(values):
-    high = values.astype(jnp.bfloat16)
-    low = (values - high.astype(jnp.float32)).astype(jnp.bfloat16)
-    return high, low
+    rounded = lax.reduce_precision(values, exponent_bits=8, mantissa_bits=7)
+    return rounded.astype(jnp.bfloat16), (values - rounded).astype(jnp.bfloat16)
 
 
 def two_pass(spec, table, signal):
@@ -46,7 +45,26 @@
     return first + jnp.einsum("gs,sij->gij", low, onehot, preferred_element_type=jnp.float32)
 
 
+def gather_weight(out_weight):
+    pair = [(0, 1), (1, 0)]
+    chip = lax.axis_index("zlo")
+    core = lax.axis_index("core")
+    cores = lax.axis_size("core")
+    mine = chip * cores + core
+    remote = lax.ppermute(out_weight, "zlo", pair)
+    neighbour = lax.ppermute(out_weight, "core", pair)
+    relayed = lax.ppermute(remote, "core", pair)
+    other_chip = (1 - chip) * cores
+    return [
+        (mine, out_weight),
+        (chip * cores + 1 - core, neighbour),
+        (other_chip + core, remote),
+        (other_chip + 1 - core, relayed),
+    ]
+
+
 def local(query_in, key_in, value_in, feature_taps, decay_rate, residues, skip_gain, out_weight):
+    weight_blocks = gather_weight(out_weight)
     query_rows = query_in[0]
     key_rows = key_in[0]
     value_rows = value_in[0]
@@ -95,28 +113,34 @@
     gated = (
         featured_q * (convolved.astype(jnp.float32) + skip_gain * kv_round.astype(jnp.float32))
     ).astype(jnp.bfloat16)
-    block_out = jnp.dot(
-        gated,
-        lax.all_gather(out_weight, "fsdp", axis=0, tiled=True),
-        preferred_element_type=jnp.float32,
-    ).astype(jnp.bfloat16)
-    return block_out[None]
+    rows = out_weight.shape[0]
+    block_out = None
+    for owner, weight in weight_blocks:
+        columns = lax.dynamic_slice_in_dim(gated, owner * rows, rows, axis=1)
+        term = jnp.dot(columns, weight, preferred_element_type=jnp.float32)
+        block_out = term if block_out is None else block_out + term
+    return block_out.astype(jnp.bfloat16)[None]
 
 
 def solution(mesh):
+    ctx_size, fsdp_size = mesh.shape["ctx"], mesh.shape["fsdp"]
+    split = jax.sharding.Mesh(
+        mesh.devices.reshape(ctx_size, fsdp_size // 2, 2), ("ctx", "zlo", "core")
+    )
+    batch = ("zlo", "core")
     return jax.shard_map(
         local,
-        mesh=mesh,
+        mesh=split,
         in_specs=(
-            P("fsdp", "ctx", None),
-            P("fsdp", "ctx", None),
-            P("fsdp", "ctx", None),
+            P(batch, "ctx", None),
+            P(batch, "ctx", None),
+            P(batch, "ctx", None),
             P(),
             P(),
             P(),
             P(),
-            P("fsdp", None),
+            P(batch, None),
         ),
-        out_specs=P("fsdp", "ctx", None),
+        out_specs=P(batch, "ctx", None),
         check_vma=False,
     )

time: 172 us -> 164 us (0.953)
  the two profiles are of different devices: /device:TPU:8 before, /device:TPU:1 now
where the time goes in v2:
time: 164 us; the launch traced here: 163 us
  starting transfers between devices  104 us (63%)
  matrix products  29.9 us (18%)
  waiting for transfers between devices  13.7 us (8%)
  local copies, waits for them, and re-layouts  8.01 us (5%)
  other arithmetic  7.25 us (4%)
    ppermute x9, starting transfers between devices, shifted(): return lax.ppermute(shard, axis, pairs)  78.2 us
    ppermute x1, starting transfers between devices, gather_weight(): relayed = lax.ppermute(remote, 'core', pair)  14.6 us
    ppermute x9, waiting for transfers between devices, shifted(): return lax.ppermute(shard, axis, pairs)  13.7 us
    ppermute x1, starting transfers between devices, gather_weight(): neighbour = lax.ppermute(out_weight, 'core', pair)  8.91 us
    dot_general x4, matrix products, local(): term = jnp.dot(columns, weight, preferred_element_type=jnp.float32)  7.49 us
    dot_general x2, matrix products, two_pass(): jnp.einsum(spec, low, signal, preferred_element_type=jnp.float32)  6.33 us
    dot_general x1, matrix products, toeplitz(): jnp.einsum('gs,sij->gij', high, onehot, preferred_element_type=jnp.float32)  5.44 us
    dot_general x2, matrix products, two_pass(): first = jnp.einsum(spec, high, signal, preferred_element_type=jnp.float32)  5.03 us
  transfers between devices with their start and end apart: 12, of which 4 were waited for; matrix products, arithmetic and copies ran while one was open for 26% of the time, Pallas kernels for 0%

profile of v2, /device:TPU:1, one launch (start us, length us, event | category | flops | bytes accessed | tf_op | source)
XLA Modules:
  0.0 163.0 jit_solution(16572318869692275932)
XLA Ops:
  0.0 8.9 %collective-permute-start.9 = (bf16[512,2048]{1,0:T(8,128)(2,1)}, bf16[512,2048]{1,0:T(8,128)(2,1)}, u32[]{:S(2)}, u32[]{:S(2)}) collective-permute-start(bf16[512,2048]{1,0:T(8,128)(2,1)} %param.15), channel_id=1, source_target_pairs={{0,1},{1,0},{2,3},{3,2},{4,5},{5,4},{6,7},{7,6},{8,9},{9,8},{10,11... | collective-permute-start | bytes 6291464 | tf_op jit(solution)/shard_map/ppermute | solution.py:55
  8.9 1.9 %collective-permute-start.10 = (bf16[512,2048]{1,0:T(8,128)(2,1)}, bf16[512,2048]{1,0:T(8,128)(2,1)}, u32[]{:S(2)}, u32[]{:S(2)}) collective-permute-start(bf16[512,2048]{1,0:T(8,128)(2,1)} %param.15), channel_id=1, source_target_pairs={{0,2},{2,0},{1,3},{3,1},{4,6},{6,4},{5,7},{7,5},{8,10},{10,8},{9,1... | collective-permute-start | bytes 6291464 | tf_op jit(solution)/shard_map/ppermute | solution.py:54
  17.7 7.9 %collective-permute-done = bf16[6,2048]{0,1:T(8,128)(2,1)S(1)} collective-permute-done((bf16[6,2048]{0,1:T(8,128)(2,1)S(1)}, bf16[6,2048]{0,1:T(8,128)(2,1)S(1)}, u32[]{:S(2)}, u32[]{:S(2)}) %collective-permute-start) | collective-permute-done | bytes 24608 | tf_op jit(solution)/shard_map/ppermute | solution.py:15
  27.6 3.0 %fusion.23 = bf16[128,2048]{0,1:T(8,128)(2,1)S(1)} fusion(f32[130,2048]{0,1:T(8,128)S(1)} %maximum_convert_fusion.2, f32[130,2048]{0,1:T(8,128)S(1)} %maximum_convert_fusion.1, f32[2048]{0:T(1024)S(1)} %bitcast.65, f32[2048]{0:T(1024)S(1)} %bitcast.66, f32[2048]{0:T(1024)S(1)} %bitcast.61, f32[2048]{0:T(1024)S(1)} %bitcast.62, f32[2048]{0:T(1024)S(1)} %bitcast.63, ...), kind=kLoop, calls=%fused_computation.31 | loop fusion | flops 3145728 | bytes 6864896 | tf_op jit(solution)/shard_map/convert_element_type | solution.py:84
  32.0 4.2 %collective-permute-start.1 = (f32[128,16,16]{0,2,1:T(8,128)S(1)}, f32[128,16,16]{0,2,1:T(8,128)S(1)}, u32[]{:S(2)}, u32[]{:S(2)}) collective-permute-start(f32[128,16,16]{0,2,1:T(8,128)S(1)} %copy.51), channel_id=1, source_target_pairs={{0,4},{4,8},{8,12},{12,16},{16,20},{20,24},{24,28},{28,32},{32,36}... | collective-permute-start | bytes 393224 | tf_op jit(solution)/shard_map/ppermute | solution.py:15
  36.3 2.5 %collective-permute-start.2 = (f32[128,16,16]{0,2,1:T(8,128)S(1)}, f32[128,16,16]{0,2,1:T(8,128)S(1)}, u32[]{:S(2)}, u32[]{:S(2)}) collective-permute-start(f32[128,16,16]{0,2,1:T(8,128)S(1)} %copy.51), channel_id=1, source_target_pairs={{0,8},{4,12},{8,16},{12,20},{16,24},{20,28},{24,32},{28,36},{32,40... | collective-permute-start | bytes 393224 | tf_op jit(solution)/shard_map/ppermute | solution.py:15
  41.0 4.9 %collective-permute-start.3 = (f32[128,16,16]{0,2,1:T(8,128)S(1)}, f32[128,16,16]{0,2,1:T(8,128)S(1)}, u32[]{:S(2)}, u32[]{:S(2)}) collective-permute-start(f32[128,16,16]{0,2,1:T(8,128)S(1)} %multiply_add_fusion.6), channel_id=1, source_target_pairs={{0,8},{4,12},{8,16},{12,20},{16,24},{20,28},{24,32},{28,36},{32,40... | collective-permute-start | bytes 393224 | tf_op jit(solution)/shard_map/ppermute | solution.py:15
  46.0 2.9 %collective-permute-done.3 = f32[128,16,16]{0,2,1:T(8,128)S(1)} collective-permute-done((f32[128,16,16]{0,2,1:T(8,128)S(1)}, f32[128,16,16]{0,2,1:T(8,128)S(1)}, u32[]{:S(2)}, u32[]{:S(2)}) %collective-permute-start.3) | collective-permute-done | bytes 131104 | tf_op jit(solution)/shard_map/ppermute | solution.py:15
  48.9 9.0 %collective-permute-start.4 = (f32[128,16,16]{0,2,1:T(8,128)S(1)}, f32[128,16,16]{0,2,1:T(8,128)S(1)}, u32[]{:S(2)}, u32[]{:S(2)}) collective-permute-start(f32[128,16,16]{0,2,1:T(8,128)S(1)} %multiply_add_fusion.5), channel_id=1, source_target_pairs={{0,16},{4,20},{8,24},{12,28},{16,32},{20,36},{24,40},{28,44},{32,4... | collective-permute-start | bytes 393224 | tf_op jit(solution)/shard_map/ppermute | solution.py:15
  57.9 1.5 fusion
  59.3 1.9 %collective-permute-done.4 = f32[128,16,16]{0,2,1:T(8,128)S(1)} collective-permute-done((f32[128,16,16]{0,2,1:T(8,128)S(1)}, f32[128,16,16]{0,2,1:T(8,128)S(1)}, u32[]{:S(2)}, u32[]{:S(2)}) %collective-permute-start.4) | collective-permute-done | bytes 131104 | tf_op jit(solution)/shard_map/ppermute | solution.py:15
  61.3 6.4 %collective-permute-start.5 = (f32[128,16,16]{0,2,1:T(8,128)S(1)}, f32[128,16,16]{0,2,1:T(8,128)S(1)}, u32[]{:S(2)}, u32[]{:S(2)}) collective-permute-start(f32[128,16,16]{0,2,1:T(8,128)S(1)} %multiply_add_fusion.4), channel_id=1, source_target_pairs={{0,32},{4,36},{8,40},{12,44},{16,48},{20,52},{24,56},{28,60},{32,6... | collective-permute-start | bytes 393224 | tf_op jit(solution)/shard_map/ppermute | solution.py:15
  67.7 5.4 %reduce-precision_convert_fusion = (bf16[128,128,128]{2,0,1:T(8,128)(2,1)}, bf16[128,128,128]{2,0,1:T(8,128)(2,1)}) fusion(f32[128,128,128]{2,0,1:T(8,128)S(1)} %fusion, s32[128,128]{1,0:T(8,128)S(1)} %broadcast_subtract_fusion, s32[128]{0:T(128)S(1)} %iota.15, f32[128,128]{1,0:T(8,128)S(1)} %bitcast.56), kind=kOutput, calls=%fused_computation.1 | convolution fusion | flops 549486592 | bytes 16908800 | tf_op jit(solution)/shard_map/gs,sij->gij/dot_general | solution.py:44
  73.6 8.8 %collective-permute-start.6 = (f32[128,16,16]{0,2,1:T(8,128)S(1)}, f32[128,16,16]{0,2,1:T(8,128)S(1)}, u32[]{:S(2)}, u32[]{:S(2)}) collective-permute-start(f32[128,16,16]{0,2,1:T(8,128)S(1)} %multiply_add_fusion.3), channel_id=1, source_target_pairs={{0,64},{4,68},{8,72},{12,76},{16,80},{20,84},{24,88},{28,92},{32,9... | collective-permute-start | bytes 393224 | tf_op jit(solution)/shard_map/ppermute | solution.py:15
  82.4 5.8 %fusion.5 = f32[128,16,128]{2,1,0:T(8,128)S(1)} fusion(bf16[128,128,16]{0,2,1:T(8,128)(2,1)S(1)} %bitcast.50, bf16[128,128,128]{2,0,1:T(8,128)(2,1)} %get-tuple-element.6), kind=kOutput, calls=%fused_computation.7 | convolution fusion | flops 67108864 | bytes 5767168 | tf_op jit(solution)/shard_map/gij,jgc->igc/dot_general | solution.py:35
  88.3 25.5 %collective-permute-start.7 = (f32[128,16,16]{0,2,1:T(8,128)S(1)}, f32[128,16,16]{0,2,1:T(8,128)S(1)}, u32[]{:S(2)}, u32[]{:S(2)}) collective-permute-start(f32[128,16,16]{0,2,1:T(8,128)S(1)} %multiply_add_fusion.2), channel_id=1, source_target_pairs={{0,128},{4,132},{8,136},{12,140},{16,144},{20,148},{24,152},{28,15... | collective-permute-start | bytes 393224 | tf_op jit(solution)/shard_map/ppermute | solution.py:15
  113.8 4.5 %fusion.15 = f32[128,16,128]{2,1,0:T(8,128)} fusion(f32[128,16,128]{2,1,0:T(8,128)S(1)} %fusion.5, bf16[128,128,16]{0,2,1:T(8,128)(2,1)S(1)} %bitcast.51, bf16[128,128,128]{2,0,1:T(8,128)(2,1)S(1)} %copy-done), kind=kOutput, calls=%fused_computation.22 | convolution fusion | flops 67371008 | bytes 6815744 | tf_op jit(solution)/shard_map/gij,jgc->igc/dot_general | solution.py:34
  118.4 15.6 %collective-permute-start.8 = (f32[128,16,16]{0,2,1:T(8,128)S(1)}, f32[128,16,16]{0,2,1:T(8,128)S(1)}, u32[]{:S(2)}, u32[]{:S(2)}) collective-permute-start(f32[128,16,16]{0,2,1:T(8,128)S(1)} %multiply_add_fusion.1), channel_id=1, source_target_pairs={{0,256},{4,260},{8,264},{12,268},{16,272},{20,276},{24,280},{28,28... | collective-permute-start | bytes 393224 | tf_op jit(solution)/shard_map/ppermute | solution.py:15
  134.0 14.6 %collective-permute-start.11 = (bf16[512,2048]{1,0:T(8,128)(2,1)}, bf16[512,2048]{1,0:T(8,128)(2,1)}, u32[]{:S(2)}, u32[]{:S(2)}) collective-permute-start(bf16[512,2048]{1,0:T(8,128)(2,1)} %collective-permute-done.10), channel_id=1, source_target_pairs={{0,1},{1,0},{2,3},{3,2},{4,5},{5,4},{6,7},{7,6},{8,9},{9,8},{10,11... | collective-permute-start | bytes 6291464 | tf_op jit(solution)/shard_map/ppermute | solution.py:56
  150.5 3.0 %fusion.19 = f32[128,16,128]{2,1,0:T(8,128)S(1)} fusion(f32[128,16,128]{2,1,0:T(8,128)} %fusion.15, f32[128,16,16]{1,2,0:T(8,128)} %copy.54, f32[128,16]{1,0:T(8,128)S(1)} %copy.53, f32[128]{0:T(128)S(1)} %iota_add_fusion, f32[128,16]{1,0:T(8,128)S(1)} %copy.48), kind=kOutput, calls=%fused_computation.26 | convolution fusion | flops 51642368 | bytes 2245120 | tf_op jit(solution)/shard_map/gni,gnc->igc/dot_general | solution.py:110
  153.5 1.9 %fusion.29 = bf16[128,2048]{0,1:T(8,128)(2,1)S(1)} fusion(f32[130,2048]{0,1:T(8,128)S(1)} %maximum_convert_fusion, f32[128,16,128]{2,1,0:T(8,128)S(1)} %fusion.19, bf16[128,2048]{0,1:T(8,128)(2,1)S(1)} %fusion.23, f32[2048]{0:T(1024)S(1)} %copy-done.5, f32[2048]{0:T(1024)S(1)} %bitcast.59, f32[2048]{0:T(1024)S(1)} %bitcast.60, f32[2048]{0:T(1024)S(1)} %bitcast.58), kind=kLoop, calls=%fused_computation.43 | loop fusion | flops 2621440 | bytes 5275648 | tf_op jit(solution)/shard_map/convert_element_type | solution.py:115
  155.9 2.1 %convolution_add_fusion.2 = f32[128,2048]{1,0:T(8,128)S(1)} fusion(f32[128,2048]{1,0:T(8,128)S(1)} %fusion.51, bf16[512,2048]{1,0:T(8,128)(2,1)} %collective-permute-done.9, bf16[128,2048]{0,1:T(8,128)(2,1)S(1)} %fusion.29, s32[]{:T(128)S(6)} %select_n.13), kind=kOutput, calls=%fused_computation.17 | convolution fusion | flops 268697600 | bytes 4325380 | tf_op jit(solution)/shard_map/dot_general | solution.py:120
  158.0 2.1 %convolution_add_fusion.1 = f32[128,2048]{1,0:T(8,128)S(1)} fusion(f32[128,2048]{1,0:T(8,128)S(1)} %convolution_add_fusion.2, bf16[512,2048]{1,0:T(8,128)(2,1)} %collective-permute-done.10, bf16[128,2048]{0,1:T(8,128)(2,1)S(1)} %fusion.29, s32[]{:T(128)S(6)} %select_n.14), kind=kOutput, calls=%fused_computation.16 | convolution fusion | flops 268697600 | bytes 4325380 | tf_op jit(solution)/shard_map/dot_general | solution.py:120
  160.1 2.9 %fusion.14 = bf16[1,128,2048]{2,1,0:T(8,128)(2,1)} fusion(f32[128,2048]{1,0:T(8,128)S(1)} %convolution_add_fusion.1, bf16[512,2048]{1,0:T(8,128)(2,1)} %collective-permute-done.11, bf16[128,2048]{0,1:T(8,128)(2,1)S(1)} %fusion.29, s32[]{:T(128)S(6)} %select_n.15), kind=kOutput, calls=%fused_computation.19 | convolution fusion | flops 268959744 | bytes 3801092 | tf_op jit(solution)/shard_map/dot_general | solution.py:120
  (55 shorter events, 15.3 us)
Async XLA Ops:
  0.0 17.2 %copy-start.3 = (bf16[1,128,2048]{2,1,0:T(8,128)(2,1)S(1)}, bf16[1,128,2048]{2,1,0:T(8,128)(2,1)}, u32[]{:S(2)}) copy-start(bf16[1,128,2048]{2,1,0:T(8,128)(2,1)} %param.10) | copy-start | bytes 1572868
  0.0 155.9 %collective-permute-start.9 = (bf16[512,2048]{1,0:T(8,128)(2,1)}, bf16[512,2048]{1,0:T(8,128)(2,1)}, u32[]{:S(2)}, u32[]{:S(2)}) collective-permute-start(bf16[512,2048]{1,0:T(8,128)(2,1)} %param.15), channel_id=1, source_target_pairs={{0,1},{1,0},{2,3},{3,2},{4,5},{5,4},{6,7},{7,6},{8,9},{9,8},{10,11... | collective-permute-start | bytes 6291464 | tf_op jit(solution)/shard_map/ppermute | solution.py:55
  8.9 125.0 %collective-permute-start.10 = (bf16[512,2048]{1,0:T(8,128)(2,1)}, bf16[512,2048]{1,0:T(8,128)(2,1)}, u32[]{:S(2)}, u32[]{:S(2)}) collective-permute-start(bf16[512,2048]{1,0:T(8,128)(2,1)} %param.15), channel_id=1, source_target_pairs={{0,2},{2,0},{1,3},{3,1},{4,6},{6,4},{5,7},{7,5},{8,10},{10,8},{9,1... | collective-permute-start | bytes 6291464 | tf_op jit(solution)/shard_map/ppermute | solution.py:54
  12.8 12.8 %collective-permute-start = (bf16[6,2048]{0,1:T(8,128)(2,1)S(1)}, bf16[6,2048]{0,1:T(8,128)(2,1)S(1)}, u32[]{:S(2)}, u32[]{:S(2)}) collective-permute-start(bf16[6,2048]{0,1:T(8,128)(2,1)S(1)} %copy.44), channel_id=1, source_target_pairs={{0,4},{4,8},{8,12},{12,16},{16,20},{20,24},{24,28},{28,32},{32,36}... | collective-permute-start | bytes 73736 | tf_op jit(solution)/shard_map/ppermute | solution.py:15
  32.0 7.9 %collective-permute-start.1 = (f32[128,16,16]{0,2,1:T(8,128)S(1)}, f32[128,16,16]{0,2,1:T(8,128)S(1)}, u32[]{:S(2)}, u32[]{:S(2)}) collective-permute-start(f32[128,16,16]{0,2,1:T(8,128)S(1)} %copy.51), channel_id=1, source_target_pairs={{0,4},{4,8},{8,12},{12,16},{16,20},{20,24},{24,28},{28,32},{32,36}... | collective-permute-start | bytes 393224 | tf_op jit(solution)/shard_map/ppermute | solution.py:15
  36.3 4.7 %collective-permute-start.2 = (f32[128,16,16]{0,2,1:T(8,128)S(1)}, f32[128,16,16]{0,2,1:T(8,128)S(1)}, u32[]{:S(2)}, u32[]{:S(2)}) collective-permute-start(f32[128,16,16]{0,2,1:T(8,128)S(1)} %copy.51), channel_id=1, source_target_pairs={{0,8},{4,12},{8,16},{12,20},{16,24},{20,28},{24,32},{28,36},{32,40... | collective-permute-start | bytes 393224 | tf_op jit(solution)/shard_map/ppermute | solution.py:15
  41.0 7.9 %collective-permute-start.3 = (f32[128,16,16]{0,2,1:T(8,128)S(1)}, f32[128,16,16]{0,2,1:T(8,128)S(1)}, u32[]{:S(2)}, u32[]{:S(2)}) collective-permute-start(f32[128,16,16]{0,2,1:T(8,128)S(1)} %multiply_add_fusion.6), channel_id=1, source_target_pairs={{0,8},{4,12},{8,16},{12,20},{16,24},{20,28},{24,32},{28,36},{32,40... | collective-permute-start | bytes 393224 | tf_op jit(solution)/shard_map/ppermute | solution.py:15
  48.9 12.4 %collective-permute-start.4 = (f32[128,16,16]{0,2,1:T(8,128)S(1)}, f32[128,16,16]{0,2,1:T(8,128)S(1)}, u32[]{:S(2)}, u32[]{:S(2)}) collective-permute-start(f32[128,16,16]{0,2,1:T(8,128)S(1)} %multiply_add_fusion.5), channel_id=1, source_target_pairs={{0,16},{4,20},{8,24},{12,28},{16,32},{20,36},{24,40},{28,44},{32,4... | collective-permute-start | bytes 393224 | tf_op jit(solution)/shard_map/ppermute | solution.py:15
  61.3 12.0 %copy-start.4 = (bf16[1,128,2048]{2,1,0:T(8,128)(2,1)S(1)}, bf16[1,128,2048]{2,1,0:T(8,128)(2,1)}, u32[]{:S(2)}) copy-start(bf16[1,128,2048]{2,1,0:T(8,128)(2,1)} %param.8) | copy-start | bytes 1572868
  61.3 12.3 %collective-permute-start.5 = (f32[128,16,16]{0,2,1:T(8,128)S(1)}, f32[128,16,16]{0,2,1:T(8,128)S(1)}, u32[]{:S(2)}, u32[]{:S(2)}) collective-permute-start(f32[128,16,16]{0,2,1:T(8,128)S(1)} %multiply_add_fusion.4), channel_id=1, source_target_pairs={{0,32},{4,36},{8,40},{12,44},{16,48},{20,52},{24,56},{28,60},{32,6... | collective-permute-start | bytes 393224 | tf_op jit(solution)/shard_map/ppermute | solution.py:15
  73.6 14.6 %collective-permute-start.6 = (f32[128,16,16]{0,2,1:T(8,128)S(1)}, f32[128,16,16]{0,2,1:T(8,128)S(1)}, u32[]{:S(2)}, u32[]{:S(2)}) collective-permute-start(f32[128,16,16]{0,2,1:T(8,128)S(1)} %multiply_add_fusion.3), channel_id=1, source_target_pairs={{0,64},{4,68},{8,72},{12,76},{16,80},{20,84},{24,88},{28,92},{32,9... | collective-permute-start | bytes 393224 | tf_op jit(solution)/shard_map/ppermute | solution.py:15
  82.4 31.4 %copy-start = (bf16[128,128,128]{2,0,1:T(8,128)(2,1)S(1)}, bf16[128,128,128]{2,0,1:T(8,128)(2,1)}, u32[]{:S(2)}) copy-start(bf16[128,128,128]{2,0,1:T(8,128)(2,1)} %get-tuple-element.5) | copy-start | bytes 12582916
  88.3 30.1 %collective-permute-start.7 = (f32[128,16,16]{0,2,1:T(8,128)S(1)}, f32[128,16,16]{0,2,1:T(8,128)S(1)}, u32[]{:S(2)}, u32[]{:S(2)}) collective-permute-start(f32[128,16,16]{0,2,1:T(8,128)S(1)} %multiply_add_fusion.2), channel_id=1, source_target_pairs={{0,128},{4,132},{8,136},{12,140},{16,144},{20,148},{24,152},{28,15... | collective-permute-start | bytes 393224 | tf_op jit(solution)/shard_map/ppermute | solution.py:15
  113.8 34.8 %copy-start.2 = (bf16[2,2048]{0,1:T(8,128)(2,1)S(1)}, bf16[2,2048]{0,1:T(8,128)(2,1)}, u32[]{:S(2)}) copy-start(bf16[2,2048]{0,1:T(8,128)(2,1)} %get-tuple-element.9) | copy-start | bytes 24580
  118.4 30.7 %collective-permute-start.8 = (f32[128,16,16]{0,2,1:T(8,128)S(1)}, f32[128,16,16]{0,2,1:T(8,128)S(1)}, u32[]{:S(2)}, u32[]{:S(2)}) collective-permute-start(f32[128,16,16]{0,2,1:T(8,128)S(1)} %multiply_add_fusion.1), channel_id=1, source_target_pairs={{0,256},{4,260},{8,264},{12,268},{16,272},{20,276},{24,280},{28,28... | collective-permute-start | bytes 393224 | tf_op jit(solution)/shard_map/ppermute | solution.py:15
  134.0 26.1 %collective-permute-start.11 = (bf16[512,2048]{1,0:T(8,128)(2,1)}, bf16[512,2048]{1,0:T(8,128)(2,1)}, u32[]{:S(2)}, u32[]{:S(2)}) collective-permute-start(bf16[512,2048]{1,0:T(8,128)(2,1)} %collective-permute-done.10), channel_id=1, source_target_pairs={{0,1},{1,0},{2,3},{3,2},{4,5},{5,4},{6,7},{7,6},{8,9},{9,8},{10,11... | collective-permute-start | bytes 6291464 | tf_op jit(solution)/shard_map/ppermute | solution.py:56
  149.1 4.4 %copy-start.5 = (f32[2048]{0:T(1024)S(1)}, f32[2048]{0:T(1024)}, u32[]{:S(2)}) copy-start(f32[2048]{0:T(1024)} %param.14) | copy-start | bytes 24580
  153.5 1.9 %copy-start.1 = (bf16[512,2048]{1,0:T(8,128)(2,1)S(1)}, bf16[512,2048]{1,0:T(8,128)(2,1)}, u32[]{:S(2)}) copy-start(bf16[512,2048]{1,0:T(8,128)(2,1)} %param.15) | copy-start | bytes 6291460

commit v3 on v2

--- a/solution.py
+++ b/solution.py
@@ -1,6 +1,10 @@
+import functools
+
 import jax
 import jax.numpy as jnp
 from jax import lax
+from jax.experimental import pallas as pl
+from jax.experimental.pallas import tpu as pltpu
 from jax.sharding import PartitionSpec as P
 
 GROUP = 16
@@ -61,6 +65,79 @@
         (other_chip + core, remote),
         (other_chip + 1 - core, relayed),
     ]
+
+
+def scan_shifts(count):
+    first = [1, 2] if count > 2 else [1]
+    later = []
+    span = 2
+    while span < count:
+        later.append(span)
+        span *= 2
+    return first, later
+
+
+def scan_kernel(count, ending_ref, decay_ref, entering_ref, sent, landed, send_sem, recv_sem):
+    me = lax.axis_index("ctx")
+    first, later = scan_shifts(count)
+    partners = sorted(set(first + later))
+
+    barrier = pltpu.get_barrier_semaphore()
+    for span in partners:
+        for target in (lax.rem(me + span, count), lax.rem(me + count - span, count)):
+            pl.semaphore_signal(barrier, inc=1, device_id={"ctx": target}, device_id_type=pl.DeviceIdType.MESH)
+    pl.semaphore_wait(barrier, 2 * len(partners))
+
+    def send(source, slot, span):
+        copy = pltpu.make_async_remote_copy(
+            src_ref=source,
+            dst_ref=landed.at[slot],
+            send_sem=send_sem.at[slot],
+            recv_sem=recv_sem.at[slot],
+            device_id={"ctx": lax.rem(me + span, count)},
+            device_id_type=pl.DeviceIdType.MESH,
+        )
+        copy.start()
+        return copy
+
+    def arrived(slot, span):
+        return jnp.where(me >= span, landed[slot], 0.0)
+
+    copies = [send(ending_ref, slot, span) for slot, span in enumerate(first)]
+    for copy in copies:
+        copy.wait_recv()
+    total = arrived(0, first[0])
+    if len(first) > 1:
+        total = total + decay_ref[0] * arrived(1, first[1])
+    for step, span in enumerate(later):
+        slot = len(first) + step
+        sent[step] = total
+        copies.append(send(sent.at[step], slot, span))
+        copies[-1].wait_recv()
+        total = total + decay_ref[step + 1] * arrived(slot, span)
+    entering_ref[...] = total
+    for copy in copies:
+        copy.wait_send()
+
+
+def scan_states(ending, decay):
+    count = lax.axis_size("ctx")
+    first, later = scan_shifts(count)
+    slots = len(first) + len(later)
+    vmem = pl.BlockSpec(memory_space=pltpu.VMEM)
+    return pl.pallas_call(
+        functools.partial(scan_kernel, count),
+        out_shape=jax.ShapeDtypeStruct(ending.shape, jnp.float32),
+        in_specs=[vmem, vmem],
+        out_specs=vmem,
+        scratch_shapes=[
+            pltpu.VMEM((max(1, len(later)),) + ending.shape, jnp.float32),
+            pltpu.VMEM((slots,) + ending.shape, jnp.float32),
+            pltpu.SemaphoreType.DMA((slots,)),
+            pltpu.SemaphoreType.DMA((slots,)),
+        ],
+        compiler_params=pltpu.CompilerParams(collective_id=0, has_side_effects=True),
+    )(ending, decay)
 
 
 def local(query_in, key_in, value_in, feature_taps, decay_rate, residues, skip_gain, out_weight):
@@ -95,19 +172,14 @@
     lagged = jnp.exp(-decay_rate[:, :, None] * (positions + 1.0)) * scale[:, :, None]
 
     inner = two_pass("gij,jgc->igc", toeplitz(kernel), kv_grouped)
-    ending = two_pass("gnj,jgc->gnc", closing, kv_grouped)
-
-    count = lax.axis_size("ctx")
-    entering = shifted(ending, "ctx", 1)
-    if count > 2:
-        step_decay = jnp.exp(-decay_rate * float(width))[:, :, None]
-        entering = entering + step_decay * shifted(ending, "ctx", 2)
-        span = 2
-        while span < count:
-            decay = jnp.exp(-decay_rate * float(width * span))[:, :, None]
-            entering = entering + decay * shifted(entering, "ctx", span)
-            span *= 2
-    crossing = jnp.einsum("gni,gnc->igc", lagged, entering, precision=exact_precision)
+    ending = two_pass("gnj,jgc->ngc", closing, kv_grouped).reshape(-1, chans)
+
+    first, later = scan_shifts(lax.axis_size("ctx"))
+    spans = jnp.asarray([1] * (len(first) - 1) + later, jnp.float32)[:, None, None] * float(width)
+    decay = jnp.exp(-jnp.transpose(decay_rate)[None, :, :] * spans)
+    decay = jnp.repeat(decay, GROUP, axis=2)
+    entering = scan_states(ending, decay).reshape(-1, groups, GROUP)
+    crossing = jnp.einsum("gni,ngc->igc", lagged, entering, precision=exact_precision)
     convolved = (inner + crossing).reshape(width, chans).astype(jnp.bfloat16)
 
     gated = (

time: 164 us -> 157 us (0.957)
  the two profiles are of different devices: /device:TPU:1 before, /device:TPU:5 now
where the time goes in v3:
time: 157 us; the launch traced here: 156 us
  Pallas kernels  86.7 us (55%)
  matrix products  25.7 us (16%)
  local copies, waits for them, and re-layouts  19.4 us (12%)
  starting transfers between devices  16.6 us (11%)
  other arithmetic  7.31 us (5%)
    pallas_call x1, Pallas kernels, scan_states(): pl.pallas_call(functools.partial(scan_kernel, count), out_shape=jax.Shape...  86.7 us
    reshape x1, local copies, waits for them, and re-layouts, local(): decay = jnp.repeat(decay, GROUP, axis=2)  7.66 us
    ppermute x1, starting transfers between devices, gather_weight(): relayed = lax.ppermute(remote, 'core', pair)  6.79 us
    dot_general x2, matrix products, two_pass(): jnp.einsum(spec, low, signal, preferred_element_type=jnp.float32)  6.34 us
    dot_general x4, matrix products, local(): term = jnp.dot(columns, weight, preferred_element_type=jnp.float32)  5.89 us
    dot_general x1, matrix products, toeplitz(): jnp.einsum('gs,sij->gij', high, onehot, preferred_element_type=jnp.float32)  5.39 us
    broadcast_in_dim x1, local copies, waits for them, and re-layouts, local(): decay = jnp.repeat(decay, GROUP, axis=2)  4.16 us
    dot_general x2, matrix products, two_pass(): first = jnp.einsum(spec, high, signal, preferred_element_type=jnp.float32)  4.05 us
  transfers between devices with their start and end apart: 4, of which 0 were waited for; matrix products, arithmetic and copies ran while one was open for 33% of the time, Pallas kernels for 56%

profile of v3, /device:TPU:5, one launch (start us, length us, event | category | flops | bytes accessed | tf_op | source)
XLA Modules:
  0.0 156.0 jit_solution(15502208749684844987)
XLA Ops:
  0.0 2.6 %collective-permute-start.1 = (bf16[512,2048]{1,0:T(8,128)(2,1)}, bf16[512,2048]{1,0:T(8,128)(2,1)}, u32[]{:S(2)}, u32[]{:S(2)}) collective-permute-start(bf16[512,2048]{1,0:T(8,128)(2,1)} %param.16), channel_id=1, source_target_pairs={{0,1},{1,0},{2,3},{3,2},{4,5},{5,4},{6,7},{7,6},{8,9},{9,8},{10,11... | collective-permute-start | bytes 6291464 | tf_op jit(solution)/shard_map/ppermute | solution.py:59
  2.6 4.0 %collective-permute-start.2 = (bf16[512,2048]{1,0:T(8,128)(2,1)}, bf16[512,2048]{1,0:T(8,128)(2,1)}, u32[]{:S(2)}, u32[]{:S(2)}) collective-permute-start(bf16[512,2048]{1,0:T(8,128)(2,1)} %param.16), channel_id=1, source_target_pairs={{0,2},{2,0},{1,3},{3,1},{4,6},{6,4},{5,7},{7,5},{8,10},{10,8},{9,1... | collective-permute-start | bytes 6291464 | tf_op jit(solution)/shard_map/ppermute | solution.py:58
  6.6 0.8 slice_bitcast_fusion.2
  7.4 0.8 slice_bitcast_fusion
  8.2 1.1 copy.33
  9.3 3.2 %collective-permute-start = (bf16[6,2048]{0,1:T(8,128)(2,1)}, bf16[6,2048]{0,1:T(8,128)(2,1)S(1)}, u32[]{:S(2)}, u32[]{:S(2)}) collective-permute-start(bf16[6,2048]{0,1:T(8,128)(2,1)} %copy.33), channel_id=1, source_target_pairs={{0,4},{4,8},{8,12},{12,16},{16,20},{20,24},{24,28},{28,32},{32,36}... | collective-permute-start | bytes 73736 | tf_op jit(solution)/shard_map/ppermute | solution.py:19
  12.5 1.1 fusion.71
  14.6 1.1 fusion.42
  15.7 1.5 fusion
  17.2 5.4 %reduce-precision_convert_fusion = (bf16[128,128,128]{2,0,1:T(8,128)(2,1)}, bf16[128,128,128]{2,0,1:T(8,128)(2,1)}) fusion(f32[128,128,128]{2,0,1:T(8,128)S(1)} %fusion, s32[128,128]{1,0:T(8,128)S(1)} %broadcast_subtract_fusion, s32[128]{0:T(128)S(1)} %iota.15, f32[128,128]{1,0:T(8,128)S(1)} %bitcast.66), kind=kOutput, calls=%fused_computation.1 | convolution fusion | flops 549486592 | bytes 16908800 | tf_op jit(solution)/shard_map/gs,sij->gij/dot_general | solution.py:48
  24.0 4.2 %broadcast_in_dim.4 = f32[7,16,128,16]{3,2,1,0:T(8,128)} broadcast(f32[7,16,128]{2,1,0:T(8,128)S(1)} %multiply_exponential_fusion.1), dimensions={0,1,2} | broadcast | bytes 974848 | tf_op jit(solution)/shard_map/broadcast_in_dim | solution.py:180
  28.1 7.7 %reshape.83.decay_ref = f32[7,16,2048]{2,1,0:T(8,128)} reshape(f32[7,16,128,16]{3,2,1,0:T(8,128)} %broadcast_in_dim.4) | data formatting | bytes 1835008 | tf_op jit(solution)/shard_map/reshape | solution.py:180
  37.0 3.2 %fusion.30 = bf16[128,2048]{0,1:T(8,128)(2,1)S(1)} fusion(f32[130,2048]{0,1:T(8,128)S(1)} %maximum_convert_fusion.2, f32[130,2048]{0,1:T(8,128)S(1)} %maximum_convert_fusion.1, f32[2048]{0:T(1024)S(1)} %bitcast.75, f32[2048]{0:T(1024)S(1)} %bitcast.76, f32[2048]{0:T(1024)S(1)} %bitcast.71, f32[2048]{0:T(1024)S(1)} %bitcast.72, f32[2048]{0:T(1024)S(1)} %bitcast.73, ...), kind=kLoop, calls=%fused_computation.31 | loop fusion | flops 3145728 | bytes 6864896 | tf_op jit(solution)/shard_map/convert_element_type | solution.py:161
  41.2 1.0 copy.45.ending_ref
  42.2 86.7 %shard_map.91 = f32[16,2048]{1,0:T(8,128)} custom-call(f32[16,2048]{1,0:T(8,128)} %copy.45.ending_ref, f32[7,16,2048]{2,1,0:T(8,128)} %reshape.83.decay_ref), custom_call_target="tpu_custom_call" | custom-call | tf_op jit(solution)/shard_map/pallas_call | solution.py:128
  128.9 1.2 copy.46
  130.1 1.4 fusion.38
  131.6 5.8 %fusion.5 = f32[128,16,128]{2,1,0:T(8,128)S(1)} fusion(bf16[128,128,16]{0,2,1:T(8,128)(2,1)S(1)} %bitcast.58, bf16[128,128,128]{2,0,1:T(8,128)(2,1)} %get-tuple-element.6), kind=kOutput, calls=%fused_computation.7 | convolution fusion | flops 67108864 | bytes 5767168 | tf_op jit(solution)/shard_map/gij,jgc->igc/dot_general | solution.py:39
  137.4 6.8 %collective-permute-start.3 = (bf16[512,2048]{1,0:T(8,128)(2,1)}, bf16[512,2048]{1,0:T(8,128)(2,1)S(1)}, u32[]{:S(2)}, u32[]{:S(2)}) collective-permute-start(bf16[512,2048]{1,0:T(8,128)(2,1)} %collective-permute-done.2), channel_id=1, source_target_pairs={{0,1},{1,0},{2,3},{3,2},{4,5},{5,4},{6,7},{7,6},{8,9},{9,8},{10,11... | collective-permute-start | bytes 6291464 | tf_op jit(solution)/shard_map/ppermute | solution.py:60
  144.6 3.5 %fusion.24 = f32[128,16,128]{2,1,0:T(8,128)S(1)} fusion(f32[128,16,128]{2,1,0:T(8,128)S(1)} %fusion.38, f32[128,16,128]{2,1,0:T(8,128)S(1)} %fusion.5, bf16[128,128,16]{0,2,1:T(8,128)(2,1)S(1)} %bitcast.59, bf16[128,128,128]{2,0,1:T(8,128)(2,1)S(1)} %copy-done), kind=kOutput, calls=%fused_computation.26 | convolution fusion | flops 68157440 | bytes 7864320 | tf_op jit(solution)/shard_map/gij,jgc->igc/dot_general | solution.py:38
  148.2 1.9 %fusion.36 = bf16[128,2048]{0,1:T(8,128)(2,1)S(1)} fusion(f32[130,2048]{0,1:T(8,128)S(1)} %maximum_convert_fusion, f32[128,16,128]{2,1,0:T(8,128)S(1)} %fusion.24, bf16[128,2048]{0,1:T(8,128)(2,1)S(1)} %fusion.30, f32[2048]{0:T(1024)S(1)} %copy-done.5, f32[2048]{0:T(1024)S(1)} %bitcast.69, f32[2048]{0:T(1024)S(1)} %bitcast.70, f32[2048]{0:T(1024)S(1)} %bitcast.68), kind=kLoop, calls=%fused_computation.43 | loop fusion | flops 2621440 | bytes 5275648 | tf_op jit(solution)/shard_map/convert_element_type | solution.py:187
  150.6 2.1 %convolution_add_fusion.2 = f32[128,2048]{1,0:T(8,128)S(1)} fusion(f32[128,2048]{1,0:T(8,128)S(1)} %fusion.59, bf16[512,2048]{1,0:T(8,128)(2,1)} %collective-permute-done.1, bf16[128,2048]{0,1:T(8,128)(2,1)S(1)} %fusion.36, s32[]{:T(128)S(6)} %select_n.13), kind=kOutput, calls=%fused_computation.17 | convolution fusion | flops 268697600 | bytes 4325380 | tf_op jit(solution)/shard_map/dot_general | solution.py:192
  152.7 2.1 %convolution_add_fusion.1 = f32[128,2048]{1,0:T(8,128)S(1)} fusion(f32[128,2048]{1,0:T(8,128)S(1)} %convolution_add_fusion.2, bf16[512,2048]{1,0:T(8,128)(2,1)} %collective-permute-done.2, bf16[128,2048]{0,1:T(8,128)(2,1)S(1)} %fusion.36, s32[]{:T(128)S(6)} %select_n.14), kind=kOutput, calls=%fused_computation.16 | convolution fusion | flops 268697600 | bytes 4325380 | tf_op jit(solution)/shard_map/dot_general | solution.py:192
  154.8 1.3 fusion.14
  (38 shorter events, 5.5 us)
Async XLA Ops:
  0.0 150.6 %collective-permute-start.1 = (bf16[512,2048]{1,0:T(8,128)(2,1)}, bf16[512,2048]{1,0:T(8,128)(2,1)}, u32[]{:S(2)}, u32[]{:S(2)}) collective-permute-start(bf16[512,2048]{1,0:T(8,128)(2,1)} %param.16), channel_id=1, source_target_pairs={{0,1},{1,0},{2,3},{3,2},{4,5},{5,4},{6,7},{7,6},{8,9},{9,8},{10,11... | collective-permute-start | bytes 6291464 | tf_op jit(solution)/shard_map/ppermute | solution.py:59
  2.6 134.8 %collective-permute-start.2 = (bf16[512,2048]{1,0:T(8,128)(2,1)}, bf16[512,2048]{1,0:T(8,128)(2,1)}, u32[]{:S(2)}, u32[]{:S(2)}) collective-permute-start(bf16[512,2048]{1,0:T(8,128)(2,1)} %param.16), channel_id=1, source_target_pairs={{0,2},{2,0},{1,3},{3,1},{4,6},{6,4},{5,7},{7,5},{8,10},{10,8},{9,1... | collective-permute-start | bytes 6291464 | tf_op jit(solution)/shard_map/ppermute | solution.py:58
  9.3 26.5 %collective-permute-start = (bf16[6,2048]{0,1:T(8,128)(2,1)}, bf16[6,2048]{0,1:T(8,128)(2,1)S(1)}, u32[]{:S(2)}, u32[]{:S(2)}) collective-permute-start(bf16[6,2048]{0,1:T(8,128)(2,1)} %copy.33), channel_id=1, source_target_pairs={{0,4},{4,8},{8,12},{12,16},{16,20},{20,24},{24,28},{28,32},{32,36}... | collective-permute-start | bytes 73736 | tf_op jit(solution)/shard_map/ppermute | solution.py:19
  17.2 5.4 %copy-start.6 = (f32[7]{0:T(128)S(1)}, f32[7]{0:T(128)}, u32[]{:S(2)}) copy-start(f32[7]{0:T(128)} %constant.30) | copy-start | bytes 88
  17.2 5.5 %copy-start.2 = (bf16[1,128,2048]{2,1,0:T(8,128)(2,1)S(1)}, bf16[1,128,2048]{2,1,0:T(8,128)(2,1)}, u32[]{:S(2)}) copy-start(bf16[1,128,2048]{2,1,0:T(8,128)(2,1)} %param.10) | copy-start | bytes 1572868
  17.2 5.8 %copy-start.3 = (bf16[1,128,2048]{2,1,0:T(8,128)(2,1)S(1)}, bf16[1,128,2048]{2,1,0:T(8,128)(2,1)}, u32[]{:S(2)}) copy-start(bf16[1,128,2048]{2,1,0:T(8,128)(2,1)} %param.11) | copy-start | bytes 1572868
  22.6 1.0 copy-start.4
  131.6 13.1 %copy-start = (bf16[128,128,128]{2,0,1:T(8,128)(2,1)S(1)}, bf16[128,128,128]{2,0,1:T(8,128)(2,1)}, u32[]{:S(2)}) copy-start(bf16[128,128,128]{2,0,1:T(8,128)(2,1)} %get-tuple-element.5) | copy-start | bytes 12582916
  137.4 17.4 %collective-permute-start.3 = (bf16[512,2048]{1,0:T(8,128)(2,1)}, bf16[512,2048]{1,0:T(8,128)(2,1)S(1)}, u32[]{:S(2)}, u32[]{:S(2)}) collective-permute-start(bf16[512,2048]{1,0:T(8,128)(2,1)} %collective-permute-done.2), channel_id=1, source_target_pairs={{0,1},{1,0},{2,3},{3,2},{4,5},{5,4},{6,7},{7,6},{8,9},{9,8},{10,11... | collective-permute-start | bytes 6291464 | tf_op jit(solution)/shard_map/ppermute | solution.py:60
  144.6 3.6 %copy-start.5 = (f32[2048]{0:T(1024)S(1)}, f32[2048]{0:T(1024)}, u32[]{:S(2)}) copy-start(f32[2048]{0:T(1024)} %param.15) | copy-start | bytes 24580
  148.2 1.9 %copy-start.1 = (bf16[512,2048]{1,0:T(8,128)(2,1)S(1)}, bf16[512,2048]{1,0:T(8,128)(2,1)}, u32[]{:S(2)}) copy-start(bf16[512,2048]{1,0:T(8,128)(2,1)} %param.16) | copy-start | bytes 6291460

commit v4 on v3

--- a/solution.py
+++ b/solution.py
@@ -44,9 +44,10 @@
     lag = lax.optimization_barrier(jnp.arange(width, dtype=jnp.int32))
     diff = lag[:, None] - lag[None, :]
     onehot = (lag[:, None, None] == diff[None, :, :]).astype(jnp.bfloat16)
-    high, low = split_bf16(kernel)
-    first = jnp.einsum("gs,sij->gij", high, onehot, preferred_element_type=jnp.float32)
-    return first + jnp.einsum("gs,sij->gij", low, onehot, preferred_element_type=jnp.float32)
+    return [
+        jnp.einsum("gs,sij->gij", part, onehot, preferred_element_type=jnp.bfloat16)
+        for part in split_bf16(kernel)
+    ]
 
 
 def gather_weight(out_weight):
@@ -171,13 +172,16 @@
     closing = jnp.exp(-decay_rate[:, :, None] * (width - 1.0 - positions))
     lagged = jnp.exp(-decay_rate[:, :, None] * (positions + 1.0)) * scale[:, :, None]
 
-    inner = two_pass("gij,jgc->igc", toeplitz(kernel), kv_grouped)
+    high, low = toeplitz(kernel)
+    inner = jnp.einsum("gij,jgc->igc", high, kv_grouped, preferred_element_type=jnp.float32)
+    inner = inner + jnp.einsum("gij,jgc->igc", low, kv_grouped, preferred_element_type=jnp.float32)
     ending = two_pass("gnj,jgc->ngc", closing, kv_grouped).reshape(-1, chans)
 
     first, later = scan_shifts(lax.axis_size("ctx"))
     spans = jnp.asarray([1] * (len(first) - 1) + later, jnp.float32)[:, None, None] * float(width)
-    decay = jnp.exp(-jnp.transpose(decay_rate)[None, :, :] * spans)
-    decay = jnp.repeat(decay, GROUP, axis=2)
+    modes = decay_rate.shape[1]
+    rate_lanes = jnp.broadcast_to(jnp.transpose(decay_rate)[:, :, None], (modes, groups, GROUP))
+    decay = jnp.exp(-rate_lanes.reshape(1, modes, chans) * spans)
     entering = scan_states(ending, decay).reshape(-1, groups, GROUP)
     crossing = jnp.einsum("gni,ngc->igc", lagged, entering, precision=exact_precision)
     convolved = (inner + crossing).reshape(width, chans).astype(jnp.bfloat16)

time: 157 us -> 157 us (level)
  local copies, waits for them, and re-layouts: 19.4 us -> 7.31 us
  Pallas kernels: 86.7 us -> 95.8 us
    dot_general x2 -> x4, matrix products: 6.87 us -> 17.5 us  [the longest x2 8.15 us: toeplitz(): jnp.einsum('gs,sij->gij', part, onehot, preferred_element_type=jnp.bfloat16)]
    pallas_call x1, Pallas kernels: 86.7 us -> 95.8 us  [scan_states(): pl.pallas_call(functools.partial(scan_kernel, count), out_shape=jax.Shape...]
    reshape x1 -> x0, local copies, waits for them, and re-layouts: 7.66 us -> none  [local(): decay = jnp.repeat(decay, GROUP, axis=2)]
    dot_general x2 -> x1, matrix products: 6.34 us -> 0.5 us  [two_pass(): jnp.einsum(spec, low, signal, preferred_element_type=jnp.float32)]
    broadcast_in_dim x1, local copies, waits for them, and re-layouts: 4.16 us -> 0.32 us  [local(): jnp.broadcast_to(jnp.transpose(decay_rate)[:, :, None], (modes, groups, G...]
    dot_general x2 -> x1, matrix products: 4.05 us -> 0.5 us  [two_pass(): first = jnp.einsum(spec, high, signal, preferred_element_type=jnp.float32)]
  transfers between devices with their start and end apart: 4 -> 4, of which waited for: 0 -> 1; matrix products, arithmetic and copies ran while one was open for 33% -> 27% of each run, Pallas kernels for 56% -> 61%
where the time goes in v4:
time: 157 us; the launch traced here: 156 us
  Pallas kernels  95.8 us (61%)
  matrix products  27 us (17%)
  starting transfers between devices  16.6 us (11%)
  other arithmetic  8.42 us (5%)
  local copies, waits for them, and re-layouts  7.31 us (5%)
    pallas_call x1, Pallas kernels, scan_states(): pl.pallas_call(functools.partial(scan_kernel, count), out_shape=jax.Shape...  95.8 us
    dot_general x2, matrix products, toeplitz(): jnp.einsum('gs,sij->gij', part, onehot, preferred_element_type=jnp.bfloat16)  8.15 us
    ppermute x1, starting transfers between devices, gather_weight(): relayed = lax.ppermute(remote, 'core', pair)  6.79 us
    dot_general x4, matrix products, local(): term = jnp.dot(columns, weight, preferred_element_type=jnp.float32)  5.89 us
    dot_general x1, matrix products, local(): jnp.einsum('gij,jgc->igc', low, kv_grouped, preferred_element_type=jnp.fl...  5.83 us
    ppermute x1, starting transfers between devices, gather_weight(): remote = lax.ppermute(out_weight, 'zlo', pair)  4 us
    dot_general x1, matrix products, local(): jnp.einsum('gij,jgc->igc', high, kv_grouped, preferred_element_type=jnp.f...  3.54 us
    convert_element_type x1, other arithmetic, local(): kv_round = (featured_k * featured_v).astype(jnp.bfloat16)  3.22 us
  transfers between devices with their start and end apart: 4, of which 1 were waited for; matrix products, arithmetic and copies ran while one was open for 27% of the time, Pallas kernels for 61%

profile of v4, /device:TPU:5, one launch (start us, length us, event | category | flops | bytes accessed | tf_op | source)
XLA Modules:
  0.0 156.0 jit_solution(14967616585180175582)
XLA Ops:
  0.0 2.6 %collective-permute-start.1 = (bf16[512,2048]{1,0:T(8,128)(2,1)}, bf16[512,2048]{1,0:T(8,128)(2,1)}, u32[]{:S(2)}, u32[]{:S(2)}) collective-permute-start(bf16[512,2048]{1,0:T(8,128)(2,1)} %param.16), channel_id=1, source_target_pairs={{0,1},{1,0},{2,3},{3,2},{4,5},{5,4},{6,7},{7,6},{8,9},{9,8},{10,11... | collective-permute-start | bytes 6291464 | tf_op jit(solution)/shard_map/ppermute | solution.py:60
  2.6 4.0 %collective-permute-start.2 = (bf16[512,2048]{1,0:T(8,128)(2,1)}, bf16[512,2048]{1,0:T(8,128)(2,1)}, u32[]{:S(2)}, u32[]{:S(2)}) collective-permute-start(bf16[512,2048]{1,0:T(8,128)(2,1)} %param.16), channel_id=1, source_target_pairs={{0,2},{2,0},{1,3},{3,1},{4,6},{6,4},{5,7},{7,5},{8,10},{10,8},{9,1... | collective-permute-start | bytes 6291464 | tf_op jit(solution)/shard_map/ppermute | solution.py:59
  6.6 0.8 slice_bitcast_fusion.2
  7.4 0.8 slice_bitcast_fusion
  8.2 1.1 copy.29
  9.3 3.2 %collective-permute-start = (bf16[6,2048]{0,1:T(8,128)(2,1)}, bf16[6,2048]{0,1:T(8,128)(2,1)S(1)}, u32[]{:S(2)}, u32[]{:S(2)}) collective-permute-start(bf16[6,2048]{0,1:T(8,128)(2,1)} %copy.29), channel_id=1, source_target_pairs={{0,4},{4,8},{8,12},{12,16},{16,20},{20,24},{24,28},{28,32},{32,36}... | collective-permute-start | bytes 73736 | tf_op jit(solution)/shard_map/ppermute | solution.py:19
  12.5 0.7 sqrt_multiply_fusion
  13.5 1.1 fusion.41
  14.7 4.0 %fusion = bf16[128,128,128]{2,0,1:T(8,128)(2,1)} fusion(s32[128,128]{1,0:T(8,128)S(1)} %broadcast_subtract_fusion, s32[128]{0:T(128)S(1)} %iota.15, f32[128,128]{1,0:T(8,128)S(1)} %bitcast.61), kind=kOutput, calls=%fused_computation | convolution fusion | flops 539017216 | bytes 4325888 | tf_op jit(solution)/shard_map/gs,sij->gij/dot_general | solution.py:48
  18.7 4.2 %fusion.2 = bf16[128,128,128]{2,0,1:T(8,128)(2,1)} fusion(s32[128,128]{1,0:T(8,128)S(1)} %broadcast_subtract_fusion, s32[128]{0:T(128)S(1)} %iota.15, f32[128,128]{1,0:T(8,128)S(1)} %bitcast.62), kind=kOutput, calls=%fused_computation.2 | convolution fusion | flops 539000832 | bytes 4325888 | tf_op jit(solution)/shard_map/gs,sij->gij/dot_general | solution.py:48
  23.9 1.2 multiply_exponential_fusion.1.decay_ref
  26.0 0.7 collective-permute-done
  27.9 3.2 %fusion.29 = bf16[128,2048]{0,1:T(8,128)(2,1)S(1)} fusion(f32[130,2048]{0,1:T(8,128)S(1)} %maximum_convert_fusion.2, f32[130,2048]{0,1:T(8,128)S(1)} %maximum_convert_fusion.1, f32[2048]{0:T(1024)S(1)} %bitcast.71, f32[2048]{0:T(1024)S(1)} %bitcast.72, f32[2048]{0:T(1024)S(1)} %bitcast.67, f32[2048]{0:T(1024)S(1)} %bitcast.68, f32[2048]{0:T(1024)S(1)} %bitcast.69, ...), kind=kLoop, calls=%fused_computation.28 | loop fusion | flops 3145728 | bytes 6864896 | tf_op jit(solution)/shard_map/convert_element_type | solution.py:162
  32.1 1.0 copy.41.ending_ref
  33.1 95.8 %shard_map.91 = f32[16,2048]{1,0:T(8,128)} custom-call(f32[16,2048]{1,0:T(8,128)} %copy.41.ending_ref, f32[7,16,2048]{2,1,0:T(8,128)} %multiply_exponential_fusion.1.decay_ref), custom_call_target="tpu_custom_call" | custom-call | tf_op jit(solution)/shard_map/pallas_call | solution.py:129
  128.9 1.2 copy.42
  130.1 1.4 fusion.37
  131.6 5.8 %fusion.4 = f32[128,16,128]{2,1,0:T(8,128)S(1)} fusion(bf16[128,128,16]{0,2,1:T(8,128)(2,1)S(1)} %bitcast.54, bf16[128,128,128]{2,0,1:T(8,128)(2,1)} %fusion), kind=kOutput, calls=%fused_computation.4 | convolution fusion | flops 67108864 | bytes 5767168 | tf_op jit(solution)/shard_map/gij,jgc->igc/dot_general | solution.py:177
  137.4 6.8 %collective-permute-start.3 = (bf16[512,2048]{1,0:T(8,128)(2,1)}, bf16[512,2048]{1,0:T(8,128)(2,1)S(1)}, u32[]{:S(2)}, u32[]{:S(2)}) collective-permute-start(bf16[512,2048]{1,0:T(8,128)(2,1)} %collective-permute-done.2), channel_id=1, source_target_pairs={{0,1},{1,0},{2,3},{3,2},{4,5},{5,4},{6,7},{7,6},{8,9},{9,8},{10,11... | collective-permute-start | bytes 6291464 | tf_op jit(solution)/shard_map/ppermute | solution.py:61
  144.6 3.5 %fusion.23 = f32[128,16,128]{2,1,0:T(8,128)S(1)} fusion(f32[128,16,128]{2,1,0:T(8,128)S(1)} %fusion.37, f32[128,16,128]{2,1,0:T(8,128)S(1)} %fusion.4, bf16[128,128,16]{0,2,1:T(8,128)(2,1)S(1)} %bitcast.55, bf16[128,128,128]{2,0,1:T(8,128)(2,1)S(1)} %copy-done), kind=kOutput, calls=%fused_computation.23 | convolution fusion | flops 68157440 | bytes 7864320 | tf_op jit(solution)/shard_map/gij,jgc->igc/dot_general | solution.py:176
  148.2 1.9 %fusion.35 = bf16[128,2048]{0,1:T(8,128)(2,1)S(1)} fusion(f32[130,2048]{0,1:T(8,128)S(1)} %maximum_convert_fusion, f32[128,16,128]{2,1,0:T(8,128)S(1)} %fusion.23, bf16[128,2048]{0,1:T(8,128)(2,1)S(1)} %fusion.29, f32[2048]{0:T(1024)S(1)} %copy-done.6, f32[2048]{0:T(1024)S(1)} %bitcast.65, f32[2048]{0:T(1024)S(1)} %bitcast.66, f32[2048]{0:T(1024)S(1)} %bitcast.64), kind=kLoop, calls=%fused_computation.40 | loop fusion | flops 2621440 | bytes 5275648 | tf_op jit(solution)/shard_map/convert_element_type | solution.py:191
  150.6 2.1 %convolution_add_fusion.2 = f32[128,2048]{1,0:T(8,128)S(1)} fusion(f32[128,2048]{1,0:T(8,128)S(1)} %fusion.58, bf16[512,2048]{1,0:T(8,128)(2,1)} %collective-permute-done.1, bf16[128,2048]{0,1:T(8,128)(2,1)S(1)} %fusion.35, s32[]{:T(128)S(6)} %select_n.13), kind=kOutput, calls=%fused_computation.14 | convolution fusion | flops 268697600 | bytes 4325380 | tf_op jit(solution)/shard_map/dot_general | solution.py:196
  152.7 2.1 %convolution_add_fusion.1 = f32[128,2048]{1,0:T(8,128)S(1)} fusion(f32[128,2048]{1,0:T(8,128)S(1)} %convolution_add_fusion.2, bf16[512,2048]{1,0:T(8,128)(2,1)} %collective-permute-done.2, bf16[128,2048]{0,1:T(8,128)(2,1)S(1)} %fusion.35, s32[]{:T(128)S(6)} %select_n.14), kind=kOutput, calls=%fused_computation.13 | convolution fusion | flops 268697600 | bytes 4325380 | tf_op jit(solution)/shard_map/dot_general | solution.py:196
  154.8 1.3 fusion.13
  (40 shorter events, 5.4 us)
Async XLA Ops:
  0.0 150.6 %collective-permute-start.1 = (bf16[512,2048]{1,0:T(8,128)(2,1)}, bf16[512,2048]{1,0:T(8,128)(2,1)}, u32[]{:S(2)}, u32[]{:S(2)}) collective-permute-start(bf16[512,2048]{1,0:T(8,128)(2,1)} %param.16), channel_id=1, source_target_pairs={{0,1},{1,0},{2,3},{3,2},{4,5},{5,4},{6,7},{7,6},{8,9},{9,8},{10,11... | collective-permute-start | bytes 6291464 | tf_op jit(solution)/shard_map/ppermute | solution.py:60
  2.6 134.8 %collective-permute-start.2 = (bf16[512,2048]{1,0:T(8,128)(2,1)}, bf16[512,2048]{1,0:T(8,128)(2,1)}, u32[]{:S(2)}, u32[]{:S(2)}) collective-permute-start(bf16[512,2048]{1,0:T(8,128)(2,1)} %param.16), channel_id=1, source_target_pairs={{0,2},{2,0},{1,3},{3,1},{4,6},{6,4},{5,7},{7,5},{8,10},{10,8},{9,1... | collective-permute-start | bytes 6291464 | tf_op jit(solution)/shard_map/ppermute | solution.py:59
  9.3 17.4 %collective-permute-start = (bf16[6,2048]{0,1:T(8,128)(2,1)}, bf16[6,2048]{0,1:T(8,128)(2,1)S(1)}, u32[]{:S(2)}, u32[]{:S(2)}) collective-permute-start(bf16[6,2048]{0,1:T(8,128)(2,1)} %copy.29), channel_id=1, source_target_pairs={{0,4},{4,8},{8,12},{12,16},{16,20},{20,24},{24,28},{28,32},{32,36}... | collective-permute-start | bytes 73736 | tf_op jit(solution)/shard_map/ppermute | solution.py:19
  18.7 4.2 %copy-start.5 = (f32[3,3,2048]{2,1,0:T(4,128)S(1)}, f32[3,3,2048]{2,1,0:T(4,128)}, u32[]{:S(2)}) copy-start(f32[3,3,2048]{2,1,0:T(4,128)} %param.12) | copy-start | bytes 221188
  22.8 1.0 copy-start.7
  22.8 2.2 %copy-start.2 = (bf16[1,128,2048]{2,1,0:T(8,128)(2,1)S(1)}, bf16[1,128,2048]{2,1,0:T(8,128)(2,1)}, u32[]{:S(2)}) copy-start(bf16[1,128,2048]{2,1,0:T(8,128)(2,1)} %param.10) | copy-start | bytes 1572868
  22.9 2.5 %copy-start.3 = (bf16[1,128,2048]{2,1,0:T(8,128)(2,1)S(1)}, bf16[1,128,2048]{2,1,0:T(8,128)(2,1)}, u32[]{:S(2)}) copy-start(bf16[1,128,2048]{2,1,0:T(8,128)(2,1)} %param.11) | copy-start | bytes 1572868
  23.2 2.5 %copy-start.4 = (bf16[1,128,2048]{2,1,0:T(8,128)(2,1)S(1)}, bf16[1,128,2048]{2,1,0:T(8,128)(2,1)}, u32[]{:S(2)}) copy-start(bf16[1,128,2048]{2,1,0:T(8,128)(2,1)} %param.9) | copy-start | bytes 1572868
  131.6 13.1 %copy-start = (bf16[128,128,128]{2,0,1:T(8,128)(2,1)S(1)}, bf16[128,128,128]{2,0,1:T(8,128)(2,1)}, u32[]{:S(2)}) copy-start(bf16[128,128,128]{2,0,1:T(8,128)(2,1)} %fusion.2) | copy-start | bytes 12582916
  137.4 17.4 %collective-permute-start.3 = (bf16[512,2048]{1,0:T(8,128)(2,1)}, bf16[512,2048]{1,0:T(8,128)(2,1)S(1)}, u32[]{:S(2)}, u32[]{:S(2)}) collective-permute-start(bf16[512,2048]{1,0:T(8,128)(2,1)} %collective-permute-done.2), channel_id=1, source_target_pairs={{0,1},{1,0},{2,3},{3,2},{4,5},{5,4},{6,7},{7,6},{8,9},{9,8},{10,11... | collective-permute-start | bytes 6291464 | tf_op jit(solution)/shard_map/ppermute | solution.py:61
  144.6 3.6 %copy-start.6 = (f32[2048]{0:T(1024)S(1)}, f32[2048]{0:T(1024)}, u32[]{:S(2)}) copy-start(f32[2048]{0:T(1024)} %param.15) | copy-start | bytes 24580
  148.2 1.9 %copy-start.1 = (bf16[512,2048]{1,0:T(8,128)(2,1)S(1)}, bf16[512,2048]{1,0:T(8,128)(2,1)}, u32[]{:S(2)}) copy-start(bf16[512,2048]{1,0:T(8,128)(2,1)} %param.16) | copy-start | bytes 6291460

commit v5 on v4

--- a/solution.py
+++ b/solution.py
@@ -89,6 +89,8 @@
             pl.semaphore_signal(barrier, inc=1, device_id={"ctx": target}, device_id_type=pl.DeviceIdType.MESH)
     pl.semaphore_wait(barrier, 2 * len(partners))
 
+    copies = []
+
     def send(source, slot, span):
         copy = pltpu.make_async_remote_copy(
             src_ref=source,
@@ -98,27 +100,37 @@
             device_id={"ctx": lax.rem(me + span, count)},
             device_id_type=pl.DeviceIdType.MESH,
         )
-        copy.start()
+
+        @pl.when(me + span < count)
+        def _():
+            copy.start()
+
+        copies.append((copy, span))
         return copy
 
-    def arrived(slot, span):
-        return jnp.where(me >= span, landed[slot], 0.0)
-
-    copies = [send(ending_ref, slot, span) for slot, span in enumerate(first)]
-    for copy in copies:
-        copy.wait_recv()
-    total = arrived(0, first[0])
-    if len(first) > 1:
-        total = total + decay_ref[0] * arrived(1, first[1])
+    def take(copy, slot, span, factor):
+        @pl.when(me >= span)
+        def _():
+            copy.wait_recv()
+            if factor is None:
+                entering_ref[...] += landed[slot]
+            else:
+                entering_ref[...] += factor * landed[slot]
+
+    entering_ref[...] = jnp.zeros(entering_ref.shape, jnp.float32)
+    opening = [send(ending_ref, slot, span) for slot, span in enumerate(first)]
+    for slot, span in enumerate(first):
+        take(opening[slot], slot, span, None if slot == 0 else decay_ref[0])
     for step, span in enumerate(later):
         slot = len(first) + step
-        sent[step] = total
-        copies.append(send(sent.at[step], slot, span))
-        copies[-1].wait_recv()
-        total = total + decay_ref[step + 1] * arrived(slot, span)
-    entering_ref[...] = total
-    for copy in copies:
-        copy.wait_send()
+        sent[step] = entering_ref[...]
+        copy = send(sent.at[step], slot, span)
+        take(copy, slot, span, decay_ref[step + 1])
+    for copy, span in copies:
+
+        @pl.when(me + span < count)
+        def _():
+            copy.wait_send()
 
 
 def scan_states(ending, decay):

time: 157 us -> 144 us (0.917)
  the two profiles are of different devices: /device:TPU:5 before, /device:TPU:389 now
where the time goes in v5:
time: 144 us
  Pallas kernels  86.4 us (60%)
  matrix products  27 us (19%)
  starting transfers between devices  13.7 us (10%)
  other arithmetic  8.24 us (6%)
  local copies, waits for them, and re-layouts  7.31 us (5%)
    pallas_call x1, Pallas kernels, scan_states(): pl.pallas_call(functools.partial(scan_kernel, count), out_shape=jax.Shape...  86.4 us
    dot_general x2, matrix products, toeplitz(): jnp.einsum('gs,sij->gij', part, onehot, preferred_element_type=jnp.bfloat16)  8.15 us
    dot_general x4, matrix products, local(): term = jnp.dot(columns, weight, preferred_element_type=jnp.float32)  5.89 us
    dot_general x1, matrix products, local(): jnp.einsum('gij,jgc->igc', low, kv_grouped, preferred_element_type=jnp.fl...  5.83 us
    ppermute x1, starting transfers between devices, gather_weight(): relayed = lax.ppermute(remote, 'core', pair)  4.87 us
    dot_general x1, matrix products, local(): jnp.einsum('gij,jgc->igc', high, kv_grouped, preferred_element_type=jnp.f...  3.54 us
    ppermute x1, starting transfers between devices, shifted(): return lax.ppermute(shard, axis, pairs)  3.19 us
    ppermute x1, starting transfers between devices, gather_weight(): remote = lax.ppermute(out_weight, 'zlo', pair)  3.1 us
  transfers between devices with their start and end apart: 4, of which 1 were waited for; matrix products, arithmetic and copies ran while one was open for 29% of the time, Pallas kernels for 60%

profile of v5, /device:TPU:389, one launch (start us, length us, event | category | flops | bytes accessed | tf_op | source)
XLA Modules:
  0.0 143.7 jit_solution(16805561535054411939)
XLA Ops:
  0.0 2.6 %collective-permute-start.1 = (bf16[512,2048]{1,0:T(8,128)(2,1)}, bf16[512,2048]{1,0:T(8,128)(2,1)}, u32[]{:S(2)}, u32[]{:S(2)}) collective-permute-start(bf16[512,2048]{1,0:T(8,128)(2,1)} %param.16), channel_id=1, source_target_pairs={{0,1},{1,0},{2,3},{3,2},{4,5},{5,4},{6,7},{7,6},{8,9},{9,8},{10,11... | collective-permute-start | bytes 6291464 | tf_op jit(solution)/shard_map/ppermute | solution.py:60
  2.6 3.1 %collective-permute-start.2 = (bf16[512,2048]{1,0:T(8,128)(2,1)}, bf16[512,2048]{1,0:T(8,128)(2,1)}, u32[]{:S(2)}, u32[]{:S(2)}) collective-permute-start(bf16[512,2048]{1,0:T(8,128)(2,1)} %param.16), channel_id=1, source_target_pairs={{0,2},{2,0},{1,3},{3,1},{4,6},{6,4},{5,7},{7,5},{8,10},{10,8},{9,1... | collective-permute-start | bytes 6291464 | tf_op jit(solution)/shard_map/ppermute | solution.py:59
  5.7 0.8 slice_bitcast_fusion.2
  6.5 0.8 slice_bitcast_fusion
  7.3 1.1 copy.29
  8.4 3.2 %collective-permute-start = (bf16[6,2048]{0,1:T(8,128)(2,1)}, bf16[6,2048]{0,1:T(8,128)(2,1)S(1)}, u32[]{:S(2)}, u32[]{:S(2)}) collective-permute-start(bf16[6,2048]{0,1:T(8,128)(2,1)} %copy.29), channel_id=1, source_target_pairs={{0,4},{4,8},{8,12},{12,16},{16,20},{20,24},{24,28},{28,32},{32,36}... | collective-permute-start | bytes 73736 | tf_op jit(solution)/shard_map/ppermute | solution.py:19
  11.6 0.7 sqrt_multiply_fusion
  12.6 1.1 fusion.41
  13.8 4.0 %fusion = bf16[128,128,128]{2,0,1:T(8,128)(2,1)} fusion(s32[128,128]{1,0:T(8,128)S(1)} %broadcast_subtract_fusion, s32[128]{0:T(128)S(1)} %iota.15, f32[128,128]{1,0:T(8,128)S(1)} %bitcast.61), kind=kOutput, calls=%fused_computation | convolution fusion | flops 539017216 | bytes 4325888 | tf_op jit(solution)/shard_map/gs,sij->gij/dot_general | solution.py:48
  17.8 4.2 %fusion.2 = bf16[128,128,128]{2,0,1:T(8,128)(2,1)} fusion(s32[128,128]{1,0:T(8,128)S(1)} %broadcast_subtract_fusion, s32[128]{0:T(128)S(1)} %iota.15, f32[128,128]{1,0:T(8,128)S(1)} %bitcast.62), kind=kOutput, calls=%fused_computation.2 | convolution fusion | flops 539000832 | bytes 4325888 | tf_op jit(solution)/shard_map/gs,sij->gij/dot_general | solution.py:48
  23.0 1.2 multiply_exponential_fusion.1.decay_ref
  25.1 0.7 collective-permute-done
  27.0 3.0 %fusion.29 = bf16[128,2048]{0,1:T(8,128)(2,1)S(1)} fusion(f32[130,2048]{0,1:T(8,128)S(1)} %maximum_convert_fusion.2, f32[130,2048]{0,1:T(8,128)S(1)} %maximum_convert_fusion.1, f32[2048]{0:T(1024)S(1)} %bitcast.71, f32[2048]{0:T(1024)S(1)} %bitcast.72, f32[2048]{0:T(1024)S(1)} %bitcast.67, f32[2048]{0:T(1024)S(1)} %bitcast.68, f32[2048]{0:T(1024)S(1)} %bitcast.69, ...), kind=kLoop, calls=%fused_computation.28 | loop fusion | flops 3145728 | bytes 6864896 | tf_op jit(solution)/shard_map/convert_element_type | solution.py:174
  31.1 1.0 copy.41.ending_ref
  32.0 86.4 %shard_map.91 = f32[16,2048]{1,0:T(8,128)} custom-call(f32[16,2048]{1,0:T(8,128)} %copy.41.ending_ref, f32[7,16,2048]{2,1,0:T(8,128)} %multiply_exponential_fusion.1.decay_ref), custom_call_target="tpu_custom_call" | custom-call | tf_op jit(solution)/shard_map/pallas_call | solution.py:141
  118.5 1.2 copy.42
  119.7 1.4 fusion.37
  121.2 5.8 %fusion.4 = f32[128,16,128]{2,1,0:T(8,128)S(1)} fusion(bf16[128,128,16]{0,2,1:T(8,128)(2,1)S(1)} %bitcast.54, bf16[128,128,128]{2,0,1:T(8,128)(2,1)} %fusion), kind=kOutput, calls=%fused_computation.4 | convolution fusion | flops 67108864 | bytes 5767168 | tf_op jit(solution)/shard_map/gij,jgc->igc/dot_general | solution.py:189
  127.0 4.9 %collective-permute-start.3 = (bf16[512,2048]{1,0:T(8,128)(2,1)}, bf16[512,2048]{1,0:T(8,128)(2,1)S(1)}, u32[]{:S(2)}, u32[]{:S(2)}) collective-permute-start(bf16[512,2048]{1,0:T(8,128)(2,1)} %collective-permute-done.2), channel_id=1, source_target_pairs={{0,1},{1,0},{2,3},{3,2},{4,5},{5,4},{6,7},{7,6},{8,9},{9,8},{10,11... | collective-permute-start | bytes 6291464 | tf_op jit(solution)/shard_map/ppermute | solution.py:61
  132.3 3.5 %fusion.23 = f32[128,16,128]{2,1,0:T(8,128)S(1)} fusion(f32[128,16,128]{2,1,0:T(8,128)S(1)} %fusion.37, f32[128,16,128]{2,1,0:T(8,128)S(1)} %fusion.4, bf16[128,128,16]{0,2,1:T(8,128)(2,1)S(1)} %bitcast.55, bf16[128,128,128]{2,0,1:T(8,128)(2,1)S(1)} %copy-done), kind=kOutput, calls=%fused_computation.23 | convolution fusion | flops 68157440 | bytes 7864320 | tf_op jit(solution)/shard_map/gij,jgc->igc/dot_general | solution.py:188
  135.9 1.9 %fusion.35 = bf16[128,2048]{0,1:T(8,128)(2,1)S(1)} fusion(f32[130,2048]{0,1:T(8,128)S(1)} %maximum_convert_fusion, f32[128,16,128]{2,1,0:T(8,128)S(1)} %fusion.23, bf16[128,2048]{0,1:T(8,128)(2,1)S(1)} %fusion.29, f32[2048]{0:T(1024)S(1)} %copy-done.6, f32[2048]{0:T(1024)S(1)} %bitcast.65, f32[2048]{0:T(1024)S(1)} %bitcast.66, f32[2048]{0:T(1024)S(1)} %bitcast.64), kind=kLoop, calls=%fused_computation.40 | loop fusion | flops 2621440 | bytes 5275648 | tf_op jit(solution)/shard_map/convert_element_type | solution.py:203
  138.3 2.1 %convolution_add_fusion.2 = f32[128,2048]{1,0:T(8,128)S(1)} fusion(f32[128,2048]{1,0:T(8,128)S(1)} %fusion.58, bf16[512,2048]{1,0:T(8,128)(2,1)} %collective-permute-done.1, bf16[128,2048]{0,1:T(8,128)(2,1)S(1)} %fusion.35, s32[]{:T(128)S(6)} %select_n.13), kind=kOutput, calls=%fused_computation.14 | convolution fusion | flops 268697600 | bytes 4325380 | tf_op jit(solution)/shard_map/dot_general | solution.py:208
  140.3 2.1 %convolution_add_fusion.1 = f32[128,2048]{1,0:T(8,128)S(1)} fusion(f32[128,2048]{1,0:T(8,128)S(1)} %convolution_add_fusion.2, bf16[512,2048]{1,0:T(8,128)(2,1)} %collective-permute-done.2, bf16[128,2048]{0,1:T(8,128)(2,1)S(1)} %fusion.35, s32[]{:T(128)S(6)} %select_n.14), kind=kOutput, calls=%fused_computation.13 | convolution fusion | flops 268697600 | bytes 4325380 | tf_op jit(solution)/shard_map/dot_general | solution.py:208
  142.4 1.3 fusion.13
  (40 shorter events, 5.4 us)
Async XLA Ops:
  0.0 138.3 %collective-permute-start.1 = (bf16[512,2048]{1,0:T(8,128)(2,1)}, bf16[512,2048]{1,0:T(8,128)(2,1)}, u32[]{:S(2)}, u32[]{:S(2)}) collective-permute-start(bf16[512,2048]{1,0:T(8,128)(2,1)} %param.16), channel_id=1, source_target_pairs={{0,1},{1,0},{2,3},{3,2},{4,5},{5,4},{6,7},{7,6},{8,9},{9,8},{10,11... | collective-permute-start | bytes 6291464 | tf_op jit(solution)/shard_map/ppermute | solution.py:60
  2.6 124.4 %collective-permute-start.2 = (bf16[512,2048]{1,0:T(8,128)(2,1)}, bf16[512,2048]{1,0:T(8,128)(2,1)}, u32[]{:S(2)}, u32[]{:S(2)}) collective-permute-start(bf16[512,2048]{1,0:T(8,128)(2,1)} %param.16), channel_id=1, source_target_pairs={{0,2},{2,0},{1,3},{3,1},{4,6},{6,4},{5,7},{7,5},{8,10},{10,8},{9,1... | collective-permute-start | bytes 6291464 | tf_op jit(solution)/shard_map/ppermute | solution.py:59
  8.4 17.4 %collective-permute-start = (bf16[6,2048]{0,1:T(8,128)(2,1)}, bf16[6,2048]{0,1:T(8,128)(2,1)S(1)}, u32[]{:S(2)}, u32[]{:S(2)}) collective-permute-start(bf16[6,2048]{0,1:T(8,128)(2,1)} %copy.29), channel_id=1, source_target_pairs={{0,4},{4,8},{8,12},{12,16},{16,20},{20,24},{24,28},{28,32},{32,36}... | collective-permute-start | bytes 73736 | tf_op jit(solution)/shard_map/ppermute | solution.py:19
  17.8 4.2 %copy-start.5 = (f32[3,3,2048]{2,1,0:T(4,128)S(1)}, f32[3,3,2048]{2,1,0:T(4,128)}, u32[]{:S(2)}) copy-start(f32[3,3,2048]{2,1,0:T(4,128)} %param.12) | copy-start | bytes 221188
  21.9 1.0 copy-start.7
  21.9 2.2 %copy-start.2 = (bf16[1,128,2048]{2,1,0:T(8,128)(2,1)S(1)}, bf16[1,128,2048]{2,1,0:T(8,128)(2,1)}, u32[]{:S(2)}) copy-start(bf16[1,128,2048]{2,1,0:T(8,128)(2,1)} %param.10) | copy-start | bytes 1572868
  22.0 2.5 %copy-start.3 = (bf16[1,128,2048]{2,1,0:T(8,128)(2,1)S(1)}, bf16[1,128,2048]{2,1,0:T(8,128)(2,1)}, u32[]{:S(2)}) copy-start(bf16[1,128,2048]{2,1,0:T(8,128)(2,1)} %param.11) | copy-start | bytes 1572868
  22.3 2.5 %copy-start.4 = (bf16[1,128,2048]{2,1,0:T(8,128)(2,1)S(1)}, bf16[1,128,2048]{2,1,0:T(8,128)(2,1)}, u32[]{:S(2)}) copy-start(bf16[1,128,2048]{2,1,0:T(8,128)(2,1)} %param.9) | copy-start | bytes 1572868
  121.1 11.1 %copy-start = (bf16[128,128,128]{2,0,1:T(8,128)(2,1)S(1)}, bf16[128,128,128]{2,0,1:T(8,128)(2,1)}, u32[]{:S(2)}) copy-start(bf16[128,128,128]{2,0,1:T(8,128)(2,1)} %fusion.2) | copy-start | bytes 12582916
  127.0 15.4 %collective-permute-start.3 = (bf16[512,2048]{1,0:T(8,128)(2,1)}, bf16[512,2048]{1,0:T(8,128)(2,1)S(1)}, u32[]{:S(2)}, u32[]{:S(2)}) collective-permute-start(bf16[512,2048]{1,0:T(8,128)(2,1)} %collective-permute-done.2), channel_id=1, source_target_pairs={{0,1},{1,0},{2,3},{3,2},{4,5},{5,4},{6,7},{7,6},{8,9},{9,8},{10,11... | collective-permute-start | bytes 6291464 | tf_op jit(solution)/shard_map/ppermute | solution.py:61
  132.3 3.6 %copy-start.6 = (f32[2048]{0:T(1024)S(1)}, f32[2048]{0:T(1024)}, u32[]{:S(2)}) copy-start(f32[2048]{0:T(1024)} %param.15) | copy-start | bytes 24580
  135.9 1.9 %copy-start.1 = (bf16[512,2048]{1,0:T(8,128)(2,1)S(1)}, bf16[512,2048]{1,0:T(8,128)(2,1)}, u32[]{:S(2)}) copy-start(bf16[512,2048]{1,0:T(8,128)(2,1)} %param.16) | copy-start | bytes 6291460

commit v6 on v5

--- a/solution.py
+++ b/solution.py
@@ -78,7 +78,29 @@
     return first, later
 
 
-def scan_kernel(count, ending_ref, decay_ref, entering_ref, sent, landed, send_sem, recv_sem):
+def conv_tiles(high_ref, low_ref, kv_ref, inner_ref, first_tile, last_tile):
+    lanes = kv_ref.shape[0]
+    per_tile = 128 // GROUP
+    owner = lax.broadcasted_iota(jnp.int32, (1, 128), 1) // GROUP
+
+    def body(tile, carry):
+        col = pl.multiple_of(tile * 128, 128)
+        block = kv_ref[:, pl.ds(col, 128)]
+        total = jnp.zeros((lanes, 128), jnp.float32)
+        for member in range(per_tile):
+            group = tile * per_tile + member
+            part = jnp.where(owner == member, block, jnp.zeros_like(block))
+            total += jnp.dot(high_ref[group], part, preferred_element_type=jnp.float32)
+            total += jnp.dot(low_ref[group], part, preferred_element_type=jnp.float32)
+        inner_ref[:, pl.ds(col, 128)] = total
+        return carry
+
+    lax.fori_loop(first_tile, last_tile, body, 0)
+
+
+def scan_kernel(
+    count, ending_ref, decay_ref, high_ref, low_ref, kv_ref, entering_ref, inner_ref, sent, landed, send_sem, recv_sem
+):
     me = lax.axis_index("ctx")
     first, later = scan_shifts(count)
     partners = sorted(set(first + later))
@@ -117,14 +139,20 @@
             else:
                 entering_ref[...] += factor * landed[slot]
 
+    tiles = kv_ref.shape[1] // 128
+    rounds = 1 + len(later)
+    bounds = [tiles * step // rounds for step in range(rounds + 1)]
+
     entering_ref[...] = jnp.zeros(entering_ref.shape, jnp.float32)
     opening = [send(ending_ref, slot, span) for slot, span in enumerate(first)]
+    conv_tiles(high_ref, low_ref, kv_ref, inner_ref, bounds[0], bounds[1])
     for slot, span in enumerate(first):
         take(opening[slot], slot, span, None if slot == 0 else decay_ref[0])
     for step, span in enumerate(later):
         slot = len(first) + step
         sent[step] = entering_ref[...]
         copy = send(sent.at[step], slot, span)
+        conv_tiles(high_ref, low_ref, kv_ref, inner_ref, bounds[step + 1], bounds[step + 2])
         take(copy, slot, span, decay_ref[step + 1])
     for copy, span in copies:
 
@@ -133,24 +161,29 @@
             copy.wait_send()
 
 
-def scan_states(ending, decay):
+def scan_states(ending, decay, high, low, kv):
     count = lax.axis_size("ctx")
     first, later = scan_shifts(count)
     slots = len(first) + len(later)
     vmem = pl.BlockSpec(memory_space=pltpu.VMEM)
     return pl.pallas_call(
         functools.partial(scan_kernel, count),
-        out_shape=jax.ShapeDtypeStruct(ending.shape, jnp.float32),
-        in_specs=[vmem, vmem],
-        out_specs=vmem,
+        out_shape=(
+            jax.ShapeDtypeStruct(ending.shape, jnp.float32),
+            jax.ShapeDtypeStruct(kv.shape, jnp.float32),
+        ),
+        in_specs=[vmem] * 5,
+        out_specs=(vmem, vmem),
         scratch_shapes=[
             pltpu.VMEM((max(1, len(later)),) + ending.shape, jnp.float32),
             pltpu.VMEM((slots,) + ending.shape, jnp.float32),
             pltpu.SemaphoreType.DMA((slots,)),
             pltpu.SemaphoreType.DMA((slots,)),
         ],
-        compiler_params=pltpu.CompilerParams(collective_id=0, has_side_effects=True),
-    )(ending, decay)
+        compiler_params=pltpu.CompilerParams(
+            collective_id=0, has_side_effects=True, vmem_limit_bytes=48 * 1024 * 1024
+        ),
+    )(ending, decay, high, low, kv)
 
 
 def local(query_in, key_in, value_in, feature_taps, decay_rate, residues, skip_gain, out_weight):
@@ -185,8 +218,6 @@
     lagged = jnp.exp(-decay_rate[:, :, None] * (positions + 1.0)) * scale[:, :, None]
 
     high, low = toeplitz(kernel)
-    inner = jnp.einsum("gij,jgc->igc", high, kv_grouped, preferred_element_type=jnp.float32)
-    inner = inner + jnp.einsum("gij,jgc->igc", low, kv_grouped, preferred_element_type=jnp.float32)
     ending = two_pass("gnj,jgc->ngc", closing, kv_grouped).reshape(-1, chans)
 
     first, later = scan_shifts(lax.axis_size("ctx"))
@@ -194,9 +225,10 @@
     modes = decay_rate.shape[1]
     rate_lanes = jnp.broadcast_to(jnp.transpose(decay_rate)[:, :, None], (modes, groups, GROUP))
     decay = jnp.exp(-rate_lanes.reshape(1, modes, chans) * spans)
-    entering = scan_states(ending, decay).reshape(-1, groups, GROUP)
+    entering, inner = scan_states(ending, decay, high, low, kv_round)
+    entering = entering.reshape(-1, groups, GROUP)
     crossing = jnp.einsum("gni,ngc->igc", lagged, entering, precision=exact_precision)
-    convolved = (inner + crossing).reshape(width, chans).astype(jnp.bfloat16)
+    convolved = (inner + crossing.reshape(width, chans)).astype(jnp.bfloat16)
 
     gated = (
         featured_q * (convolved.astype(jnp.float32) + skip_gain * kv_round.astype(jnp.float32))

time: 144 us -> 140 us (0.972)
  the two profiles are of different devices: /device:TPU:389 before, /device:TPU:333 now
where the time goes in v6:
time: 140 us; the launch traced here: 139 us
  Pallas kernels  65.5 us (47%)
  local copies, waits for them, and re-layouts  23.9 us (17%)
  matrix products  21.5 us (15%)
  waiting for transfers between devices  13.7 us (10%)
  starting transfers between devices  10.7 us (8%)
  other arithmetic  3.4 us (2%)
    pallas_call x1, Pallas kernels, scan_states(): pl.pallas_call(functools.partial(scan_kernel, count), out_shape=(jax.Shap...  65.5 us
    ppermute x1, waiting for transfers between devices, gather_weight(): remote = lax.ppermute(out_weight, 'zlo', pair)  13.7 us
    dot_general x2, local copies, waits for them, and re-layouts, toeplitz(): jnp.einsum('gs,sij->gij', part, onehot, preferred_element_type=jnp.bfloat16)  11.7 us
    dot_general x2, matrix products, toeplitz(): jnp.einsum('gs,sij->gij', part, onehot, preferred_element_type=jnp.bfloat16)  8.19 us
    dot_general x4, matrix products, local(): term = jnp.dot(columns, weight, preferred_element_type=jnp.float32)  7.37 us
    ppermute x1, starting transfers between devices, shifted(): return lax.ppermute(shard, axis, pairs)  3.2 us
  transfers between devices with their start and end apart: 4, of which 1 were waited for; matrix products, arithmetic and copies ran while one was open for 32% of the time, Pallas kernels for 47%

profile of v6, /device:TPU:333, one launch (start us, length us, event | category | flops | bytes accessed | tf_op | source)
XLA Modules:
  0.0 138.9 jit_solution(4710361510074498750)
XLA Ops:
  0.0 2.6 %collective-permute-start.1 = (bf16[512,2048]{1,0:T(8,128)(2,1)}, bf16[512,2048]{1,0:T(8,128)(2,1)}, u32[]{:S(2)}, u32[]{:S(2)}) collective-permute-start(bf16[512,2048]{1,0:T(8,128)(2,1)} %param.16), channel_id=1, source_target_pairs={{0,1},{1,0},{2,3},{3,2},{4,5},{5,4},{6,7},{7,6},{8,9},{9,8},{10,11... | collective-permute-start | bytes 6291464 | tf_op jit(solution)/shard_map/ppermute | solution.py:60
  2.6 2.2 %collective-permute-start.2 = (bf16[512,2048]{1,0:T(8,128)(2,1)}, bf16[512,2048]{1,0:T(8,128)(2,1)}, u32[]{:S(2)}, u32[]{:S(2)}) collective-permute-start(bf16[512,2048]{1,0:T(8,128)(2,1)} %param.16), channel_id=1, source_target_pairs={{0,2},{2,0},{1,3},{3,1},{4,6},{6,4},{5,7},{7,5},{8,10},{10,8},{9,1... | collective-permute-start | bytes 6291464 | tf_op jit(solution)/shard_map/ppermute | solution.py:59
  5.6 0.8 slice_bitcast_fusion
  6.4 3.2 %collective-permute-start = (bf16[6,2048]{1,0:T(8,128)(2,1)S(1)}, bf16[6,2048]{1,0:T(8,128)(2,1)S(1)}, u32[]{:S(2)}, u32[]{:S(2)}) collective-permute-start(bf16[6,2048]{1,0:T(8,128)(2,1)S(1)} %pad_maximum_fusion), channel_id=1, source_target_pairs={{0,4},{4,8},{8,12},{12,16},{16,20},{20,24},{24,28},{28,32},{32,36}... | collective-permute-start | bytes 73736 | tf_op jit(solution)/shard_map/ppermute | solution.py:19
  9.6 1.6 %fusion.53 = (f32[1,1,2048]{2,1,0:T(1,128)S(1)}, f32[1,1,2048]{2,1,0:T(1,128)S(1)}, f32[1,1,2048]{2,1,0:T(1,128)S(1)}, f32[1,1,2048]{2,1,0:T(1,128)S(1)}, f32[1,...) fusion(f32[3,3,2048]{2,1,0:T(4,128)} %param.12), kind=kLoop, calls=%fused_computation.82 | loop fusion | bytes 147456 | tf_op jit(solution)/shard_map/slice | solution.py:25
  13.3 1.2 fusion.25
  14.4 4.2 %fusion.2 = bf16[128,128,128]{2,0,1:T(8,128)(2,1)} fusion(s32[128,128]{1,0:T(8,128)S(1)} %broadcast_subtract_fusion, s32[128]{0:T(128)S(1)} %iota.16, f32[128,128]{1,0:T(8,128)S(1)} %bitcast.55), kind=kOutput, calls=%fused_computation.2 | convolution fusion | flops 539000832 | bytes 4325888 | tf_op jit(solution)/shard_map/gs,sij->gij/dot_general | solution.py:48
  18.8 4.0 %fusion = bf16[128,128,128]{2,0,1:T(8,128)(2,1)} fusion(s32[128,128]{1,0:T(8,128)S(1)} %broadcast_subtract_fusion, s32[128]{0:T(128)S(1)} %iota.16, f32[128,128]{1,0:T(8,128)S(1)} %bitcast.56), kind=kOutput, calls=%fused_computation | convolution fusion | flops 539017216 | bytes 4325888 | tf_op jit(solution)/shard_map/gs,sij->gij/dot_general | solution.py:48
  24.1 7.0 %copy.22.high_ref = bf16[128,128,128]{2,1,0:T(8,128)(2,1)} copy(bf16[128,128,128]{2,0,1:T(8,128)(2,1)} %fusion.2) | data formatting | bytes 8388608 | tf_op jit(solution)/shard_map/gs,sij->gij/dot_general | solution.py:48
  31.1 4.7 %copy.23.low_ref = bf16[128,128,128]{2,1,0:T(8,128)(2,1)} copy(bf16[128,128,128]{2,0,1:T(8,128)(2,1)S(1)} %copy-done) | data formatting | bytes 8388608 | tf_op jit(solution)/shard_map/gs,sij->gij/dot_general | solution.py:48
  36.7 0.9 fusion.13.kv_ref
  38.4 13.7 %collective-permute-done.2 = bf16[512,2048]{1,0:T(8,128)(2,1)} collective-permute-done((bf16[512,2048]{1,0:T(8,128)(2,1)}, bf16[512,2048]{1,0:T(8,128)(2,1)}, u32[]{:S(2)}, u32[]{:S(2)}) %collective-permute-start.2) | collective-permute-done | bytes 2097184 | tf_op jit(solution)/shard_map/ppermute | solution.py:59
  52.0 2.7 %collective-permute-start.3 = (bf16[512,2048]{1,0:T(8,128)(2,1)}, bf16[512,2048]{1,0:T(8,128)(2,1)}, u32[]{:S(2)}, u32[]{:S(2)}) collective-permute-start(bf16[512,2048]{1,0:T(8,128)(2,1)} %collective-permute-done.2), channel_id=1, source_target_pairs={{0,1},{1,0},{2,3},{3,2},{4,5},{5,4},{6,7},{7,6},{8,9},{9,8},{10,11... | collective-permute-start | bytes 6291464 | tf_op jit(solution)/shard_map/ppermute | solution.py:61
  54.8 1.5 %convolution_add_fusion.3 = f32[128,16,16]{2,1,0:T(8,128)} fusion(f32[128,16,16]{2,1,0:T(8,128)S(1)} %fusion.30, bf16[128,128,16]{0,2,1:T(8,128)(2,1)S(1)} %bitcast.48, f32[128]{0:T(128)S(1)} %iota_subtract_fusion, f32[128,16]{1,0:T(8,128)S(1)} %copy.20), kind=kOutput, calls=%fused_computation.15 | convolution fusion | flops 9469952 | bytes 795136 | tf_op jit(solution)/shard_map/gnj,jgc->ngc/dot_general | solution.py:39
  56.2 1.5 %copy.29.ending_ref = f32[16,2048]{1,0:T(8,128)S(1)} copy(f32[16,2048]{0,1:T(8,128)} %bitcast.51) | data formatting | bytes 262144 | tf_op jit(solution)/shard_map/reshape | solution.py:221
  57.8 65.5 %shard_map.91 = (f32[16,2048]{1,0:T(8,128)S(1)}, f32[128,2048]{1,0:T(8,128)S(1)}) custom-call(f32[16,2048]{1,0:T(8,128)S(1)} %copy.29.ending_ref, f32[7,16,2048]{2,1,0:T(8,128)S(1)} %multiply_exponential_fusion.1.decay_ref, bf16[128,128,128]{2,1,0:T(8,128)(2,1)} %copy.22.high_ref, bf16[128,128,128]{2,1,0:T(8,128)(2,1)} %copy.23.low_ref, ...), custom_call_target="tpu_custom_call" | custom-call | tf_op jit(solution)/shard_map/pallas_call | solution.py:169
  123.3 1.3 copy.30
  124.6 2.8 %fusion.21 = f32[128,16,128]{2,1,0:T(8,128)S(1)} fusion(f32[16,128,16]{0,2,1:T(8,128)} %bitcast.49, f32[128,16]{1,0:T(8,128)} %copy.24, f32[128]{0:T(128)} %iota_add_fusion, f32[128,16]{1,0:T(8,128)} %copy-done.3), kind=kOutput, calls=%fused_computation.37 | convolution fusion | flops 50855936 | bytes 1196544 | tf_op jit(solution)/shard_map/gni,ngc->igc/dot_general | solution.py:230
  127.4 1.3 copy.26
  128.9 1.0 copy-done.1
  130.4 1.1 copy-done.2
  132.0 2.0 %convolution_add_fusion.2 = f32[128,2048]{1,0:T(8,128)S(1)} fusion(f32[128,2048]{1,0:T(8,128)S(1)} %fusion.42, bf16[512,2048]{1,0:T(8,128)(2,1)} %collective-permute-done.1, bf16[128,2048]{1,0:T(8,128)(2,1)S(1)} %fusion.19, s32[]{:T(128)S(6)} %select_n.13), kind=kOutput, calls=%fused_computation.10 | convolution fusion | flops 268697600 | bytes 4325380 | tf_op jit(solution)/shard_map/dot_general | solution.py:240
  134.0 2.0 %convolution_add_fusion.1 = f32[128,2048]{1,0:T(8,128)S(1)} fusion(f32[128,2048]{1,0:T(8,128)S(1)} %convolution_add_fusion.2, bf16[512,2048]{1,0:T(8,128)(2,1)} %collective-permute-done.2, bf16[128,2048]{1,0:T(8,128)(2,1)S(1)} %fusion.19, s32[]{:T(128)S(6)} %select_n.14), kind=kOutput, calls=%fused_computation.9 | convolution fusion | flops 268697600 | bytes 4325380 | tf_op jit(solution)/shard_map/dot_general | solution.py:240
  136.1 2.8 %fusion.9 = bf16[1,128,2048]{2,1,0:T(8,128)(2,1)} fusion(f32[128,2048]{1,0:T(8,128)S(1)} %convolution_add_fusion.1, bf16[512,2048]{1,0:T(8,128)(2,1)} %collective-permute-done.3, bf16[128,2048]{1,0:T(8,128)(2,1)S(1)} %fusion.19, s32[]{:T(128)S(6)} %select_n.15), kind=kOutput, calls=%fused_computation.12 | convolution fusion | flops 268959744 | bytes 3801092 | tf_op jit(solution)/shard_map/dot_general | solution.py:240
  (44 shorter events, 7.1 us)
Async XLA Ops:
  0.0 132.0 %collective-permute-start.1 = (bf16[512,2048]{1,0:T(8,128)(2,1)}, bf16[512,2048]{1,0:T(8,128)(2,1)}, u32[]{:S(2)}, u32[]{:S(2)}) collective-permute-start(bf16[512,2048]{1,0:T(8,128)(2,1)} %param.16), channel_id=1, source_target_pairs={{0,1},{1,0},{2,3},{3,2},{4,5},{5,4},{6,7},{7,6},{8,9},{9,8},{10,11... | collective-permute-start | bytes 6291464 | tf_op jit(solution)/shard_map/ppermute | solution.py:60
  2.6 49.5 %collective-permute-start.2 = (bf16[512,2048]{1,0:T(8,128)(2,1)}, bf16[512,2048]{1,0:T(8,128)(2,1)}, u32[]{:S(2)}, u32[]{:S(2)}) collective-permute-start(bf16[512,2048]{1,0:T(8,128)(2,1)} %param.16), channel_id=1, source_target_pairs={{0,2},{2,0},{1,3},{3,1},{4,6},{6,4},{5,7},{7,5},{8,10},{10,8},{9,1... | collective-permute-start | bytes 6291464 | tf_op jit(solution)/shard_map/ppermute | solution.py:59
  6.4 29.4 %collective-permute-start = (bf16[6,2048]{1,0:T(8,128)(2,1)S(1)}, bf16[6,2048]{1,0:T(8,128)(2,1)S(1)}, u32[]{:S(2)}, u32[]{:S(2)}) collective-permute-start(bf16[6,2048]{1,0:T(8,128)(2,1)S(1)} %pad_maximum_fusion), channel_id=1, source_target_pairs={{0,4},{4,8},{8,12},{12,16},{16,20},{20,24},{24,28},{28,32},{32,36}... | collective-permute-start | bytes 73736 | tf_op jit(solution)/shard_map/ppermute | solution.py:19
  12.1 42.7 %copy-start.3 = (f32[128,16]{1,0:T(8,128)}, f32[128,16]{1,0:T(8,128)S(1)}, u32[]{:S(2)}) copy-start(f32[128,16]{1,0:T(8,128)S(1)} %copy.20) | copy-start | bytes 24580
  14.4 4.2 %copy-start.10 = (f32[7]{0:T(128)S(1)}, f32[7]{0:T(128)}, u32[]{:S(2)}) copy-start(f32[7]{0:T(128)} %constant.30) | copy-start | bytes 88
  24.1 7.0 %copy-start = (bf16[128,128,128]{2,0,1:T(8,128)(2,1)S(1)}, bf16[128,128,128]{2,0,1:T(8,128)(2,1)}, u32[]{:S(2)}) copy-start(bf16[128,128,128]{2,0,1:T(8,128)(2,1)} %fusion) | copy-start | bytes 12582916
  31.1 5.3 %copy-start.4 = (bf16[1,128,2048]{2,1,0:T(8,128)(2,1)S(1)}, bf16[1,128,2048]{2,1,0:T(8,128)(2,1)}, u32[]{:S(2)}) copy-start(bf16[1,128,2048]{2,1,0:T(8,128)(2,1)} %param.10) | copy-start | bytes 1572868
  31.1 5.5 %copy-start.5 = (bf16[1,128,2048]{2,1,0:T(8,128)(2,1)S(1)}, bf16[1,128,2048]{2,1,0:T(8,128)(2,1)}, u32[]{:S(2)}) copy-start(bf16[1,128,2048]{2,1,0:T(8,128)(2,1)} %param.11) | copy-start | bytes 1572868
  52.0 84.0 %collective-permute-start.3 = (bf16[512,2048]{1,0:T(8,128)(2,1)}, bf16[512,2048]{1,0:T(8,128)(2,1)}, u32[]{:S(2)}, u32[]{:S(2)}) collective-permute-start(bf16[512,2048]{1,0:T(8,128)(2,1)} %collective-permute-done.2), channel_id=1, source_target_pairs={{0,1},{1,0},{2,3},{3,2},{4,5},{5,4},{6,7},{7,6},{8,9},{9,8},{10,11... | collective-permute-start | bytes 6291464 | tf_op jit(solution)/shard_map/ppermute | solution.py:61
  124.6 4.1 %copy-start.6 = (bf16[1,128,2048]{2,1,0:T(8,128)(2,1)S(1)}, bf16[1,128,2048]{2,1,0:T(8,128)(2,1)}, u32[]{:S(2)}) copy-start(bf16[1,128,2048]{2,1,0:T(8,128)(2,1)} %param.9) | copy-start | bytes 1572868
  124.6 4.1 %copy-start.8 = (bf16[2,2048]{1,0:T(2,128)(2,1)S(1)}, bf16[2,2048]{1,0:T(2,128)(2,1)}, u32[]{:S(2)}) copy-start(bf16[2,2048]{1,0:T(2,128)(2,1)} %get-tuple-element.20) | copy-start | bytes 24580
  127.4 1.5 %copy-start.7 = (f32[1,1,2048]{2,1,0:T(1,128)S(1)}, f32[1,1,2048]{2,1,0:T(1,128)}, u32[]{:S(2)}) copy-start(f32[1,1,2048]{2,1,0:T(1,128)} %get-tuple-element.15) | copy-start | bytes 24580
  127.4 1.5 %copy-start.9 = (f32[2048]{0:T(1024)S(1)}, f32[2048]{0:T(1024)}, u32[]{:S(2)}) copy-start(f32[2048]{0:T(1024)} %param.15) | copy-start | bytes 24580
  128.7 1.2 copy-start.1
  129.9 1.6 %copy-start.2 = (bf16[512,2048]{1,0:T(8,128)(2,1)S(1)}, bf16[512,2048]{1,0:T(8,128)(2,1)}, u32[]{:S(2)}) copy-start(bf16[512,2048]{1,0:T(8,128)(2,1)} %param.16) | copy-start | bytes 6291460

commit v7 on v6

--- a/solution.py
+++ b/solution.py
@@ -37,35 +37,6 @@
     high, low = split_bf16(table)
     first = jnp.einsum(spec, high, signal, preferred_element_type=jnp.float32)
     return first + jnp.einsum(spec, low, signal, preferred_element_type=jnp.float32)
-
-
-def toeplitz(kernel):
-    width = kernel.shape[1]
-    lag = lax.optimization_barrier(jnp.arange(width, dtype=jnp.int32))
-    diff = lag[:, None] - lag[None, :]
-    onehot = (lag[:, None, None] == diff[None, :, :]).astype(jnp.bfloat16)
-    return [
-        jnp.einsum("gs,sij->gij", part, onehot, preferred_element_type=jnp.bfloat16)
-        for part in split_bf16(kernel)
-    ]
-
-
-def gather_weight(out_weight):
-    pair = [(0, 1), (1, 0)]
-    chip = lax.axis_index("zlo")
-    core = lax.axis_index("core")
-    cores = lax.axis_size("core")
-    mine = chip * cores + core
-    remote = lax.ppermute(out_weight, "zlo", pair)
-    neighbour = lax.ppermute(out_weight, "core", pair)
-    relayed = lax.ppermute(remote, "core", pair)
-    other_chip = (1 - chip) * cores
-    return [
-        (mine, out_weight),
-        (chip * cores + 1 - core, neighbour),
-        (other_chip + core, remote),
-        (other_chip + 1 - core, relayed),
-    ]
 
 
 def scan_shifts(count):
@@ -79,19 +50,27 @@
 
 
 def conv_tiles(high_ref, low_ref, kv_ref, inner_ref, first_tile, last_tile):
-    lanes = kv_ref.shape[0]
+    width = kv_ref.shape[0]
     per_tile = 128 // GROUP
     owner = lax.broadcasted_iota(jnp.int32, (1, 128), 1) // GROUP
+    causal = lax.broadcasted_iota(jnp.int32, (width, width), 1) <= lax.broadcasted_iota(
+        jnp.int32, (width, width), 0
+    )
+
+    def toeplitz_part(ref, group):
+        row = ref[pl.ds(group, 1), :]
+        rolled = pltpu.roll(jnp.broadcast_to(row, (width, width)), 0, 1, stride=1, stride_axis=0)
+        return jnp.where(causal, rolled, 0.0).astype(jnp.bfloat16)
 
     def body(tile, carry):
         col = pl.multiple_of(tile * 128, 128)
         block = kv_ref[:, pl.ds(col, 128)]
-        total = jnp.zeros((lanes, 128), jnp.float32)
+        total = jnp.zeros((width, 128), jnp.float32)
         for member in range(per_tile):
             group = tile * per_tile + member
             part = jnp.where(owner == member, block, jnp.zeros_like(block))
-            total += jnp.dot(high_ref[group], part, preferred_element_type=jnp.float32)
-            total += jnp.dot(low_ref[group], part, preferred_element_type=jnp.float32)
+            total += jnp.dot(toeplitz_part(high_ref, group), part, preferred_element_type=jnp.float32)
+            total += jnp.dot(toeplitz_part(low_ref, group), part, preferred_element_type=jnp.float32)
         inner_ref[:, pl.ds(col, 128)] = total
         return carry
 
@@ -187,7 +166,17 @@
 
 
 def local(query_in, key_in, value_in, feature_taps, decay_rate, residues, skip_gain, out_weight):
-    weight_blocks = gather_weight(out_weight)
+    pair = [(0, 1), (1, 0)]
+    chip = lax.axis_index("zlo")
+    core = lax.axis_index("core")
+    cores = lax.axis_size("core")
+    other_chip = (1 - chip) * cores
+    remote = lax.ppermute(out_weight, "zlo", pair)
+    weight_blocks = [
+        (chip * cores + core, out_weight),
+        (chip * cores + 1 - core, lax.ppermute(out_weight, "core", pair)),
+        (other_chip + core, remote),
+    ]
     query_rows = query_in[0]
     key_rows = key_in[0]
     value_rows = value_in[0]
@@ -217,7 +206,9 @@
     closing = jnp.exp(-decay_rate[:, :, None] * (width - 1.0 - positions))
     lagged = jnp.exp(-decay_rate[:, :, None] * (positions + 1.0)) * scale[:, :, None]
 
-    high, low = toeplitz(kernel)
+    taps = jnp.roll(kernel[:, ::-1], 1, axis=1)
+    high = lax.reduce_precision(taps, exponent_bits=8, mantissa_bits=7)
+    low = lax.reduce_precision(taps - high, exponent_bits=8, mantissa_bits=7)
     ending = two_pass("gnj,jgc->ngc", closing, kv_grouped).reshape(-1, chans)
 
     first, later = scan_shifts(lax.axis_size("ctx"))
@@ -226,6 +217,8 @@
     rate_lanes = jnp.broadcast_to(jnp.transpose(decay_rate)[:, :, None], (modes, groups, GROUP))
     decay = jnp.exp(-rate_lanes.reshape(1, modes, chans) * spans)
     entering, inner = scan_states(ending, decay, high, low, kv_round)
+    entering, remote = lax.optimization_barrier((entering, remote))
+    weight_blocks.append((other_chip + 1 - core, lax.ppermute(remote, "core", [(0, 1), (1, 0)])))
     entering = entering.reshape(-1, groups, GROUP)
     crossing = jnp.einsum("gni,ngc->igc", lagged, entering, precision=exact_precision)
     convolved = (inner + crossing.reshape(width, chans)).astype(jnp.bfloat16)

time: 140 us -> 119 us (0.85)
  the two profiles are of different devices: /device:TPU:333 before, /device:TPU:389 now
where the time goes in v7:
time: 119 us; the launch traced here: 118 us
  Pallas kernels  73.3 us (62%)
  starting transfers between devices  15.5 us (13%)
  matrix products  14.2 us (12%)
  local copies, waits for them, and re-layouts  10.6 us (9%)
  other arithmetic  4.06 us (3%)
    pallas_call x1, Pallas kernels, scan_states(): pl.pallas_call(functools.partial(scan_kernel, count), out_shape=(jax.Shap...  73.3 us
    dot_general x4, matrix products, local(): term = jnp.dot(columns, weight, preferred_element_type=jnp.float32)  7.41 us
    ppermute x1, starting transfers between devices, local(): lax.ppermute(remote, 'core', [(0, 1), (1, 0)])  6.34 us
    dot_general x1, matrix products, local(): jnp.einsum('gni,ngc->igc', lagged, entering, precision=exact_precision)  3.63 us
    ppermute x1, starting transfers between devices, shifted(): return lax.ppermute(shard, axis, pairs)  3.2 us
    ppermute x1, starting transfers between devices, local(): remote = lax.ppermute(out_weight, 'zlo', pair)  3.09 us
    ppermute x1, starting transfers between devices, local(): lax.ppermute(out_weight, 'core', pair)  2.87 us
    reshape x1, local copies, waits for them, and re-layouts, local(): convolved = (inner + crossing.reshape(width, chans)).astype(jnp.bfloat16)  2.59 us
  transfers between devices with their start and end apart: 4, of which 0 were waited for; matrix products, arithmetic and copies ran while one was open for 20% of the time, Pallas kernels for 62%

profile of v7, /device:TPU:389, one launch (start us, length us, event | category | flops | bytes accessed | tf_op | source)
XLA Modules:
  0.0 117.9 jit_solution(8801795309087848586)
XLA Ops:
  0.0 3.1 %collective-permute-start.1 = (bf16[512,2048]{1,0:T(8,128)(2,1)}, bf16[512,2048]{1,0:T(8,128)(2,1)}, u32[]{:S(2)}, u32[]{:S(2)}) collective-permute-start(bf16[512,2048]{1,0:T(8,128)(2,1)} %param.16), channel_id=1, source_target_pairs={{0,2},{2,0},{1,3},{3,1},{4,6},{6,4},{5,7},{7,5},{8,10},{10,8},{9,1... | collective-permute-start | bytes 6291464 | tf_op jit(solution)/shard_map/ppermute | solution.py:174
  3.1 2.9 %collective-permute-start.2 = (bf16[512,2048]{1,0:T(8,128)(2,1)}, bf16[512,2048]{1,0:T(8,128)(2,1)}, u32[]{:S(2)}, u32[]{:S(2)}) collective-permute-start(bf16[512,2048]{1,0:T(8,128)(2,1)} %param.16), channel_id=1, source_target_pairs={{0,1},{1,0},{2,3},{3,2},{4,5},{5,4},{6,7},{7,6},{8,9},{9,8},{10,11... | collective-permute-start | bytes 6291464 | tf_op jit(solution)/shard_map/ppermute | solution.py:177
  6.0 0.8 slice_bitcast_fusion.2
  6.8 0.8 slice_bitcast_fusion
  7.6 3.2 %collective-permute-start = (bf16[6,2048]{1,0:T(8,128)(2,1)S(1)}, bf16[6,2048]{1,0:T(8,128)(2,1)S(1)}, u32[]{:S(2)}, u32[]{:S(2)}) collective-permute-start(bf16[6,2048]{1,0:T(8,128)(2,1)S(1)} %pad_maximum_fusion.1), channel_id=1, source_target_pairs={{0,4},{4,8},{8,12},{12,16},{16,20},{20,24},{24,28},{28,32},{32,36}... | collective-permute-start | bytes 73736 | tf_op jit(solution)/shard_map/ppermute | solution.py:19
  10.8 1.0 fusion.43
  11.8 0.7 sqrt_multiply_fusion
  12.7 1.2 fusion.18
  14.4 0.6 neg.24
  15.6 0.8 copy-done.2
  16.6 0.7 fusion.6.kv_ref
  17.5 0.5 fusion.23
  18.0 1.5 %convolution_add_fusion.2 = f32[128,16,16]{2,1,0:T(8,128)} fusion(f32[128,16,16]{2,1,0:T(8,128)S(1)} %fusion.23, bf16[128,128,16]{0,2,1:T(8,128)(2,1)S(1)} %bitcast.43, f32[128]{0:T(128)S(1)} %iota_subtract_fusion, f32[128,16]{1,0:T(8,128)S(1)} %copy.18), kind=kOutput, calls=%fused_computation.7 | convolution fusion | flops 9469952 | bytes 795136 | tf_op jit(solution)/shard_map/gnj,jgc->ngc/dot_general | solution.py:39
  19.5 1.5 %copy.25.ending_ref = f32[16,2048]{1,0:T(8,128)S(1)} copy(f32[16,2048]{0,1:T(8,128)} %bitcast.46) | data formatting | bytes 262144 | tf_op jit(solution)/shard_map/reshape | solution.py:212
  21.1 73.3 %shard_map.91 = (f32[16,2048]{1,0:T(8,128)S(1)}, f32[128,2048]{1,0:T(8,128)S(1)}) custom-call(f32[16,2048]{1,0:T(8,128)S(1)} %copy.25.ending_ref, f32[7,16,2048]{2,1,0:T(8,128)S(1)} %multiply_exponential_fusion.1.decay_ref, f32[128,128]{1,0:T(8,128)S(1)} %get-tuple-element.14.high_ref, f32[128,128]{1,0:T(8,128)S(1)} %get-tuple-element.13.low_ref, ...), custom_call_target="tpu_custom_call" | custom-call | tf_op jit(solution)/shard_map/pallas_call | solution.py:148
  94.3 6.3 %collective-permute-start.3 = (bf16[512,2048]{1,0:T(8,128)(2,1)}, bf16[512,2048]{1,0:T(8,128)(2,1)}, u32[]{:S(2)}, u32[]{:S(2)}) collective-permute-start(bf16[512,2048]{1,0:T(8,128)(2,1)} %collective-permute-done.1), channel_id=1, source_target_pairs={{0,1},{1,0},{2,3},{3,2},{4,5},{5,4},{6,7},{7,6},{8,9},{9,8},{10,11... | collective-permute-start | bytes 6291464 | tf_op jit(solution)/shard_map/ppermute | solution.py:221
  101.0 1.4 %copy.26 = f32[16,2048]{0,1:T(8,128)} copy(f32[16,2048]{1,0:T(8,128)S(1)} %get-tuple-element.11) | data formatting | bytes 262144 | tf_op jit(solution)/shard_map/reshape | solution.py:222
  102.3 3.6 %fusion.14 = f32[128,16,128]{2,1,0:T(8,128)} fusion(f32[16,128,16]{0,2,1:T(8,128)} %bitcast.44, f32[128,16]{1,0:T(8,128)S(1)} %copy.20, f32[128]{0:T(128)S(1)} %iota_add_fusion, f32[128,16]{1,0:T(8,128)S(1)} %copy.18), kind=kOutput, calls=%fused_computation.29 | convolution fusion | flops 50855936 | bytes 1196544 | tf_op jit(solution)/shard_map/gni,ngc->igc/dot_general | solution.py:223
  106.0 2.6 %copy.22 = f32[128,2048]{1,0:T(8,128)} copy(f32[128,2048]{0,1:T(8,128)} %bitcast.45) | data formatting | bytes 2097152 | tf_op jit(solution)/shard_map/reshape | solution.py:224
  108.6 1.9 %fusion.12 = bf16[128,2048]{1,0:T(8,128)(2,1)S(1)} fusion(f32[130,2048]{1,0:T(8,128)S(1)} %maximum_convert_fusion, bf16[128,2048]{1,0:T(8,128)(2,1)S(1)} %fusion.6.kv_ref, f32[128,2048]{1,0:T(8,128)S(1)} %get-tuple-element.9, f32[128,2048]{1,0:T(8,128)} %copy.22, f32[2048]{0:T(1024)S(1)} %copy-done.4, f32[2048]{0:T(1024)S(1)} %bitcast.54, ...), kind=kLoop, calls=%fused_computation.24 | loop fusion | flops 3407872 | bytes 6324224 | tf_op jit(solution)/shard_map/convert_element_type | solution.py:228
  110.5 0.4 fusion.36
  110.9 2.0 %convolution_add_fusion.1 = f32[128,2048]{1,0:T(8,128)S(1)} fusion(f32[128,2048]{1,0:T(8,128)S(1)} %fusion.36, bf16[512,2048]{1,0:T(8,128)(2,1)} %collective-permute-done.2, bf16[128,2048]{1,0:T(8,128)(2,1)S(1)} %fusion.12, s32[]{:T(128)S(6)} %select_n.13), kind=kOutput, calls=%fused_computation.2 | convolution fusion | flops 268697600 | bytes 4325380 | tf_op jit(solution)/shard_map/dot_general | solution.py:233
  113.0 2.0 %fusion.32 = f32[128,2048]{1,0:T(8,128)S(1)} fusion(bf16[512,2048]{1,0:T(8,128)(2,1)} %collective-permute-done.3, bf16[128,2048]{1,0:T(8,128)(2,1)S(1)} %fusion.12, s32[]{:T(128)S(6)} %select_n.15), kind=kOutput, calls=%fused_computation.51 | convolution fusion | flops 268435456 | bytes 3276804 | tf_op jit(solution)/shard_map/dot_general | solution.py:233
  115.0 2.9 %fusion.2 = bf16[1,128,2048]{2,1,0:T(8,128)(2,1)} fusion(f32[128,2048]{1,0:T(8,128)S(1)} %fusion.32, f32[128,2048]{1,0:T(8,128)S(1)} %convolution_add_fusion.1, bf16[512,2048]{1,0:T(8,128)(2,1)} %collective-permute-done.1, bf16[128,2048]{1,0:T(8,128)(2,1)S(1)} %fusion.12, s32[]{:T(128)S(6)} %select_n.14), kind=kOutput, calls=%fused_computation.4 | convolution fusion | flops 269221888 | bytes 4849668 | tf_op jit(solution)/shard_map/dot_general | solution.py:233
  (31 shorter events, 1.9 us)
Async XLA Ops:
  0.0 94.3 %collective-permute-start.1 = (bf16[512,2048]{1,0:T(8,128)(2,1)}, bf16[512,2048]{1,0:T(8,128)(2,1)}, u32[]{:S(2)}, u32[]{:S(2)}) collective-permute-start(bf16[512,2048]{1,0:T(8,128)(2,1)} %param.16), channel_id=1, source_target_pairs={{0,2},{2,0},{1,3},{3,1},{4,6},{6,4},{5,7},{7,5},{8,10},{10,8},{9,1... | collective-permute-start | bytes 6291464 | tf_op jit(solution)/shard_map/ppermute | solution.py:174
  3.1 107.8 %collective-permute-start.2 = (bf16[512,2048]{1,0:T(8,128)(2,1)}, bf16[512,2048]{1,0:T(8,128)(2,1)}, u32[]{:S(2)}, u32[]{:S(2)}) collective-permute-start(bf16[512,2048]{1,0:T(8,128)(2,1)} %param.16), channel_id=1, source_target_pairs={{0,1},{1,0},{2,3},{3,2},{4,5},{5,4},{6,7},{7,6},{8,9},{9,8},{10,11... | collective-permute-start | bytes 6291464 | tf_op jit(solution)/shard_map/ppermute | solution.py:177
  7.6 7.8 %collective-permute-start = (bf16[6,2048]{1,0:T(8,128)(2,1)S(1)}, bf16[6,2048]{1,0:T(8,128)(2,1)S(1)}, u32[]{:S(2)}, u32[]{:S(2)}) collective-permute-start(bf16[6,2048]{1,0:T(8,128)(2,1)S(1)} %pad_maximum_fusion.1), channel_id=1, source_target_pairs={{0,4},{4,8},{8,12},{12,16},{16,20},{20,24},{24,28},{28,32},{32,36}... | collective-permute-start | bytes 73736 | tf_op jit(solution)/shard_map/ppermute | solution.py:19
  14.1 1.1 copy-start.5
  14.4 1.0 copy-start.1
  15.4 1.1 copy-start.2
  21.1 79.8 %copy-start.3 = (bf16[1,128,2048]{2,1,0:T(8,128)(2,1)S(1)}, bf16[1,128,2048]{2,1,0:T(8,128)(2,1)}, u32[]{:S(2)}) copy-start(bf16[1,128,2048]{2,1,0:T(8,128)(2,1)} %param.9) | copy-start | bytes 1572868
  94.3 18.6 %collective-permute-start.3 = (bf16[512,2048]{1,0:T(8,128)(2,1)}, bf16[512,2048]{1,0:T(8,128)(2,1)}, u32[]{:S(2)}, u32[]{:S(2)}) collective-permute-start(bf16[512,2048]{1,0:T(8,128)(2,1)} %collective-permute-done.1), channel_id=1, source_target_pairs={{0,1},{1,0},{2,3},{3,2},{4,5},{5,4},{6,7},{7,6},{8,9},{9,8},{10,11... | collective-permute-start | bytes 6291464 | tf_op jit(solution)/shard_map/ppermute | solution.py:221
  106.0 2.6 %copy-start.4 = (f32[2048]{0:T(1024)S(1)}, f32[2048]{0:T(1024)}, u32[]{:S(2)}) copy-start(f32[2048]{0:T(1024)} %param.15) | copy-start | bytes 24580
  108.5 1.9 %copy-start = (bf16[512,2048]{1,0:T(8,128)(2,1)S(1)}, bf16[512,2048]{1,0:T(8,128)(2,1)}, u32[]{:S(2)}) copy-start(bf16[512,2048]{1,0:T(8,128)(2,1)} %param.16) | copy-start | bytes 6291460

commit v8 on v7

--- a/solution.py
+++ b/solution.py
@@ -78,11 +78,12 @@
 
 
 def scan_kernel(
-    count, ending_ref, decay_ref, high_ref, low_ref, kv_ref, entering_ref, inner_ref, sent, landed, send_sem, recv_sem
+    count, parts, ending_ref, decay_ref, high_ref, low_ref, kv_ref, entering_ref, inner_ref, sent, landed, send_sem, recv_sem
 ):
     me = lax.axis_index("ctx")
     first, later = scan_shifts(count)
     partners = sorted(set(first + later))
+    share = ending_ref.shape[1] // parts
 
     barrier = pltpu.get_barrier_semaphore()
     for span in partners:
@@ -90,14 +91,14 @@
             pl.semaphore_signal(barrier, inc=1, device_id={"ctx": target}, device_id_type=pl.DeviceIdType.MESH)
     pl.semaphore_wait(barrier, 2 * len(partners))
 
-    copies = []
-
-    def send(source, slot, span):
+    started = []
+
+    def send(source, slot, part, span):
         copy = pltpu.make_async_remote_copy(
             src_ref=source,
-            dst_ref=landed.at[slot],
-            send_sem=send_sem.at[slot],
-            recv_sem=recv_sem.at[slot],
+            dst_ref=landed.at[slot, part],
+            send_sem=send_sem.at[slot, part],
+            recv_sem=recv_sem.at[slot, part],
             device_id={"ctx": lax.rem(me + span, count)},
             device_id_type=pl.DeviceIdType.MESH,
         )
@@ -106,47 +107,60 @@
         def _():
             copy.start()
 
-        copies.append((copy, span))
-        return copy
-
-    def take(copy, slot, span, factor):
+        started.append((copy, span))
+        return (copy, slot, part, span)
+
+    def take(copy, slot, part, span, factor):
+        columns = pl.ds(part * share, share)
+
         @pl.when(me >= span)
         def _():
             copy.wait_recv()
             if factor is None:
-                entering_ref[...] += landed[slot]
+                entering_ref[:, columns] += landed[slot, part]
             else:
-                entering_ref[...] += factor * landed[slot]
+                entering_ref[:, columns] += decay_ref[factor, :, columns] * landed[slot, part]
 
     tiles = kv_ref.shape[1] // 128
     rounds = 1 + len(later)
     bounds = [tiles * step // rounds for step in range(rounds + 1)]
 
     entering_ref[...] = jnp.zeros(entering_ref.shape, jnp.float32)
-    opening = [send(ending_ref, slot, span) for slot, span in enumerate(first)]
+    pending = []
+    for part in range(parts):
+        columns = pl.ds(part * share, share)
+        pending.append(
+            [
+                send(ending_ref.at[:, columns], slot, part, span) + (None if slot == 0 else 0,)
+                for slot, span in enumerate(first)
+            ]
+        )
     conv_tiles(high_ref, low_ref, kv_ref, inner_ref, bounds[0], bounds[1])
-    for slot, span in enumerate(first):
-        take(opening[slot], slot, span, None if slot == 0 else decay_ref[0])
-    for step, span in enumerate(later):
-        slot = len(first) + step
-        sent[step] = entering_ref[...]
-        copy = send(sent.at[step], slot, span)
-        conv_tiles(high_ref, low_ref, kv_ref, inner_ref, bounds[step + 1], bounds[step + 2])
-        take(copy, slot, span, decay_ref[step + 1])
-    for copy, span in copies:
+    for step in range(len(later) + 1):
+        for part in range(parts):
+            for copy, slot, owner, span, factor in pending[part]:
+                take(copy, slot, owner, span, factor)
+            if step < len(later):
+                slot = len(first) + step
+                sent[step, part] = entering_ref[:, pl.ds(part * share, share)]
+                pending[part] = [send(sent.at[step, part], slot, part, later[step]) + (step + 1,)]
+        if step < len(later):
+            conv_tiles(high_ref, low_ref, kv_ref, inner_ref, bounds[step + 1], bounds[step + 2])
+    for copy, span in started:
 
         @pl.when(me + span < count)
         def _():
             copy.wait_send()
 
 
-def scan_states(ending, decay, high, low, kv):
+def scan_states(ending, decay, high, low, kv, parts=2):
     count = lax.axis_size("ctx")
     first, later = scan_shifts(count)
     slots = len(first) + len(later)
+    share = (ending.shape[0], ending.shape[1] // parts)
     vmem = pl.BlockSpec(memory_space=pltpu.VMEM)
     return pl.pallas_call(
-        functools.partial(scan_kernel, count),
+        functools.partial(scan_kernel, count, parts),
         out_shape=(
             jax.ShapeDtypeStruct(ending.shape, jnp.float32),
             jax.ShapeDtypeStruct(kv.shape, jnp.float32),
@@ -154,10 +168,10 @@
         in_specs=[vmem] * 5,
         out_specs=(vmem, vmem),
         scratch_shapes=[
-            pltpu.VMEM((max(1, len(later)),) + ending.shape, jnp.float32),
-            pltpu.VMEM((slots,) + ending.shape, jnp.float32),
-            pltpu.SemaphoreType.DMA((slots,)),
-            pltpu.SemaphoreType.DMA((slots,)),
+            pltpu.VMEM((max(1, len(later)), parts) + share, jnp.float32),
+            pltpu.VMEM((slots, parts) + share, jnp.float32),
+            pltpu.SemaphoreType.DMA((slots, parts)),
+            pltpu.SemaphoreType.DMA((slots, parts)),
         ],
         compiler_params=pltpu.CompilerParams(
             collective_id=0, has_side_effects=True, vmem_limit_bytes=48 * 1024 * 1024

time: 119 us -> 117 us (0.983)
  Pallas kernels: 73.3 us -> 72 us
    pallas_call x1, Pallas kernels: 73.3 us -> 72 us  [scan_states(): pl.pallas_call(functools.partial(scan_kernel, count, parts), out_shape=(j...]
where the time goes in v8:
time: 117 us
  Pallas kernels  72 us (62%)
  starting transfers between devices  15.5 us (13%)
  matrix products  14.2 us (12%)
  local copies, waits for them, and re-layouts  10.6 us (9%)
  other arithmetic  4.06 us (3%)
    pallas_call x1, Pallas kernels, scan_states(): pl.pallas_call(functools.partial(scan_kernel, count, parts), out_shape=(j...  72 us
    dot_general x4, matrix products, local(): term = jnp.dot(columns, weight, preferred_element_type=jnp.float32)  7.41 us
    ppermute x1, starting transfers between devices, local(): lax.ppermute(remote, 'core', [(0, 1), (1, 0)])  6.34 us
    dot_general x1, matrix products, local(): jnp.einsum('gni,ngc->igc', lagged, entering, precision=exact_precision)  3.63 us
    ppermute x1, starting transfers between devices, shifted(): return lax.ppermute(shard, axis, pairs)  3.2 us
    ppermute x1, starting transfers between devices, local(): remote = lax.ppermute(out_weight, 'zlo', pair)  3.09 us
    ppermute x1, starting transfers between devices, local(): lax.ppermute(out_weight, 'core', pair)  2.87 us
    reshape x1, local copies, waits for them, and re-layouts, local(): convolved = (inner + crossing.reshape(width, chans)).astype(jnp.bfloat16)  2.59 us
  transfers between devices with their start and end apart: 4, of which 0 were waited for; matrix products, arithmetic and copies ran while one was open for 20% of the time, Pallas kernels for 62%

profile of v8, /device:TPU:389, one launch (start us, length us, event | category | flops | bytes accessed | tf_op | source)
XLA Modules:
  0.0 116.7 jit_solution(5788914712961049677)
XLA Ops:
  0.0 3.1 %collective-permute-start.1 = (bf16[512,2048]{1,0:T(8,128)(2,1)}, bf16[512,2048]{1,0:T(8,128)(2,1)}, u32[]{:S(2)}, u32[]{:S(2)}) collective-permute-start(bf16[512,2048]{1,0:T(8,128)(2,1)} %param.16), channel_id=1, source_target_pairs={{0,2},{2,0},{1,3},{3,1},{4,6},{6,4},{5,7},{7,5},{8,10},{10,8},{9,1... | collective-permute-start | bytes 6291464 | tf_op jit(solution)/shard_map/ppermute | solution.py:188
  3.1 2.9 %collective-permute-start.2 = (bf16[512,2048]{1,0:T(8,128)(2,1)}, bf16[512,2048]{1,0:T(8,128)(2,1)}, u32[]{:S(2)}, u32[]{:S(2)}) collective-permute-start(bf16[512,2048]{1,0:T(8,128)(2,1)} %param.16), channel_id=1, source_target_pairs={{0,1},{1,0},{2,3},{3,2},{4,5},{5,4},{6,7},{7,6},{8,9},{9,8},{10,11... | collective-permute-start | bytes 6291464 | tf_op jit(solution)/shard_map/ppermute | solution.py:191
  6.0 0.8 slice_bitcast_fusion.2
  6.8 0.8 slice_bitcast_fusion
  7.6 3.2 %collective-permute-start = (bf16[6,2048]{1,0:T(8,128)(2,1)S(1)}, bf16[6,2048]{1,0:T(8,128)(2,1)S(1)}, u32[]{:S(2)}, u32[]{:S(2)}) collective-permute-start(bf16[6,2048]{1,0:T(8,128)(2,1)S(1)} %pad_maximum_fusion.1), channel_id=1, source_target_pairs={{0,4},{4,8},{8,12},{12,16},{16,20},{20,24},{24,28},{28,32},{32,36}... | collective-permute-start | bytes 73736 | tf_op jit(solution)/shard_map/ppermute | solution.py:19
  10.8 1.0 fusion.43
  11.8 0.7 sqrt_multiply_fusion
  12.7 1.2 fusion.18
  14.4 0.6 neg.24
  15.6 0.8 copy-done.2
  16.6 0.7 fusion.6.kv_ref
  17.5 0.5 fusion.23
  18.0 1.5 %convolution_add_fusion.2 = f32[128,16,16]{2,1,0:T(8,128)} fusion(f32[128,16,16]{2,1,0:T(8,128)S(1)} %fusion.23, bf16[128,128,16]{0,2,1:T(8,128)(2,1)S(1)} %bitcast.43, f32[128]{0:T(128)S(1)} %iota_subtract_fusion, f32[128,16]{1,0:T(8,128)S(1)} %copy.18), kind=kOutput, calls=%fused_computation.7 | convolution fusion | flops 9469952 | bytes 795136 | tf_op jit(solution)/shard_map/gnj,jgc->ngc/dot_general | solution.py:39
  19.5 1.5 %copy.25.ending_ref = f32[16,2048]{1,0:T(8,128)S(1)} copy(f32[16,2048]{0,1:T(8,128)} %bitcast.46) | data formatting | bytes 262144 | tf_op jit(solution)/shard_map/reshape | solution.py:226
  21.1 72.0 %shard_map.91 = (f32[16,2048]{1,0:T(8,128)S(1)}, f32[128,2048]{1,0:T(8,128)S(1)}) custom-call(f32[16,2048]{1,0:T(8,128)S(1)} %copy.25.ending_ref, f32[7,16,2048]{2,1,0:T(8,128)S(1)} %multiply_exponential_fusion.1.decay_ref, f32[128,128]{1,0:T(8,128)S(1)} %get-tuple-element.14.high_ref, f32[128,128]{1,0:T(8,128)S(1)} %get-tuple-element.13.low_ref, ...), custom_call_target="tpu_custom_call" | custom-call | tf_op jit(solution)/shard_map/pallas_call | solution.py:162
  93.1 6.3 %collective-permute-start.3 = (bf16[512,2048]{1,0:T(8,128)(2,1)}, bf16[512,2048]{1,0:T(8,128)(2,1)}, u32[]{:S(2)}, u32[]{:S(2)}) collective-permute-start(bf16[512,2048]{1,0:T(8,128)(2,1)} %collective-permute-done.1), channel_id=1, source_target_pairs={{0,1},{1,0},{2,3},{3,2},{4,5},{5,4},{6,7},{7,6},{8,9},{9,8},{10,11... | collective-permute-start | bytes 6291464 | tf_op jit(solution)/shard_map/ppermute | solution.py:235
  99.7 1.4 %copy.26 = f32[16,2048]{0,1:T(8,128)} copy(f32[16,2048]{1,0:T(8,128)S(1)} %get-tuple-element.11) | data formatting | bytes 262144 | tf_op jit(solution)/shard_map/reshape | solution.py:236
  101.1 3.6 %fusion.14 = f32[128,16,128]{2,1,0:T(8,128)} fusion(f32[16,128,16]{0,2,1:T(8,128)} %bitcast.44, f32[128,16]{1,0:T(8,128)S(1)} %copy.20, f32[128]{0:T(128)S(1)} %iota_add_fusion, f32[128,16]{1,0:T(8,128)S(1)} %copy.18), kind=kOutput, calls=%fused_computation.29 | convolution fusion | flops 50855936 | bytes 1196544 | tf_op jit(solution)/shard_map/gni,ngc->igc/dot_general | solution.py:237
  104.7 2.6 %copy.22 = f32[128,2048]{1,0:T(8,128)} copy(f32[128,2048]{0,1:T(8,128)} %bitcast.45) | data formatting | bytes 2097152 | tf_op jit(solution)/shard_map/reshape | solution.py:238
  107.3 1.9 %fusion.12 = bf16[128,2048]{1,0:T(8,128)(2,1)S(1)} fusion(f32[130,2048]{1,0:T(8,128)S(1)} %maximum_convert_fusion, bf16[128,2048]{1,0:T(8,128)(2,1)S(1)} %fusion.6.kv_ref, f32[128,2048]{1,0:T(8,128)S(1)} %get-tuple-element.9, f32[128,2048]{1,0:T(8,128)} %copy.22, f32[2048]{0:T(1024)S(1)} %copy-done.4, f32[2048]{0:T(1024)S(1)} %bitcast.54, ...), kind=kLoop, calls=%fused_computation.24 | loop fusion | flops 3407872 | bytes 6324224 | tf_op jit(solution)/shard_map/convert_element_type | solution.py:242
  109.2 0.4 fusion.36
  109.7 2.0 %convolution_add_fusion.1 = f32[128,2048]{1,0:T(8,128)S(1)} fusion(f32[128,2048]{1,0:T(8,128)S(1)} %fusion.36, bf16[512,2048]{1,0:T(8,128)(2,1)} %collective-permute-done.2, bf16[128,2048]{1,0:T(8,128)(2,1)S(1)} %fusion.12, s32[]{:T(128)S(6)} %select_n.13), kind=kOutput, calls=%fused_computation.2 | convolution fusion | flops 268697600 | bytes 4325380 | tf_op jit(solution)/shard_map/dot_general | solution.py:247
  111.7 2.0 %fusion.32 = f32[128,2048]{1,0:T(8,128)S(1)} fusion(bf16[512,2048]{1,0:T(8,128)(2,1)} %collective-permute-done.3, bf16[128,2048]{1,0:T(8,128)(2,1)S(1)} %fusion.12, s32[]{:T(128)S(6)} %select_n.15), kind=kOutput, calls=%fused_computation.51 | convolution fusion | flops 268435456 | bytes 3276804 | tf_op jit(solution)/shard_map/dot_general | solution.py:247
  113.8 2.9 %fusion.2 = bf16[1,128,2048]{2,1,0:T(8,128)(2,1)} fusion(f32[128,2048]{1,0:T(8,128)S(1)} %fusion.32, f32[128,2048]{1,0:T(8,128)S(1)} %convolution_add_fusion.1, bf16[512,2048]{1,0:T(8,128)(2,1)} %collective-permute-done.1, bf16[128,2048]{1,0:T(8,128)(2,1)S(1)} %fusion.12, s32[]{:T(128)S(6)} %select_n.14), kind=kOutput, calls=%fused_computation.4 | convolution fusion | flops 269221888 | bytes 4849668 | tf_op jit(solution)/shard_map/dot_general | solution.py:247
  (31 shorter events, 1.9 us)
Async XLA Ops:
  0.0 93.1 %collective-permute-start.1 = (bf16[512,2048]{1,0:T(8,128)(2,1)}, bf16[512,2048]{1,0:T(8,128)(2,1)}, u32[]{:S(2)}, u32[]{:S(2)}) collective-permute-start(bf16[512,2048]{1,0:T(8,128)(2,1)} %param.16), channel_id=1, source_target_pairs={{0,2},{2,0},{1,3},{3,1},{4,6},{6,4},{5,7},{7,5},{8,10},{10,8},{9,1... | collective-permute-start | bytes 6291464 | tf_op jit(solution)/shard_map/ppermute | solution.py:188
  3.1 106.5 %collective-permute-start.2 = (bf16[512,2048]{1,0:T(8,128)(2,1)}, bf16[512,2048]{1,0:T(8,128)(2,1)}, u32[]{:S(2)}, u32[]{:S(2)}) collective-permute-start(bf16[512,2048]{1,0:T(8,128)(2,1)} %param.16), channel_id=1, source_target_pairs={{0,1},{1,0},{2,3},{3,2},{4,5},{5,4},{6,7},{7,6},{8,9},{9,8},{10,11... | collective-permute-start | bytes 6291464 | tf_op jit(solution)/shard_map/ppermute | solution.py:191
  7.6 7.8 %collective-permute-start = (bf16[6,2048]{1,0:T(8,128)(2,1)S(1)}, bf16[6,2048]{1,0:T(8,128)(2,1)S(1)}, u32[]{:S(2)}, u32[]{:S(2)}) collective-permute-start(bf16[6,2048]{1,0:T(8,128)(2,1)S(1)} %pad_maximum_fusion.1), channel_id=1, source_target_pairs={{0,4},{4,8},{8,12},{12,16},{16,20},{20,24},{24,28},{28,32},{32,36}... | collective-permute-start | bytes 73736 | tf_op jit(solution)/shard_map/ppermute | solution.py:19
  14.1 1.1 copy-start.5
  14.4 1.0 copy-start.1
  15.4 1.1 copy-start.2
  21.1 78.5 %copy-start.3 = (bf16[1,128,2048]{2,1,0:T(8,128)(2,1)S(1)}, bf16[1,128,2048]{2,1,0:T(8,128)(2,1)}, u32[]{:S(2)}) copy-start(bf16[1,128,2048]{2,1,0:T(8,128)(2,1)} %param.9) | copy-start | bytes 1572868
  93.1 18.6 %collective-permute-start.3 = (bf16[512,2048]{1,0:T(8,128)(2,1)}, bf16[512,2048]{1,0:T(8,128)(2,1)}, u32[]{:S(2)}, u32[]{:S(2)}) collective-permute-start(bf16[512,2048]{1,0:T(8,128)(2,1)} %collective-permute-done.1), channel_id=1, source_target_pairs={{0,1},{1,0},{2,3},{3,2},{4,5},{5,4},{6,7},{7,6},{8,9},{9,8},{10,11... | collective-permute-start | bytes 6291464 | tf_op jit(solution)/shard_map/ppermute | solution.py:235
  104.7 2.6 %copy-start.4 = (f32[2048]{0:T(1024)S(1)}, f32[2048]{0:T(1024)}, u32[]{:S(2)}) copy-start(f32[2048]{0:T(1024)} %param.15) | copy-start | bytes 24580
  107.3 1.9 %copy-start = (bf16[512,2048]{1,0:T(8,128)(2,1)S(1)}, bf16[512,2048]{1,0:T(8,128)(2,1)}, u32[]{:S(2)}) copy-start(bf16[512,2048]{1,0:T(8,128)(2,1)} %param.16) | copy-start | bytes 6291460

commit v9 on v8

--- a/solution.py
+++ b/solution.py
@@ -78,18 +78,52 @@
 
 
 def scan_kernel(
-    count, parts, ending_ref, decay_ref, high_ref, low_ref, kv_ref, entering_ref, inner_ref, sent, landed, send_sem, recv_sem
+    count,
+    parts,
+    ending_ref,
+    decay_ref,
+    high_ref,
+    low_ref,
+    kv_ref,
+    weight_ref,
+    entering_ref,
+    inner_ref,
+    blocks_ref,
+    sent,
+    landed,
+    send_sem,
+    recv_sem,
+    weight_send,
+    weight_recv,
 ):
     me = lax.axis_index("ctx")
     first, later = scan_shifts(count)
     partners = sorted(set(first + later))
     share = ending_ref.shape[1] // parts
+    core_partner = {"core": 1 - lax.axis_index("core")}
+    chip_partner = {"zlo": 1 - lax.axis_index("zlo")}
 
     barrier = pltpu.get_barrier_semaphore()
     for span in partners:
         for target in (lax.rem(me + span, count), lax.rem(me + count - span, count)):
             pl.semaphore_signal(barrier, inc=1, device_id={"ctx": target}, device_id_type=pl.DeviceIdType.MESH)
-    pl.semaphore_wait(barrier, 2 * len(partners))
+    for partner in (core_partner, chip_partner):
+        pl.semaphore_signal(barrier, inc=1, device_id=partner, device_id_type=pl.DeviceIdType.MESH)
+    pl.semaphore_wait(barrier, 2 * len(partners) + 2)
+
+    def weight_copy(source, slot, partner):
+        copy = pltpu.make_async_remote_copy(
+            src_ref=source,
+            dst_ref=blocks_ref.at[slot],
+            send_sem=weight_send.at[slot],
+            recv_sem=weight_recv.at[slot],
+            device_id=partner,
+            device_id_type=pl.DeviceIdType.MESH,
+        )
+        copy.start()
+        return copy
+
+    weight_copies = [weight_copy(weight_ref, 0, core_partner), weight_copy(weight_ref, 1, chip_partner)]
 
     started = []
 
@@ -144,8 +178,15 @@
                 slot = len(first) + step
                 sent[step, part] = entering_ref[:, pl.ds(part * share, share)]
                 pending[part] = [send(sent.at[step, part], slot, part, later[step]) + (step + 1,)]
+        if step == len(later) - 1:
+            weight_copies[1].wait_recv()
+            weight_copies.append(weight_copy(blocks_ref.at[1], 2, core_partner))
         if step < len(later):
             conv_tiles(high_ref, low_ref, kv_ref, inner_ref, bounds[step + 1], bounds[step + 2])
+    for copy in weight_copies:
+        copy.wait_send()
+    weight_copies[0].wait_recv()
+    weight_copies[2].wait_recv()
     for copy, span in started:
 
         @pl.when(me + span < count)
@@ -153,44 +194,37 @@
             copy.wait_send()
 
 
-def scan_states(ending, decay, high, low, kv, parts=2):
+def scan_states(ending, decay, high, low, kv, weight, parts=2):
     count = lax.axis_size("ctx")
     first, later = scan_shifts(count)
     slots = len(first) + len(later)
     share = (ending.shape[0], ending.shape[1] // parts)
     vmem = pl.BlockSpec(memory_space=pltpu.VMEM)
+    anywhere = pl.BlockSpec(memory_space=pl.ANY)
     return pl.pallas_call(
         functools.partial(scan_kernel, count, parts),
         out_shape=(
             jax.ShapeDtypeStruct(ending.shape, jnp.float32),
             jax.ShapeDtypeStruct(kv.shape, jnp.float32),
+            jax.ShapeDtypeStruct((3,) + weight.shape, weight.dtype),
         ),
-        in_specs=[vmem] * 5,
-        out_specs=(vmem, vmem),
+        in_specs=[vmem] * 5 + [anywhere],
+        out_specs=(vmem, vmem, anywhere),
         scratch_shapes=[
             pltpu.VMEM((max(1, len(later)), parts) + share, jnp.float32),
             pltpu.VMEM((slots, parts) + share, jnp.float32),
             pltpu.SemaphoreType.DMA((slots, parts)),
             pltpu.SemaphoreType.DMA((slots, parts)),
+            pltpu.SemaphoreType.DMA((3,)),
+            pltpu.SemaphoreType.DMA((3,)),
         ],
         compiler_params=pltpu.CompilerParams(
             collective_id=0, has_side_effects=True, vmem_limit_bytes=48 * 1024 * 1024
         ),
-    )(ending, decay, high, low, kv)
+    )(ending, decay, high, low, kv, weight)
 
 
 def local(query_in, key_in, value_in, feature_taps, decay_rate, residues, skip_gain, out_weight):
-    pair = [(0, 1), (1, 0)]
-    chip = lax.axis_index("zlo")
-    core = lax.axis_index("core")
-    cores = lax.axis_size("core")
-    other_chip = (1 - chip) * cores
-    remote = lax.ppermute(out_weight, "zlo", pair)
-    weight_blocks = [
-        (chip * cores + core, out_weight),
-        (chip * cores + 1 - core, lax.ppermute(out_weight, "core", pair)),
-        (other_chip + core, remote),
-    ]
     query_rows = query_in[0]
     key_rows = key_in[0]
     value_rows = value_in[0]
@@ -230,9 +264,17 @@
     modes = decay_rate.shape[1]
     rate_lanes = jnp.broadcast_to(jnp.transpose(decay_rate)[:, :, None], (modes, groups, GROUP))
     decay = jnp.exp(-rate_lanes.reshape(1, modes, chans) * spans)
-    entering, inner = scan_states(ending, decay, high, low, kv_round)
-    entering, remote = lax.optimization_barrier((entering, remote))
-    weight_blocks.append((other_chip + 1 - core, lax.ppermute(remote, "core", [(0, 1), (1, 0)])))
+    entering, inner, blocks = scan_states(ending, decay, high, low, kv_round, out_weight)
+    chip = lax.axis_index("zlo")
+    core = lax.axis_index("core")
+    cores = lax.axis_size("core")
+    other_chip = (1 - chip) * cores
+    weight_blocks = [
+        (chip * cores + core, out_weight),
+        (chip * cores + 1 - core, blocks[0]),
+        (other_chip + core, blocks[1]),
+        (other_chip + 1 - core, blocks[2]),
+    ]
     entering = entering.reshape(-1, groups, GROUP)
     crossing = jnp.einsum("gni,ngc->igc", lagged, entering, precision=exact_precision)
     convolved = (inner + crossing.reshape(width, chans)).astype(jnp.bfloat16)

time: 117 us -> 144 us (1.23)
  Pallas kernels: 72 us -> 103 us
  starting transfers between devices: 15.5 us -> 3.2 us
  local copies, waits for them, and re-layouts: 10.6 us -> 19.5 us
  matrix products: 14.2 us -> 12.5 us
    pallas_call x1, Pallas kernels: 72 us -> 103 us  [scan_states(): pl.pallas_call(functools.partial(scan_kernel, count, parts), out_shape=(j...]
    ppermute x3 -> x0, starting transfers between devices: 12.3 us -> none  [the longest x1 6.34 us: local(): lax.ppermute(remote, 'core', [(0, 1), (1, 0)])]
    unnamed x12 -> x44, local copies, waits for them, and re-layouts: 0.9 us -> 6.16 us
    dot_general x4, matrix products: 7.41 us -> 4.44 us  [local(): term = jnp.dot(columns, weight, preferred_element_type=jnp.float32)]
  transfers between devices with their start and end apart: 4 -> 1, of which waited for: 0 -> 0; matrix products, arithmetic and copies ran while one was open for 20% -> 5% of each run, Pallas kernels for 62% -> 0%
where the time goes in v9:
time: 144 us
  Pallas kernels  103 us (72%)
  local copies, waits for them, and re-layouts  19.5 us (14%)
  matrix products  12.5 us (9%)
  other arithmetic  5.25 us (4%)
  starting transfers between devices  3.2 us (2%)
    pallas_call x1, Pallas kernels, scan_states(): pl.pallas_call(functools.partial(scan_kernel, count, parts), out_shape=(j...  103 us
    unnamed x44, local copies, waits for them, and re-layouts  6.16 us
    dot_general x4, matrix products, local(): term = jnp.dot(columns, weight, preferred_element_type=jnp.float32)  4.44 us
    dot_general x1, matrix products, local(): jnp.einsum('gni,ngc->igc', lagged, entering, precision=exact_precision)  3.68 us
    ppermute x1, starting transfers between devices, shifted(): return lax.ppermute(shard, axis, pairs)  3.2 us
  transfers between devices with their start and end apart: 1, of which 0 were waited for; matrix products, arithmetic and copies ran while one was open for 5% of the time, Pallas kernels for 0%

profile of v9, /device:TPU:389, one launch (start us, length us, event | category | flops | bytes accessed | tf_op | source)
XLA Modules:
  0.0 143.7 jit_solution(2313517390984339203)
XLA Ops:
  0.0 0.8 slice_bitcast_fusion.2
  0.8 0.8 slice_bitcast_fusion
  1.6 3.2 %collective-permute-start = (bf16[6,2048]{1,0:T(8,128)(2,1)S(1)}, bf16[6,2048]{1,0:T(8,128)(2,1)S(1)}, u32[]{:S(2)}, u32[]{:S(2)}) collective-permute-start(bf16[6,2048]{1,0:T(8,128)(2,1)S(1)} %pad_maximum_fusion.1), channel_id=1, source_target_pairs={{0,4},{4,8},{8,12},{12,16},{16,20},{20,24},{24,28},{28,32},{32,36}... | collective-permute-start | bytes 73736 | tf_op jit(solution)/shard_map/ppermute | solution.py:19
  4.8 1.6 %fusion.47 = (f32[1,1,2048]{2,1,0:T(1,128)S(1)}, f32[1,1,2048]{2,1,0:T(1,128)S(1)}, f32[1,1,2048]{2,1,0:T(1,128)S(1)}, f32[1,1,2048]{2,1,0:T(1,128)S(1)}, f32[1,...) fusion(f32[3,3,2048]{2,1,0:T(4,128)} %param.12), kind=kLoop, calls=%fused_computation.77 | loop fusion | bytes 147456 | tf_op jit(solution)/shard_map/slice | solution.py:25
  6.5 0.7 sqrt_multiply_fusion
  7.4 1.1 fusion.23
  9.7 0.7 subtract_reduce-precision_fusion
  11.2 0.7 copy.20
  12.9 0.7 fusion.11.kv_ref
  13.9 0.8 copy-done.7
  15.2 2.7 %convolution_add_fusion.3 = f32[128,16,16]{2,1,0:T(8,128)} fusion(f32[128,16,16]{2,1,0:T(8,128)S(1)} %fusion.28, bf16[128,128,16]{0,2,1:T(8,128)(2,1)} %bitcast.51, f32[128]{0:T(128)} %copy-done.17, f32[128,16]{1,0:T(8,128)} %copy-done.8), kind=kOutput, calls=%fused_computation.13 | convolution fusion | flops 9469952 | bytes 795136 | tf_op jit(solution)/shard_map/gnj,jgc->ngc/dot_general | solution.py:39
  17.9 2.2 %copy.25.ending_ref = f32[16,2048]{1,0:T(8,128)} copy(f32[16,2048]{0,1:T(8,128)} %bitcast.54) | data formatting | bytes 262144 | tf_op jit(solution)/shard_map/reshape | solution.py:260
  20.1 0.9 copy-done.3
  21.0 0.8 copy-done.4
  21.8 0.8 copy-done.5
  22.6 102.9 %shard_map.91 = (f32[16,2048]{1,0:T(8,128)S(1)}, f32[128,2048]{1,0:T(8,128)S(1)}, bf16[3,512,2048]{2,1,0:T(8,128)(2,1)}) custom-call(f32[16,2048]{1,0:T(8,128)S(1)} %copy-done.3, f32[7,16,2048]{2,1,0:T(8,128)S(1)} %multiply_exponential_fusion.1.decay_ref, f32[128,128]{1,0:T(8,128)S(1)} %copy-done.5, f32[128,128]{1,0:T(8,128)S(1)} %copy-done.4, ...), custom_call_target="tpu_custom_call" | custom-call | tf_op jit(solution)/shard_map/pallas_call | solution.py:204
  125.6 0.9 copy-done.1
  127.2 2.4 %copy.26 = f32[16,2048]{0,1:T(8,128)} copy(f32[16,2048]{1,0:T(8,128)} %copy-done.6) | data formatting | bytes 262144 | tf_op jit(solution)/shard_map/reshape | solution.py:278
  129.6 3.7 %fusion.19 = f32[128,16,128]{2,1,0:T(8,128)} fusion(f32[16,128,16]{0,2,1:T(8,128)} %bitcast.52, f32[128,16]{1,0:T(8,128)S(1)} %copy-done.13, f32[128]{0:T(128)S(1)} %copy-done.18, f32[128,16]{1,0:T(8,128)S(1)} %copy-done.9), kind=kOutput, calls=%fused_computation.35 | convolution fusion | flops 50855936 | bytes 1196544 | tf_op jit(solution)/shard_map/gni,ngc->igc/dot_general | solution.py:279
  133.3 2.7 %copy.22 = f32[128,2048]{1,0:T(8,128)} copy(f32[128,2048]{0,1:T(8,128)} %bitcast.53) | data formatting | bytes 2097152 | tf_op jit(solution)/shard_map/reshape | solution.py:280
  136.1 1.1 copy-done.2
  137.2 1.9 %fusion.17 = bf16[128,2048]{1,0:T(8,128)(2,1)S(1)} fusion(f32[130,2048]{1,0:T(8,128)S(1)} %maximum_convert_fusion, bf16[128,2048]{1,0:T(8,128)(2,1)S(1)} %fusion.11.kv_ref, f32[128,2048]{1,0:T(8,128)S(1)} %copy-done.2, f32[128,2048]{1,0:T(8,128)} %copy.22, f32[2048]{0:T(1024)S(1)} %copy-done.16, f32[2048]{0:T(1024)S(1)} %bitcast.62, f32[2048]{0:T(1024)S(1)} %bitcast.63, ...), kind=kLoop, calls=%fused_computation.30 | loop fusion | flops 3407872 | bytes 6324224 | tf_op jit(solution)/shard_map/convert_element_type | solution.py:284
  139.5 2.3 %convolution_add_fusion.2 = f32[128,2048]{1,0:T(8,128)S(1)} fusion(f32[128,2048]{1,0:T(8,128)S(1)} %fusion.40, bf16[3,512,2048]{2,1,0:T(8,128)(2,1)} %get-tuple-element.10, bf16[128,2048]{1,0:T(8,128)(2,1)S(1)} %fusion.17, s32[]{:T(128)S(6)} %select_n.13), kind=kOutput, calls=%fused_computation.2 | convolution fusion | flops 268697600 | bytes 4325380 | tf_op jit(solution)/shard_map/dot_general | solution.py:289
  142.4 1.3 fusion.1
  (58 shorter events, 5.6 us)
Async XLA Ops:
  1.6 10.4 %collective-permute-start = (bf16[6,2048]{1,0:T(8,128)(2,1)S(1)}, bf16[6,2048]{1,0:T(8,128)(2,1)S(1)}, u32[]{:S(2)}, u32[]{:S(2)}) collective-permute-start(bf16[6,2048]{1,0:T(8,128)(2,1)S(1)} %pad_maximum_fusion.1), channel_id=1, source_target_pairs={{0,4},{4,8},{8,12},{12,16},{16,20},{20,24},{24,28},{28,32},{32,36}... | collective-permute-start | bytes 73736 | tf_op jit(solution)/shard_map/ppermute | solution.py:19
  4.8 9.0 %copy-start.17 = (f32[128]{0:T(128)}, f32[128]{0:T(128)S(1)}, u32[]{:S(2)}) copy-start(f32[128]{0:T(128)S(1)} %iota_subtract_fusion) | copy-start | bytes 1540
  7.3 6.6 %copy-start.8 = (f32[128,16]{1,0:T(8,128)}, f32[128,16]{1,0:T(8,128)S(1)}, u32[]{:S(2)}) copy-start(f32[128,16]{1,0:T(8,128)S(1)} %copy.18) | copy-start | bytes 24580
  8.7 1.7 %copy-start.19 = (f32[7]{0:T(128)S(1)}, f32[7]{0:T(128)}, u32[]{:S(2)}) copy-start(f32[7]{0:T(128)} %constant.30) | copy-start | bytes 88
  9.1 3.5 %copy-start.10 = (bf16[1,128,2048]{2,1,0:T(8,128)(2,1)S(1)}, bf16[1,128,2048]{2,1,0:T(8,128)(2,1)}, u32[]{:S(2)}) copy-start(bf16[1,128,2048]{2,1,0:T(8,128)(2,1)} %param.10) | copy-start | bytes 1572868
  10.7 2.1 %copy-start.11 = (bf16[1,128,2048]{2,1,0:T(8,128)(2,1)S(1)}, bf16[1,128,2048]{2,1,0:T(8,128)(2,1)}, u32[]{:S(2)}) copy-start(bf16[1,128,2048]{2,1,0:T(8,128)(2,1)} %param.11) | copy-start | bytes 1572868
  13.9 0.8 copy-start.7
  15.2 4.9 %copy-start = (bf16[512,2048]{1,0:T(8,128)(2,1)S(1)}, bf16[512,2048]{1,0:T(8,128)(2,1)}, u32[]{:S(2)}) copy-start(bf16[512,2048]{1,0:T(8,128)(2,1)} %weight_ref.1) | copy-start | bytes 6291460
  20.1 0.9 copy-start.3
  21.0 0.8 copy-start.4
  21.8 0.8 copy-start.5
  125.6 1.0 copy-start.1
  126.6 0.7 copy-start.6
  127.2 2.4 %copy-start.9 = (f32[128,16]{1,0:T(8,128)S(1)}, f32[128,16]{1,0:T(8,128)}, u32[]{:S(2)}) copy-start(f32[128,16]{1,0:T(8,128)} %copy-done.8) | copy-start | bytes 24580
  127.2 2.4 %copy-start.13 = (f32[128,16]{1,0:T(8,128)S(1)}, f32[128,16]{1,0:T(8,128)}, u32[]{:S(2)}) copy-start(f32[128,16]{1,0:T(8,128)} %copy.20) | copy-start | bytes 24580
  127.2 2.4 %copy-start.18 = (f32[128]{0:T(128)S(1)}, f32[128]{0:T(128)}, u32[]{:S(2)}) copy-start(f32[128]{0:T(128)} %iota_add_fusion) | copy-start | bytes 1540
  133.3 2.7 %copy-start.12 = (bf16[1,128,2048]{2,1,0:T(8,128)(2,1)S(1)}, bf16[1,128,2048]{2,1,0:T(8,128)(2,1)}, u32[]{:S(2)}) copy-start(bf16[1,128,2048]{2,1,0:T(8,128)(2,1)} %param.9) | copy-start | bytes 1572868
  133.3 2.7 %copy-start.15 = (bf16[2,2048]{1,0:T(2,128)(2,1)S(1)}, bf16[2,2048]{1,0:T(2,128)(2,1)}, u32[]{:S(2)}) copy-start(bf16[2,2048]{1,0:T(2,128)(2,1)} %get-tuple-element.24) | copy-start | bytes 24580
  136.0 1.2 copy-start.2
  136.0 1.2 copy-start.14
  136.0 1.2 copy-start.16
  137.2 4.6 %slice-start = ((s8[6291456]{0:T(1024)(128)(4,1)}), s8[2097152]{0:T(1024)(128)(4,1)S(1)}, s32[]{:S(2)}) async-start(s8[6291456]{0:T(1024)(128)(4,1)} %bitcast.48), calls=%async_computation | async-start | bytes 4194304
  139.1 2.8 %slice-start.1 = ((s8[6291456]{0:T(1024)(128)(4,1)}), s8[4194304]{0:T(1024)(128)(4,1)S(1)}, s32[]{:S(2)}) async-start(s8[6291456]{0:T(1024)(128)(4,1)} %bitcast.48), calls=%async_computation.1 | async-start | bytes 8388608

commit v10 on v8

--- a/solution.py
+++ b/solution.py
@@ -153,7 +153,7 @@
             copy.wait_send()
 
 
-def scan_states(ending, decay, high, low, kv, parts=2):
+def scan_states(ending, decay, high, low, kv, parts=4):
     count = lax.axis_size("ctx")
     first, later = scan_shifts(count)
     slots = len(first) + len(later)

time: 117 us -> 117 us (level)
  no operation moved by 1% of the time
where the time goes in v10:
time: 117 us; the launch traced here: 116 us
  Pallas kernels  71.6 us (61%)
  starting transfers between devices  15.5 us (13%)
  matrix products  14.2 us (12%)
  local copies, waits for them, and re-layouts  10.6 us (9%)
  other arithmetic  4.06 us (3%)
    pallas_call x1, Pallas kernels, scan_states(): pl.pallas_call(functools.partial(scan_kernel, count, parts), out_shape=(j...  71.6 us
    dot_general x4, matrix products, local(): term = jnp.dot(columns, weight, preferred_element_type=jnp.float32)  7.41 us
    ppermute x1, starting transfers between devices, local(): lax.ppermute(remote, 'core', [(0, 1), (1, 0)])  6.34 us
    dot_general x1, matrix products, local(): jnp.einsum('gni,ngc->igc', lagged, entering, precision=exact_precision)  3.63 us
    ppermute x1, starting transfers between devices, shifted(): return lax.ppermute(shard, axis, pairs)  3.2 us
    ppermute x1, starting transfers between devices, local(): remote = lax.ppermute(out_weight, 'zlo', pair)  3.09 us
    ppermute x1, starting transfers between devices, local(): lax.ppermute(out_weight, 'core', pair)  2.87 us
    reshape x1, local copies, waits for them, and re-layouts, local(): convolved = (inner + crossing.reshape(width, chans)).astype(jnp.bfloat16)  2.59 us
  transfers between devices with their start and end apart: 4, of which 0 were waited for; matrix products, arithmetic and copies ran while one was open for 20% of the time, Pallas kernels for 62%

profile of v10, /device:TPU:389, one launch (start us, length us, event | category | flops | bytes accessed | tf_op | source)
XLA Modules:
  0.0 116.3 jit_solution(2577534050074810899)
XLA Ops:
  0.0 3.1 %collective-permute-start.1 = (bf16[512,2048]{1,0:T(8,128)(2,1)}, bf16[512,2048]{1,0:T(8,128)(2,1)}, u32[]{:S(2)}, u32[]{:S(2)}) collective-permute-start(bf16[512,2048]{1,0:T(8,128)(2,1)} %param.16), channel_id=1, source_target_pairs={{0,2},{2,0},{1,3},{3,1},{4,6},{6,4},{5,7},{7,5},{8,10},{10,8},{9,1... | collective-permute-start | bytes 6291464 | tf_op jit(solution)/shard_map/ppermute | solution.py:188
  3.1 2.9 %collective-permute-start.2 = (bf16[512,2048]{1,0:T(8,128)(2,1)}, bf16[512,2048]{1,0:T(8,128)(2,1)}, u32[]{:S(2)}, u32[]{:S(2)}) collective-permute-start(bf16[512,2048]{1,0:T(8,128)(2,1)} %param.16), channel_id=1, source_target_pairs={{0,1},{1,0},{2,3},{3,2},{4,5},{5,4},{6,7},{7,6},{8,9},{9,8},{10,11... | collective-permute-start | bytes 6291464 | tf_op jit(solution)/shard_map/ppermute | solution.py:191
  6.0 0.8 slice_bitcast_fusion.2
  6.8 0.8 slice_bitcast_fusion
  7.6 3.2 %collective-permute-start = (bf16[6,2048]{1,0:T(8,128)(2,1)S(1)}, bf16[6,2048]{1,0:T(8,128)(2,1)S(1)}, u32[]{:S(2)}, u32[]{:S(2)}) collective-permute-start(bf16[6,2048]{1,0:T(8,128)(2,1)S(1)} %pad_maximum_fusion.1), channel_id=1, source_target_pairs={{0,4},{4,8},{8,12},{12,16},{16,20},{20,24},{24,28},{28,32},{32,36}... | collective-permute-start | bytes 73736 | tf_op jit(solution)/shard_map/ppermute | solution.py:19
  10.8 1.0 fusion.43
  11.8 0.7 sqrt_multiply_fusion
  12.7 1.2 fusion.18
  14.4 0.6 neg.24
  15.6 0.8 copy-done.2
  16.6 0.7 fusion.6.kv_ref
  17.5 0.5 fusion.23
  18.0 1.5 %convolution_add_fusion.2 = f32[128,16,16]{2,1,0:T(8,128)} fusion(f32[128,16,16]{2,1,0:T(8,128)S(1)} %fusion.23, bf16[128,128,16]{0,2,1:T(8,128)(2,1)S(1)} %bitcast.43, f32[128]{0:T(128)S(1)} %iota_subtract_fusion, f32[128,16]{1,0:T(8,128)S(1)} %copy.18), kind=kOutput, calls=%fused_computation.7 | convolution fusion | flops 9469952 | bytes 795136 | tf_op jit(solution)/shard_map/gnj,jgc->ngc/dot_general | solution.py:39
  19.5 1.5 %copy.25.ending_ref = f32[16,2048]{1,0:T(8,128)S(1)} copy(f32[16,2048]{0,1:T(8,128)} %bitcast.46) | data formatting | bytes 262144 | tf_op jit(solution)/shard_map/reshape | solution.py:226
  21.1 71.6 %shard_map.91 = (f32[16,2048]{1,0:T(8,128)S(1)}, f32[128,2048]{1,0:T(8,128)S(1)}) custom-call(f32[16,2048]{1,0:T(8,128)S(1)} %copy.25.ending_ref, f32[7,16,2048]{2,1,0:T(8,128)S(1)} %multiply_exponential_fusion.1.decay_ref, f32[128,128]{1,0:T(8,128)S(1)} %get-tuple-element.14.high_ref, f32[128,128]{1,0:T(8,128)S(1)} %get-tuple-element.13.low_ref, ...), custom_call_target="tpu_custom_call" | custom-call | tf_op jit(solution)/shard_map/pallas_call | solution.py:162
  92.7 6.3 %collective-permute-start.3 = (bf16[512,2048]{1,0:T(8,128)(2,1)}, bf16[512,2048]{1,0:T(8,128)(2,1)}, u32[]{:S(2)}, u32[]{:S(2)}) collective-permute-start(bf16[512,2048]{1,0:T(8,128)(2,1)} %collective-permute-done.1), channel_id=1, source_target_pairs={{0,1},{1,0},{2,3},{3,2},{4,5},{5,4},{6,7},{7,6},{8,9},{9,8},{10,11... | collective-permute-start | bytes 6291464 | tf_op jit(solution)/shard_map/ppermute | solution.py:235
  99.3 1.4 %copy.26 = f32[16,2048]{0,1:T(8,128)} copy(f32[16,2048]{1,0:T(8,128)S(1)} %get-tuple-element.11) | data formatting | bytes 262144 | tf_op jit(solution)/shard_map/reshape | solution.py:236
  100.7 3.6 %fusion.14 = f32[128,16,128]{2,1,0:T(8,128)} fusion(f32[16,128,16]{0,2,1:T(8,128)} %bitcast.44, f32[128,16]{1,0:T(8,128)S(1)} %copy.20, f32[128]{0:T(128)S(1)} %iota_add_fusion, f32[128,16]{1,0:T(8,128)S(1)} %copy.18), kind=kOutput, calls=%fused_computation.29 | convolution fusion | flops 50855936 | bytes 1196544 | tf_op jit(solution)/shard_map/gni,ngc->igc/dot_general | solution.py:237
  104.3 2.6 %copy.22 = f32[128,2048]{1,0:T(8,128)} copy(f32[128,2048]{0,1:T(8,128)} %bitcast.45) | data formatting | bytes 2097152 | tf_op jit(solution)/shard_map/reshape | solution.py:238
  106.9 1.9 %fusion.12 = bf16[128,2048]{1,0:T(8,128)(2,1)S(1)} fusion(f32[130,2048]{1,0:T(8,128)S(1)} %maximum_convert_fusion, bf16[128,2048]{1,0:T(8,128)(2,1)S(1)} %fusion.6.kv_ref, f32[128,2048]{1,0:T(8,128)S(1)} %get-tuple-element.9, f32[128,2048]{1,0:T(8,128)} %copy.22, f32[2048]{0:T(1024)S(1)} %copy-done.4, f32[2048]{0:T(1024)S(1)} %bitcast.54, ...), kind=kLoop, calls=%fused_computation.24 | loop fusion | flops 3407872 | bytes 6324224 | tf_op jit(solution)/shard_map/convert_element_type | solution.py:242
  108.8 0.4 fusion.36
  109.2 2.0 %convolution_add_fusion.1 = f32[128,2048]{1,0:T(8,128)S(1)} fusion(f32[128,2048]{1,0:T(8,128)S(1)} %fusion.36, bf16[512,2048]{1,0:T(8,128)(2,1)} %collective-permute-done.2, bf16[128,2048]{1,0:T(8,128)(2,1)S(1)} %fusion.12, s32[]{:T(128)S(6)} %select_n.13), kind=kOutput, calls=%fused_computation.2 | convolution fusion | flops 268697600 | bytes 4325380 | tf_op jit(solution)/shard_map/dot_general | solution.py:247
  111.3 2.0 %fusion.32 = f32[128,2048]{1,0:T(8,128)S(1)} fusion(bf16[512,2048]{1,0:T(8,128)(2,1)} %collective-permute-done.3, bf16[128,2048]{1,0:T(8,128)(2,1)S(1)} %fusion.12, s32[]{:T(128)S(6)} %select_n.15), kind=kOutput, calls=%fused_computation.51 | convolution fusion | flops 268435456 | bytes 3276804 | tf_op jit(solution)/shard_map/dot_general | solution.py:247
  113.4 2.9 %fusion.2 = bf16[1,128,2048]{2,1,0:T(8,128)(2,1)} fusion(f32[128,2048]{1,0:T(8,128)S(1)} %fusion.32, f32[128,2048]{1,0:T(8,128)S(1)} %convolution_add_fusion.1, bf16[512,2048]{1,0:T(8,128)(2,1)} %collective-permute-done.1, bf16[128,2048]{1,0:T(8,128)(2,1)S(1)} %fusion.12, s32[]{:T(128)S(6)} %select_n.14), kind=kOutput, calls=%fused_computation.4 | convolution fusion | flops 269221888 | bytes 4849668 | tf_op jit(solution)/shard_map/dot_general | solution.py:247
  (31 shorter events, 1.9 us)
Async XLA Ops:
  0.0 92.7 %collective-permute-start.1 = (bf16[512,2048]{1,0:T(8,128)(2,1)}, bf16[512,2048]{1,0:T(8,128)(2,1)}, u32[]{:S(2)}, u32[]{:S(2)}) collective-permute-start(bf16[512,2048]{1,0:T(8,128)(2,1)} %param.16), channel_id=1, source_target_pairs={{0,2},{2,0},{1,3},{3,1},{4,6},{6,4},{5,7},{7,5},{8,10},{10,8},{9,1... | collective-permute-start | bytes 6291464 | tf_op jit(solution)/shard_map/ppermute | solution.py:188
  3.1 106.1 %collective-permute-start.2 = (bf16[512,2048]{1,0:T(8,128)(2,1)}, bf16[512,2048]{1,0:T(8,128)(2,1)}, u32[]{:S(2)}, u32[]{:S(2)}) collective-permute-start(bf16[512,2048]{1,0:T(8,128)(2,1)} %param.16), channel_id=1, source_target_pairs={{0,1},{1,0},{2,3},{3,2},{4,5},{5,4},{6,7},{7,6},{8,9},{9,8},{10,11... | collective-permute-start | bytes 6291464 | tf_op jit(solution)/shard_map/ppermute | solution.py:191
  7.6 7.8 %collective-permute-start = (bf16[6,2048]{1,0:T(8,128)(2,1)S(1)}, bf16[6,2048]{1,0:T(8,128)(2,1)S(1)}, u32[]{:S(2)}, u32[]{:S(2)}) collective-permute-start(bf16[6,2048]{1,0:T(8,128)(2,1)S(1)} %pad_maximum_fusion.1), channel_id=1, source_target_pairs={{0,4},{4,8},{8,12},{12,16},{16,20},{20,24},{24,28},{28,32},{32,36}... | collective-permute-start | bytes 73736 | tf_op jit(solution)/shard_map/ppermute | solution.py:19
  14.1 1.1 copy-start.5
  14.4 1.0 copy-start.1
  15.4 1.1 copy-start.2
  21.1 78.1 %copy-start.3 = (bf16[1,128,2048]{2,1,0:T(8,128)(2,1)S(1)}, bf16[1,128,2048]{2,1,0:T(8,128)(2,1)}, u32[]{:S(2)}) copy-start(bf16[1,128,2048]{2,1,0:T(8,128)(2,1)} %param.9) | copy-start | bytes 1572868
  92.7 18.6 %collective-permute-start.3 = (bf16[512,2048]{1,0:T(8,128)(2,1)}, bf16[512,2048]{1,0:T(8,128)(2,1)}, u32[]{:S(2)}, u32[]{:S(2)}) collective-permute-start(bf16[512,2048]{1,0:T(8,128)(2,1)} %collective-permute-done.1), channel_id=1, source_target_pairs={{0,1},{1,0},{2,3},{3,2},{4,5},{5,4},{6,7},{7,6},{8,9},{9,8},{10,11... | collective-permute-start | bytes 6291464 | tf_op jit(solution)/shard_map/ppermute | solution.py:235
  104.3 2.6 %copy-start.4 = (f32[2048]{0:T(1024)S(1)}, f32[2048]{0:T(1024)}, u32[]{:S(2)}) copy-start(f32[2048]{0:T(1024)} %param.15) | copy-start | bytes 24580
  106.9 1.9 %copy-start = (bf16[512,2048]{1,0:T(8,128)(2,1)S(1)}, bf16[512,2048]{1,0:T(8,128)(2,1)}, u32[]{:S(2)}) copy-start(bf16[512,2048]{1,0:T(8,128)(2,1)} %param.16) | copy-start | bytes 6291460

commit v11 on v10

--- a/solution.py
+++ b/solution.py
@@ -207,7 +207,7 @@
     featured_q = featurize(query_rows, tails[0:keep], feature_taps[0])
     featured_k = featurize(key_rows, tails[keep : 2 * keep], feature_taps[1])
     featured_v = featurize(value_rows, tails[2 * keep :], feature_taps[2])
-    kv_round = (featured_k * featured_v).astype(jnp.bfloat16)
+    kv_round = lax.optimization_barrier((featured_k * featured_v).astype(jnp.bfloat16))
 
     groups = chans // GROUP
     width = rows_here
@@ -218,7 +218,6 @@
     powers = jnp.exp(-decay_rate[:, :, None] * positions)
     kernel = jnp.einsum("gm,gmt->gt", scale, powers, precision=exact_precision)
     closing = jnp.exp(-decay_rate[:, :, None] * (width - 1.0 - positions))
-    lagged = jnp.exp(-decay_rate[:, :, None] * (positions + 1.0)) * scale[:, :, None]
 
     taps = jnp.roll(kernel[:, ::-1], 1, axis=1)
     high = lax.reduce_precision(taps, exponent_bits=8, mantissa_bits=7)
@@ -233,9 +232,12 @@
     entering, inner = scan_states(ending, decay, high, low, kv_round)
     entering, remote = lax.optimization_barrier((entering, remote))
     weight_blocks.append((other_chip + 1 - core, lax.ppermute(remote, "core", [(0, 1), (1, 0)])))
-    entering = entering.reshape(-1, groups, GROUP)
-    crossing = jnp.einsum("gni,ngc->igc", lagged, entering, precision=exact_precision)
-    convolved = (inner + crossing.reshape(width, chans)).astype(jnp.bfloat16)
+    scale_lanes = jnp.broadcast_to(jnp.transpose(scale)[:, :, None], (modes, groups, GROUP)).reshape(modes, 1, chans)
+    steps = (positions + 1.0)[None, :, None]
+    crossing = jnp.sum(
+        scale_lanes * jnp.exp(-rate_lanes.reshape(modes, 1, chans) * steps) * entering[:, None, :], axis=0
+    )
+    convolved = lax.optimization_barrier((inner + crossing).astype(jnp.bfloat16))
 
     gated = (
         featured_q * (convolved.astype(jnp.float32) + skip_gain * kv_round.astype(jnp.float32))

time: 117 us -> 111 us (0.949)
  matrix products: 14.2 us -> 8.95 us
  other arithmetic: 4.06 us -> 7.78 us
  Pallas kernels: 71.6 us -> 68.7 us
  local copies, waits for them, and re-layouts: 10.6 us -> 9.28 us
    reshape x2 -> x0, local copies, waits for them, and re-layouts: 3.95 us -> none  [the longest x1 2.59 us: local(): convolved = (inner + crossing.reshape(width, chans)).astype(jnp.bfloat16)]
    dot_general x1 -> x0, matrix products: 3.63 us -> none  [local(): jnp.einsum('gni,ngc->igc', lagged, entering, precision=exact_precision)]
    reduce_sum x0 -> x1, other arithmetic: none -> 3.36 us  [local(): jnp.sum(scale_lanes * jnp.exp(-rate_lanes.reshape(modes, 1, chans) * step...]
    pallas_call x1, Pallas kernels: 71.6 us -> 68.7 us  [scan_states(): pl.pallas_call(functools.partial(scan_kernel, count, parts), out_shape=(j...]
    dot_general x4, matrix products: 7.41 us -> 5.81 us  [local(): term = jnp.dot(columns, weight, preferred_element_type=jnp.float32)]
    convert_element_type x1, other arithmetic: 1.88 us -> 0.5 us  [local(): gated = (featured_q * (convolved.astype(jnp.float32) + skip_gain * kv_rou...]
  transfers between devices with their start and end apart: 4 -> 4, of which waited for: 0 -> 0; matrix products, arithmetic and copies ran while one was open for 20% -> 19% of each run, Pallas kernels for 62% -> 62%
where the time goes in v11:
time: 111 us
  Pallas kernels  68.7 us (62%)
  starting transfers between devices  15.7 us (14%)
  local copies, waits for them, and re-layouts  9.28 us (8%)
  matrix products  8.95 us (8%)
  other arithmetic  7.78 us (7%)
    pallas_call x1, Pallas kernels, scan_states(): pl.pallas_call(functools.partial(scan_kernel, count, parts), out_shape=(j...  68.7 us
    ppermute x1, starting transfers between devices, local(): lax.ppermute(remote, 'core', [(0, 1), (1, 0)])  6.52 us
    dot_general x4, matrix products, local(): term = jnp.dot(columns, weight, preferred_element_type=jnp.float32)  5.81 us
    reduce_sum x1, other arithmetic, local(): jnp.sum(scale_lanes * jnp.exp(-rate_lanes.reshape(modes, 1, chans) * step...  3.36 us
    ppermute x1, starting transfers between devices, shifted(): return lax.ppermute(shard, axis, pairs)  3.19 us
    ppermute x1, starting transfers between devices, local(): remote = lax.ppermute(out_weight, 'zlo', pair)  3.09 us
    ppermute x1, starting transfers between devices, local(): lax.ppermute(out_weight, 'core', pair)  2.87 us
  transfers between devices with their start and end apart: 4, of which 0 were waited for; matrix products, arithmetic and copies ran while one was open for 19% of the time, Pallas kernels for 62%

profile of v11, /device:TPU:389, one launch (start us, length us, event | category | flops | bytes accessed | tf_op | source)
XLA Modules:
  0.0 110.7 jit_solution(85840988207283435)
XLA Ops:
  0.0 3.1 %collective-permute-start.1 = (bf16[512,2048]{1,0:T(8,128)(2,1)}, bf16[512,2048]{1,0:T(8,128)(2,1)}, u32[]{:S(2)}, u32[]{:S(2)}) collective-permute-start(bf16[512,2048]{1,0:T(8,128)(2,1)} %param.16), channel_id=1, source_target_pairs={{0,2},{2,0},{1,3},{3,1},{4,6},{6,4},{5,7},{7,5},{8,10},{10,8},{9,1... | collective-permute-start | bytes 6291464 | tf_op jit(solution)/shard_map/ppermute | solution.py:188
  3.1 2.9 %collective-permute-start.2 = (bf16[512,2048]{1,0:T(8,128)(2,1)}, bf16[512,2048]{1,0:T(8,128)(2,1)}, u32[]{:S(2)}, u32[]{:S(2)}) collective-permute-start(bf16[512,2048]{1,0:T(8,128)(2,1)} %param.16), channel_id=1, source_target_pairs={{0,1},{1,0},{2,3},{3,2},{4,5},{5,4},{6,7},{7,6},{8,9},{9,8},{10,11... | collective-permute-start | bytes 6291464 | tf_op jit(solution)/shard_map/ppermute | solution.py:191
  6.0 0.8 slice_bitcast_fusion.2
  6.8 0.8 slice_bitcast_fusion
  7.6 0.6 pad_maximum_fusion.1
  8.2 3.2 %collective-permute-start = (bf16[6,2048]{1,0:T(8,128)(2,1)}, bf16[6,2048]{1,0:T(8,128)(2,1)}, u32[]{:S(2)}, u32[]{:S(2)}) collective-permute-start(bf16[6,2048]{1,0:T(8,128)(2,1)} %pad_maximum_fusion.1), channel_id=1, source_target_pairs={{0,4},{4,8},{8,12},{12,16},{16,20},{20,24},{24,28},{28,32},{32,36}... | collective-permute-start | bytes 73736 | tf_op jit(solution)/shard_map/ppermute | solution.py:19
  11.4 0.6 iota_subtract_fusion
  12.0 1.0 fusion.38
  13.0 0.7 fusion.32
  14.0 1.2 %fusion.14 = f32[128,1,128]{2,1,0:T(1,128)S(1)} fusion(f32[128,16,1]{1,2,0:T(1,128)S(1)} %copy.20, f32[128,16]{1,0:T(8,128)S(1)} %copy.18), kind=kOutput, calls=%fused_computation.30 | convolution fusion | flops 3407872 | bytes 81920 | tf_op jit(solution)/shard_map/gm,gmt->gt/dot_general | solution.py:219
  15.6 0.6 neg.29
  17.4 0.6 mul.244
  18.0 0.9 fusion.39
  19.3 0.7 fusion.6.kv_ref
  20.2 0.5 fusion.19
  20.8 1.5 %convolution_add_fusion.2 = f32[128,16,16]{2,1,0:T(8,128)} fusion(f32[128,16,16]{2,1,0:T(8,128)S(1)} %fusion.19, bf16[128,128,16]{0,2,1:T(8,128)(2,1)S(1)} %bitcast.41, f32[128]{0:T(128)S(1)} %copy-done.5, f32[128,16]{1,0:T(8,128)S(1)} %copy.18), kind=kOutput, calls=%fused_computation.8 | convolution fusion | flops 9469952 | bytes 795136 | tf_op jit(solution)/shard_map/gnj,jgc->ngc/dot_general | solution.py:39
  22.4 1.5 %copy.22.ending_ref = f32[16,2048]{1,0:T(8,128)S(1)} copy(f32[16,2048]{0,1:T(8,128)} %bitcast.42) | data formatting | bytes 262144 | tf_op jit(solution)/shard_map/reshape | solution.py:225
  23.9 68.7 %shard_map.91 = (f32[16,2048]{1,0:T(8,128)S(1)}, f32[128,2048]{1,0:T(8,128)S(1)}) custom-call(f32[16,2048]{1,0:T(8,128)S(1)} %copy.22.ending_ref, f32[7,16,2048]{2,1,0:T(8,128)S(1)} %multiply_exponential_fusion.1.decay_ref, f32[128,128]{1,0:T(8,128)S(1)} %get-tuple-element.14.high_ref, f32[128,128]{1,0:T(8,128)S(1)} %get-tuple-element.13.low_ref, ...), custom_call_target="tpu_custom_call" | custom-call | tf_op jit(solution)/shard_map/pallas_call | solution.py:162
  92.7 6.5 %collective-permute-start.3 = (bf16[512,2048]{1,0:T(8,128)(2,1)}, bf16[512,2048]{1,0:T(8,128)(2,1)S(1)}, u32[]{:S(2)}, u32[]{:S(2)}) collective-permute-start(bf16[512,2048]{1,0:T(8,128)(2,1)} %collective-permute-done.1), channel_id=1, source_target_pairs={{0,1},{1,0},{2,3},{3,2},{4,5},{5,4},{6,7},{7,6},{8,9},{9,8},{10,11... | collective-permute-start | bytes 6291464 | tf_op jit(solution)/shard_map/ppermute | solution.py:234
  99.2 3.4 %multiply_reduce_fusion = f32[128,2048]{1,0:T(8,128)S(1)} fusion(f32[16,2048]{1,0:T(8,128)S(1)} %get-tuple-element.11, f32[128]{0:T(128)S(1)} %copy-done.7, f32[16,2048]{1,0:T(8,128)S(1)} %neg.29, f32[16,2048]{1,0:T(8,128)S(1)} %mul.244), kind=kLoop, calls=%fused_computation | loop fusion | flops 16515072 | bytes 1442304 | tf_op jit(solution)/shard_map/reduce_sum | solution.py:237
  102.7 0.6 copy-done.4
  103.8 1.1 copy-done
  105.3 2.0 %convolution_add_fusion.1 = f32[128,2048]{1,0:T(8,128)S(1)} fusion(f32[128,2048]{1,0:T(8,128)S(1)} %fusion.29, bf16[512,2048]{1,0:T(8,128)(2,1)} %collective-permute-done.2, bf16[128,2048]{1,0:T(8,128)(2,1)S(1)} %fusion.12, s32[]{:T(128)S(6)} %select_n.13), kind=kOutput, calls=%fused_computation.3 | convolution fusion | flops 268697600 | bytes 4325380 | tf_op jit(solution)/shard_map/dot_general | solution.py:249
  107.8 2.9 %fusion.2 = bf16[1,128,2048]{2,1,0:T(8,128)(2,1)} fusion(f32[128,2048]{1,0:T(8,128)S(1)} %fusion.25, f32[128,2048]{1,0:T(8,128)S(1)} %convolution_add_fusion.1, bf16[512,2048]{1,0:T(8,128)(2,1)} %collective-permute-done.1, bf16[128,2048]{1,0:T(8,128)(2,1)S(1)} %fusion.12, s32[]{:T(128)S(6)} %select_n.14), kind=kOutput, calls=%fused_computation.5 | convolution fusion | flops 269221888 | bytes 4849668 | tf_op jit(solution)/shard_map/dot_general | solution.py:249
  (35 shorter events, 4.0 us)
Async XLA Ops:
  0.0 92.7 %collective-permute-start.1 = (bf16[512,2048]{1,0:T(8,128)(2,1)}, bf16[512,2048]{1,0:T(8,128)(2,1)}, u32[]{:S(2)}, u32[]{:S(2)}) collective-permute-start(bf16[512,2048]{1,0:T(8,128)(2,1)} %param.16), channel_id=1, source_target_pairs={{0,2},{2,0},{1,3},{3,1},{4,6},{6,4},{5,7},{7,5},{8,10},{10,8},{9,1... | collective-permute-start | bytes 6291464 | tf_op jit(solution)/shard_map/ppermute | solution.py:188
  3.1 102.2 %collective-permute-start.2 = (bf16[512,2048]{1,0:T(8,128)(2,1)}, bf16[512,2048]{1,0:T(8,128)(2,1)}, u32[]{:S(2)}, u32[]{:S(2)}) collective-permute-start(bf16[512,2048]{1,0:T(8,128)(2,1)} %param.16), channel_id=1, source_target_pairs={{0,1},{1,0},{2,3},{3,2},{4,5},{5,4},{6,7},{7,6},{8,9},{9,8},{10,11... | collective-permute-start | bytes 6291464 | tf_op jit(solution)/shard_map/ppermute | solution.py:191
  6.8 9.6 %copy-start.6 = (f32[7]{0:T(128)S(1)}, f32[7]{0:T(128)}, u32[]{:S(2)}) copy-start(f32[7]{0:T(128)} %constant.32) | copy-start | bytes 88
  8.2 9.8 %collective-permute-start = (bf16[6,2048]{1,0:T(8,128)(2,1)}, bf16[6,2048]{1,0:T(8,128)(2,1)}, u32[]{:S(2)}, u32[]{:S(2)}) collective-permute-start(bf16[6,2048]{1,0:T(8,128)(2,1)} %pad_maximum_fusion.1), channel_id=1, source_target_pairs={{0,4},{4,8},{8,12},{12,16},{16,20},{20,24},{24,28},{28,32},{32,36}... | collective-permute-start | bytes 73736 | tf_op jit(solution)/shard_map/ppermute | solution.py:19
  16.3 2.7 %copy-start.1 = (bf16[1,128,2048]{2,1,0:T(8,128)(2,1)S(1)}, bf16[1,128,2048]{2,1,0:T(8,128)(2,1)}, u32[]{:S(2)}) copy-start(bf16[1,128,2048]{2,1,0:T(8,128)(2,1)} %param.10) | copy-start | bytes 1572868
  16.6 2.5 %copy-start.2 = (bf16[1,128,2048]{2,1,0:T(8,128)(2,1)S(1)}, bf16[1,128,2048]{2,1,0:T(8,128)(2,1)}, u32[]{:S(2)}) copy-start(bf16[1,128,2048]{2,1,0:T(8,128)(2,1)} %param.11) | copy-start | bytes 1572868
  19.3 1.0 copy-start.5
  20.2 2.0 %copy-start.3 = (bf16[1,128,2048]{2,1,0:T(8,128)(2,1)S(1)}, bf16[1,128,2048]{2,1,0:T(8,128)(2,1)}, u32[]{:S(2)}) copy-start(bf16[1,128,2048]{2,1,0:T(8,128)(2,1)} %param.9) | copy-start | bytes 1572868
  22.2 77.0 %copy-start.7 = (f32[128]{0:T(128)S(1)}, f32[128]{0:T(128)}, u32[]{:S(2)}) copy-start(f32[128]{0:T(128)} %iota_add_fusion) | copy-start | bytes 1540
  92.7 14.7 %collective-permute-start.3 = (bf16[512,2048]{1,0:T(8,128)(2,1)}, bf16[512,2048]{1,0:T(8,128)(2,1)S(1)}, u32[]{:S(2)}, u32[]{:S(2)}) collective-permute-start(bf16[512,2048]{1,0:T(8,128)(2,1)} %collective-permute-done.1), channel_id=1, source_target_pairs={{0,1},{1,0},{2,3},{3,2},{4,5},{5,4},{6,7},{7,6},{8,9},{9,8},{10,11... | collective-permute-start | bytes 6291464 | tf_op jit(solution)/shard_map/ppermute | solution.py:234
  102.6 0.7 copy-start.4
  103.3 1.6 %copy-start = (bf16[512,2048]{1,0:T(8,128)(2,1)S(1)}, bf16[512,2048]{1,0:T(8,128)(2,1)}, u32[]{:S(2)}) copy-start(bf16[512,2048]{1,0:T(8,128)(2,1)} %param.16) | copy-start | bytes 6291460

commit v12 on v11

--- a/solution.py
+++ b/solution.py
@@ -57,8 +57,17 @@
         jnp.int32, (width, width), 0
     )
 
-    def toeplitz_part(ref, group):
-        row = ref[pl.ds(group, 1), :]
+    lag = lax.broadcasted_iota(jnp.int32, (1, width), 1)
+    lag = jnp.where(lag == 0, 0, width - lag).astype(jnp.float32)
+
+    def taps_row(group):
+        row = jnp.zeros((1, width), jnp.float32)
+        for mode in range(high_ref.shape[1]):
+            row = row + low_ref[group, mode] * jnp.exp(-high_ref[group, mode] * lag)
+        high = row.astype(jnp.bfloat16).astype(jnp.float32)
+        return high, (row - high).astype(jnp.bfloat16).astype(jnp.float32)
+
+    def toeplitz_part(row):
         rolled = pltpu.roll(jnp.broadcast_to(row, (width, width)), 0, 1, stride=1, stride_axis=0)
         return jnp.where(causal, rolled, 0.0).astype(jnp.bfloat16)
 
@@ -69,8 +78,8 @@
         for member in range(per_tile):
             group = tile * per_tile + member
             part = jnp.where(owner == member, block, jnp.zeros_like(block))
-            total += jnp.dot(toeplitz_part(high_ref, group), part, preferred_element_type=jnp.float32)
-            total += jnp.dot(toeplitz_part(low_ref, group), part, preferred_element_type=jnp.float32)
+            for row in taps_row(group):
+                total += jnp.dot(toeplitz_part(row), part, preferred_element_type=jnp.float32)
         inner_ref[:, pl.ds(col, 128)] = total
         return carry
 
@@ -119,7 +128,8 @@
             if factor is None:
                 entering_ref[:, columns] += landed[slot, part]
             else:
-                entering_ref[:, columns] += decay_ref[factor, :, columns] * landed[slot, part]
+                decay = jnp.exp(decay_ref[:, columns] * (-float(factor * kv_ref.shape[0])))
+                entering_ref[:, columns] += decay * landed[slot, part]
 
     tiles = kv_ref.shape[1] // 128
     rounds = 1 + len(later)
@@ -131,7 +141,7 @@
         columns = pl.ds(part * share, share)
         pending.append(
             [
-                send(ending_ref.at[:, columns], slot, part, span) + (None if slot == 0 else 0,)
+                send(ending_ref.at[:, columns], slot, part, span) + (None if slot == 0 else 1,)
                 for slot, span in enumerate(first)
             ]
         )
@@ -143,7 +153,7 @@
             if step < len(later):
                 slot = len(first) + step
                 sent[step, part] = entering_ref[:, pl.ds(part * share, share)]
-                pending[part] = [send(sent.at[step, part], slot, part, later[step]) + (step + 1,)]
+                pending[part] = [send(sent.at[step, part], slot, part, later[step]) + (later[step],)]
         if step < len(later):
             conv_tiles(high_ref, low_ref, kv_ref, inner_ref, bounds[step + 1], bounds[step + 2])
     for copy, span in started:
@@ -159,13 +169,14 @@
     slots = len(first) + len(later)
     share = (ending.shape[0], ending.shape[1] // parts)
     vmem = pl.BlockSpec(memory_space=pltpu.VMEM)
+    smem = pl.BlockSpec(memory_space=pltpu.SMEM)
     return pl.pallas_call(
         functools.partial(scan_kernel, count, parts),
         out_shape=(
             jax.ShapeDtypeStruct(ending.shape, jnp.float32),
             jax.ShapeDtypeStruct(kv.shape, jnp.float32),
         ),
-        in_specs=[vmem] * 5,
+        in_specs=[vmem, vmem, smem, smem, vmem],
         out_specs=(vmem, vmem),
         scratch_shapes=[
             pltpu.VMEM((max(1, len(later)), parts) + share, jnp.float32),
@@ -215,21 +226,13 @@
 
     positions = jnp.arange(width, dtype=jnp.float32)
     scale = residues * jnp.sqrt(-jnp.expm1(-2.0 * decay_rate))
-    powers = jnp.exp(-decay_rate[:, :, None] * positions)
-    kernel = jnp.einsum("gm,gmt->gt", scale, powers, precision=exact_precision)
     closing = jnp.exp(-decay_rate[:, :, None] * (width - 1.0 - positions))
 
-    taps = jnp.roll(kernel[:, ::-1], 1, axis=1)
-    high = lax.reduce_precision(taps, exponent_bits=8, mantissa_bits=7)
-    low = lax.reduce_precision(taps - high, exponent_bits=8, mantissa_bits=7)
     ending = two_pass("gnj,jgc->ngc", closing, kv_grouped).reshape(-1, chans)
 
-    first, later = scan_shifts(lax.axis_size("ctx"))
-    spans = jnp.asarray([1] * (len(first) - 1) + later, jnp.float32)[:, None, None] * float(width)
     modes = decay_rate.shape[1]
     rate_lanes = jnp.broadcast_to(jnp.transpose(decay_rate)[:, :, None], (modes, groups, GROUP))
-    decay = jnp.exp(-rate_lanes.reshape(1, modes, chans) * spans)
-    entering, inner = scan_states(ending, decay, high, low, kv_round)
+    entering, inner = scan_states(ending, rate_lanes.reshape(modes, chans), decay_rate, scale, kv_round)
     entering, remote = lax.optimization_barrier((entering, remote))
     weight_blocks.append((other_chip + 1 - core, lax.ppermute(remote, "core", [(0, 1), (1, 0)])))
     scale_lanes = jnp.broadcast_to(jnp.transpose(scale)[:, :, None], (modes, groups, GROUP)).reshape(modes, 1, chans)

time: 111 us -> 112 us (level)
  Pallas kernels: 68.7 us -> 73 us
  matrix products: 8.95 us -> 6.82 us
  other arithmetic: 7.78 us -> 5.88 us
    pallas_call x1, Pallas kernels: 68.7 us -> 73 us  [scan_states(): pl.pallas_call(functools.partial(scan_kernel, count, parts), out_shape=(j...]
    unnamed x16 -> x12, local copies, waits for them, and re-layouts: 1.7 us -> 3.28 us
    reshape x1, local copies, waits for them, and re-layouts: 1.52 us -> 0.3 us  [local(): ending = two_pass('gnj,jgc->ngc', closing, kv_grouped).reshape(-1, chans)]
    dot_general x1 -> x0, matrix products: 1.15 us -> none  [local(): kernel = jnp.einsum('gm,gmt->gt', scale, powers, precision=exact_precision)]
  transfers between devices with their start and end apart: 4 -> 4, of which waited for: 0 -> 0; matrix products, arithmetic and copies ran while one was open for 19% -> 15% of each run, Pallas kernels for 62% -> 66%
where the time goes in v12:
time: 112 us; the launch traced here: 111 us
  Pallas kernels  73 us (65%)
  starting transfers between devices  15.7 us (14%)
  local copies, waits for them, and re-layouts  9.37 us (8%)
  matrix products  6.82 us (6%)
  other arithmetic  5.88 us (5%)
    pallas_call x1, Pallas kernels, scan_states(): pl.pallas_call(functools.partial(scan_kernel, count, parts), out_shape=(j...  73 us
    ppermute x1, starting transfers between devices, local(): lax.ppermute(remote, 'core', [(0, 1), (1, 0)])  6.52 us
    dot_general x4, matrix products, local(): term = jnp.dot(columns, weight, preferred_element_type=jnp.float32)  5.81 us
    reduce_sum x1, other arithmetic, local(): jnp.sum(scale_lanes * jnp.exp(-rate_lanes.reshape(modes, 1, chans) * step...  3.36 us
    unnamed x12, local copies, waits for them, and re-layouts  3.28 us
    ppermute x1, starting transfers between devices, shifted(): return lax.ppermute(shard, axis, pairs)  3.2 us
    ppermute x1, starting transfers between devices, local(): remote = lax.ppermute(out_weight, 'zlo', pair)  3.09 us
    ppermute x1, starting transfers between devices, local(): lax.ppermute(out_weight, 'core', pair)  2.87 us
  transfers between devices with their start and end apart: 4, of which 0 were waited for; matrix products, arithmetic and copies ran while one was open for 15% of the time, Pallas kernels for 66%

profile of v12, /device:TPU:389, one launch (start us, length us, event | category | flops | bytes accessed | tf_op | source)
XLA Modules:
  0.0 111.0 jit_solution(17584596342825247015)
XLA Ops:
  0.0 3.1 %collective-permute-start.1 = (bf16[512,2048]{1,0:T(8,128)(2,1)}, bf16[512,2048]{1,0:T(8,128)(2,1)}, u32[]{:S(2)}, u32[]{:S(2)}) collective-permute-start(bf16[512,2048]{1,0:T(8,128)(2,1)} %param.15), channel_id=1, source_target_pairs={{0,2},{2,0},{1,3},{3,1},{4,6},{6,4},{5,7},{7,5},{8,10},{10,8},{9,1... | collective-permute-start | bytes 6291464 | tf_op jit(solution)/shard_map/ppermute | solution.py:199
  3.1 2.9 %collective-permute-start.2 = (bf16[512,2048]{1,0:T(8,128)(2,1)}, bf16[512,2048]{1,0:T(8,128)(2,1)}, u32[]{:S(2)}, u32[]{:S(2)}) collective-permute-start(bf16[512,2048]{1,0:T(8,128)(2,1)} %param.15), channel_id=1, source_target_pairs={{0,1},{1,0},{2,3},{3,2},{4,5},{5,4},{6,7},{7,6},{8,9},{9,8},{10,11... | collective-permute-start | bytes 6291464 | tf_op jit(solution)/shard_map/ppermute | solution.py:202
  6.0 0.8 slice_bitcast_fusion.2
  6.8 0.8 slice_bitcast_fusion
  7.6 3.2 %collective-permute-start = (bf16[6,2048]{1,0:T(8,128)(2,1)S(1)}, bf16[6,2048]{1,0:T(8,128)(2,1)S(1)}, u32[]{:S(2)}, u32[]{:S(2)}) collective-permute-start(bf16[6,2048]{1,0:T(8,128)(2,1)S(1)} %pad_maximum_fusion), channel_id=1, source_target_pairs={{0,4},{4,8},{8,12},{12,16},{16,20},{20,24},{24,28},{28,32},{32,36}... | collective-permute-start | bytes 73736 | tf_op jit(solution)/shard_map/ppermute | solution.py:19
  10.8 1.0 fusion.30
  11.9 0.7 multiply_exponential-minus-one_fusion
  12.7 0.8 copy.38
  13.5 0.8 copy.39.high_ref
  14.4 1.0 broadcast_in_dim.6
  15.5 0.6 reshape.56.decay_ref
  16.5 0.6 mul.210
  17.5 0.7 fusion.6.kv_ref
  18.5 0.5 fusion.15
  19.0 0.5 convolution_add_fusion.2
  20.0 73.0 %shard_map.82 = (f32[16,2048]{1,0:T(8,128)S(1)}, f32[128,2048]{1,0:T(8,128)S(1)}) custom-call(f32[16,2048]{1,0:T(8,128)S(1)} %copy.41.ending_ref, f32[16,2048]{1,0:T(8,128)S(1)} %reshape.56.decay_ref, f32[128,16]{1,0:T(8,128)S(1)} %copy.39.high_ref, f32[128,16]{1,0:T(8,128)S(1)} %sqrt_multiply_fusion.low_ref, bf16[128,2048]{1,0:T(8,128)(2,1)S(1)} %fusion.6.kv_ref), custom_call_target="tpu_custom_call" | custom-call | tf_op jit(solution)/shard_map/pallas_call | solution.py:173
  93.0 6.5 %collective-permute-start.3 = (bf16[512,2048]{1,0:T(8,128)(2,1)}, bf16[512,2048]{1,0:T(8,128)(2,1)S(1)}, u32[]{:S(2)}, u32[]{:S(2)}) collective-permute-start(bf16[512,2048]{1,0:T(8,128)(2,1)} %collective-permute-done.1), channel_id=1, source_target_pairs={{0,1},{1,0},{2,3},{3,2},{4,5},{5,4},{6,7},{7,6},{8,9},{9,8},{10,11... | collective-permute-start | bytes 6291464 | tf_op jit(solution)/shard_map/ppermute | solution.py:237
  99.5 3.4 %multiply_reduce_fusion = f32[128,2048]{1,0:T(8,128)S(1)} fusion(f32[16,2048]{1,0:T(8,128)S(1)} %get-tuple-element.11, f32[128]{0:T(128)S(1)} %iota_add_fusion, f32[16,2048]{1,0:T(8,128)S(1)} %neg.17, f32[16,2048]{1,0:T(8,128)S(1)} %mul.210), kind=kLoop, calls=%fused_computation | loop fusion | flops 16515072 | bytes 1442304 | tf_op jit(solution)/shard_map/reduce_sum | solution.py:240
  103.0 0.6 copy-done.4
  103.6 0.5 fusion.12
  104.1 1.1 copy-done
  105.6 2.0 %convolution_add_fusion.1 = f32[128,2048]{1,0:T(8,128)S(1)} fusion(f32[128,2048]{1,0:T(8,128)S(1)} %fusion.24, bf16[512,2048]{1,0:T(8,128)(2,1)} %collective-permute-done.2, bf16[128,2048]{1,0:T(8,128)(2,1)S(1)} %fusion.12, s32[]{:T(128)S(6)} %select_n.13), kind=kOutput, calls=%fused_computation.3 | convolution fusion | flops 268697600 | bytes 4325380 | tf_op jit(solution)/shard_map/dot_general | solution.py:252
  107.7 0.4 fusion.20
  108.2 2.9 %fusion.2 = bf16[1,128,2048]{2,1,0:T(8,128)(2,1)} fusion(f32[128,2048]{1,0:T(8,128)S(1)} %fusion.20, f32[128,2048]{1,0:T(8,128)S(1)} %convolution_add_fusion.1, bf16[512,2048]{1,0:T(8,128)(2,1)} %collective-permute-done.1, bf16[128,2048]{1,0:T(8,128)(2,1)S(1)} %fusion.12, s32[]{:T(128)S(6)} %select_n.14), kind=kOutput, calls=%fused_computation.5 | convolution fusion | flops 269221888 | bytes 4849668 | tf_op jit(solution)/shard_map/dot_general | solution.py:252
  (29 shorter events, 2.3 us)
Async XLA Ops:
  0.0 93.0 %collective-permute-start.1 = (bf16[512,2048]{1,0:T(8,128)(2,1)}, bf16[512,2048]{1,0:T(8,128)(2,1)}, u32[]{:S(2)}, u32[]{:S(2)}) collective-permute-start(bf16[512,2048]{1,0:T(8,128)(2,1)} %param.15), channel_id=1, source_target_pairs={{0,2},{2,0},{1,3},{3,1},{4,6},{6,4},{5,7},{7,5},{8,10},{10,8},{9,1... | collective-permute-start | bytes 6291464 | tf_op jit(solution)/shard_map/ppermute | solution.py:199
  3.1 102.5 %collective-permute-start.2 = (bf16[512,2048]{1,0:T(8,128)(2,1)}, bf16[512,2048]{1,0:T(8,128)(2,1)}, u32[]{:S(2)}, u32[]{:S(2)}) collective-permute-start(bf16[512,2048]{1,0:T(8,128)(2,1)} %param.15), channel_id=1, source_target_pairs={{0,1},{1,0},{2,3},{3,2},{4,5},{5,4},{6,7},{7,6},{8,9},{9,8},{10,11... | collective-permute-start | bytes 6291464 | tf_op jit(solution)/shard_map/ppermute | solution.py:202
  7.6 9.6 %collective-permute-start = (bf16[6,2048]{1,0:T(8,128)(2,1)S(1)}, bf16[6,2048]{1,0:T(8,128)(2,1)S(1)}, u32[]{:S(2)}, u32[]{:S(2)}) collective-permute-start(bf16[6,2048]{1,0:T(8,128)(2,1)S(1)} %pad_maximum_fusion), channel_id=1, source_target_pairs={{0,4},{4,8},{8,12},{12,16},{16,20},{20,24},{24,28},{28,32},{32,36}... | collective-permute-start | bytes 73736 | tf_op jit(solution)/shard_map/ppermute | solution.py:19
  15.5 1.7 %copy-start.1 = (bf16[1,128,2048]{2,1,0:T(8,128)(2,1)S(1)}, bf16[1,128,2048]{2,1,0:T(8,128)(2,1)}, u32[]{:S(2)}) copy-start(bf16[1,128,2048]{2,1,0:T(8,128)(2,1)} %param.9) | copy-start | bytes 1572868
  16.1 1.2 %copy-start.2 = (bf16[1,128,2048]{2,1,0:T(8,128)(2,1)S(1)}, bf16[1,128,2048]{2,1,0:T(8,128)(2,1)}, u32[]{:S(2)}) copy-start(bf16[1,128,2048]{2,1,0:T(8,128)(2,1)} %param.10) | copy-start | bytes 1572868
  18.5 1.0 copy-start.3
  93.0 14.7 %collective-permute-start.3 = (bf16[512,2048]{1,0:T(8,128)(2,1)}, bf16[512,2048]{1,0:T(8,128)(2,1)S(1)}, u32[]{:S(2)}, u32[]{:S(2)}) collective-permute-start(bf16[512,2048]{1,0:T(8,128)(2,1)} %collective-permute-done.1), channel_id=1, source_target_pairs={{0,1},{1,0},{2,3},{3,2},{4,5},{5,4},{6,7},{7,6},{8,9},{9,8},{10,11... | collective-permute-start | bytes 6291464 | tf_op jit(solution)/shard_map/ppermute | solution.py:237
  102.9 0.7 copy-start.4
  103.6 1.6 %copy-start = (bf16[512,2048]{1,0:T(8,128)(2,1)S(1)}, bf16[512,2048]{1,0:T(8,128)(2,1)}, u32[]{:S(2)}) copy-start(bf16[512,2048]{1,0:T(8,128)(2,1)} %param.15) | copy-start | bytes 6291460

commit v13 on v11

--- a/solution.py
+++ b/solution.py
@@ -233,10 +233,12 @@
     entering, remote = lax.optimization_barrier((entering, remote))
     weight_blocks.append((other_chip + 1 - core, lax.ppermute(remote, "core", [(0, 1), (1, 0)])))
     scale_lanes = jnp.broadcast_to(jnp.transpose(scale)[:, :, None], (modes, groups, GROUP)).reshape(modes, 1, chans)
-    steps = (positions + 1.0)[None, :, None]
-    crossing = jnp.sum(
-        scale_lanes * jnp.exp(-rate_lanes.reshape(modes, 1, chans) * steps) * entering[:, None, :], axis=0
-    )
+    fine_len = 8
+    rate_rows = rate_lanes.reshape(modes, 1, 1, chans)
+    coarse = jnp.exp(-rate_rows * (fine_len * jnp.arange(width // fine_len, dtype=jnp.float32))[None, :, None, None])
+    fine = jnp.exp(-rate_rows * (jnp.arange(fine_len, dtype=jnp.float32) + 1.0)[None, None, :, None])
+    weighted = (scale_lanes.reshape(modes, chans) * entering)[:, None, None, :]
+    crossing = jnp.sum(weighted * coarse * fine, axis=0).reshape(width, chans)
     convolved = lax.optimization_barrier((inner + crossing).astype(jnp.bfloat16))
 
     gated = (

time: 111 us -> 111 us (level)
    reduce_sum x1, other arithmetic: 3.36 us -> 1.36 us  [local(): crossing = jnp.sum(weighted * coarse * fine, axis=0).reshape(width, chans)]
    reshape x1, local copies, waits for them, and re-layouts: 1.52 us -> 0.3 us  [local(): ending = two_pass('gnj,jgc->ngc', closing, kv_grouped).reshape(-1, chans)]
    exp x0 -> x1, other arithmetic: none -> 1.2 us  [local(): jnp.exp(-rate_rows * (jnp.arange(fine_len, dtype=jnp.float32) + 1.0)[None...]
  transfers between devices with their start and end apart: 4 -> 4, of which waited for: 0 -> 0; matrix products, arithmetic and copies ran while one was open for 19% -> 18% of each run, Pallas kernels for 62% -> 62%
where the time goes in v13:
time: 111 us; the launch traced here: 110 us
  Pallas kernels  68.6 us (62%)
  starting transfers between devices  15.8 us (14%)
  local copies, waits for them, and re-layouts  9.27 us (8%)
  other arithmetic  8.18 us (7%)
  matrix products  7.97 us (7%)
    pallas_call x1, Pallas kernels, scan_states(): pl.pallas_call(functools.partial(scan_kernel, count, parts), out_shape=(j...  68.6 us
    ppermute x1, starting transfers between devices, local(): lax.ppermute(remote, 'core', [(0, 1), (1, 0)])  6.52 us
    dot_general x4, matrix products, local(): term = jnp.dot(columns, weight, preferred_element_type=jnp.float32)  5.81 us
    ppermute x1, starting transfers between devices, local(): remote = lax.ppermute(out_weight, 'zlo', pair)  3.22 us
    ppermute x1, starting transfers between devices, shifted(): return lax.ppermute(shard, axis, pairs)  3.19 us
    ppermute x1, starting transfers between devices, local(): lax.ppermute(out_weight, 'core', pair)  2.87 us
  transfers between devices with their start and end apart: 4, of which 0 were waited for; matrix products, arithmetic and copies ran while one was open for 18% of the time, Pallas kernels for 62%

profile of v13, /device:TPU:389, one launch (start us, length us, event | category | flops | bytes accessed | tf_op | source)
XLA Modules:
  0.0 110.2 jit_solution(13796654331940638695)
XLA Ops:
  0.0 3.2 %collective-permute-start.1 = (bf16[512,2048]{1,0:T(8,128)(2,1)}, bf16[512,2048]{1,0:T(8,128)(2,1)}, u32[]{:S(2)}, u32[]{:S(2)}) collective-permute-start(bf16[512,2048]{1,0:T(8,128)(2,1)} %param.16), channel_id=1, source_target_pairs={{0,2},{2,0},{1,3},{3,1},{4,6},{6,4},{5,7},{7,5},{8,10},{10,8},{9,1... | collective-permute-start | bytes 6291464 | tf_op jit(solution)/shard_map/ppermute | solution.py:188
  3.2 2.9 %collective-permute-start.2 = (bf16[512,2048]{1,0:T(8,128)(2,1)}, bf16[512,2048]{1,0:T(8,128)(2,1)}, u32[]{:S(2)}, u32[]{:S(2)}) collective-permute-start(bf16[512,2048]{1,0:T(8,128)(2,1)} %param.16), channel_id=1, source_target_pairs={{0,1},{1,0},{2,3},{3,2},{4,5},{5,4},{6,7},{7,6},{8,9},{9,8},{10,11... | collective-permute-start | bytes 6291464 | tf_op jit(solution)/shard_map/ppermute | solution.py:191
  6.1 0.8 slice_bitcast_fusion.2
  6.9 0.8 slice_bitcast_fusion
  7.7 0.6 pad_maximum_fusion.1
  8.3 3.2 %collective-permute-start = (bf16[6,2048]{1,0:T(8,128)(2,1)}, bf16[6,2048]{1,0:T(8,128)(2,1)}, u32[]{:S(2)}, u32[]{:S(2)}) collective-permute-start(bf16[6,2048]{1,0:T(8,128)(2,1)} %pad_maximum_fusion.1), channel_id=1, source_target_pairs={{0,4},{4,8},{8,12},{12,16},{16,20},{20,24},{24,28},{28,32},{32,36}... | collective-permute-start | bytes 73736 | tf_op jit(solution)/shard_map/ppermute | solution.py:19
  11.5 0.5 iota_subtract_fusion
  12.1 1.6 %fusion.39 = (f32[1,1,2048]{2,1,0:T(1,128)S(1)}, f32[1,1,2048]{2,1,0:T(1,128)}, f32[1,1,2048]{2,1,0:T(1,128)}, f32[1,1,2048]{2,1,0:T(1,128)}, f32[1,1,2048]{2,1,...) fusion(f32[3,3,2048]{2,1,0:T(4,128)} %param.12), kind=kLoop, calls=%fused_computation.72 | loop fusion | bytes 147456 | tf_op jit(solution)/shard_map/slice | solution.py:25
  13.7 0.7 fusion.33
  14.6 1.2 %fusion.15 = f32[128,1,128]{2,1,0:T(1,128)S(1)} fusion(f32[128,16,1]{1,2,0:T(1,128)S(1)} %copy.20, f32[128,16]{1,0:T(8,128)S(1)} %copy.18), kind=kOutput, calls=%fused_computation.33 | convolution fusion | flops 3407872 | bytes 81920 | tf_op jit(solution)/shard_map/gm,gmt->gt/dot_general | solution.py:219
  16.3 0.6 neg.30
  17.2 1.2 %multiply_exponential_fusion = f32[16,8,2048]{2,1,0:T(8,128)} fusion(f32[8]{0:T(128)S(1)} %iota_add_fusion, f32[16,2048]{1,0:T(8,128)S(1)} %neg.30), kind=kLoop, calls=%fused_computation.32 | loop fusion | flops 262144 | bytes 1179680 | tf_op jit(solution)/shard_map/exp | solution.py:239
  18.5 0.6 iota_multiply_fusion
  19.4 0.6 reshape_reshape.3
  20.0 1.5 %fusion.40 = (bf16[2,2048]{1,0:T(2,128)(2,1)}, bf16[2,2048]{1,0:T(2,128)(2,1)S(1)}, bf16[2,2048]{1,0:T(2,128)(2,1)S(1)}) fusion(bf16[6,2048]{1,0:T(8,128)(2,1)} %collective-permute-done), kind=kLoop, calls=%fused_computation.73 | loop fusion | bytes 49152 | tf_op jit(solution)/shard_map/slice | solution.py:207
  21.9 0.7 fusion.6.kv_ref
  24.2 68.6 %shard_map.91 = (f32[16,2048]{1,0:T(8,128)S(1)}, f32[128,2048]{1,0:T(8,128)S(1)}) custom-call(f32[16,2048]{1,0:T(8,128)S(1)} %copy.22.ending_ref, f32[7,16,2048]{2,1,0:T(8,128)S(1)} %multiply_exponential_fusion.2.decay_ref, f32[128,128]{1,0:T(8,128)S(1)} %get-tuple-element.14.high_ref, f32[128,128]{1,0:T(8,128)S(1)} %get-tuple-element.13.low_ref, ...), custom_call_target="tpu_custom_call" | custom-call | tf_op jit(solution)/shard_map/pallas_call | solution.py:162
  92.8 0.9 maximum_convert_fusion
  93.8 6.5 %collective-permute-start.3 = (bf16[512,2048]{1,0:T(8,128)(2,1)}, bf16[512,2048]{1,0:T(8,128)(2,1)S(1)}, u32[]{:S(2)}, u32[]{:S(2)}) collective-permute-start(bf16[512,2048]{1,0:T(8,128)(2,1)} %collective-permute-done.1), channel_id=1, source_target_pairs={{0,1},{1,0},{2,3},{3,2},{4,5},{5,4},{6,7},{7,6},{8,9},{9,8},{10,11... | collective-permute-start | bytes 6291464 | tf_op jit(solution)/shard_map/ppermute | solution.py:234
  100.7 1.4 %multiply_reduce_fusion = f32[16,8,2048]{2,1,0:T(8,128)S(1)} fusion(f32[16,8,2048]{2,1,0:T(8,128)S(1)} %copy-done, f32[16,16,2048]{2,1,0:T(8,128)S(1)} %exponential_multiply_fusion), kind=kLoop, calls=%fused_computation | loop fusion | flops 8126464 | bytes 4194304 | tf_op jit(solution)/shard_map/reduce_sum | solution.py:241
  102.2 0.6 copy-done.5
  103.3 1.1 copy-done.1
  104.8 2.0 %convolution_add_fusion.1 = f32[128,2048]{1,0:T(8,128)S(1)} fusion(f32[128,2048]{1,0:T(8,128)S(1)} %fusion.30, bf16[512,2048]{1,0:T(8,128)(2,1)} %collective-permute-done.2, bf16[128,2048]{1,0:T(8,128)(2,1)S(1)} %fusion.12, s32[]{:T(128)S(6)} %select_n.13), kind=kOutput, calls=%fused_computation.3 | convolution fusion | flops 268697600 | bytes 4325380 | tf_op jit(solution)/shard_map/dot_general | solution.py:251
  107.3 2.9 %fusion.2 = bf16[1,128,2048]{2,1,0:T(8,128)(2,1)} fusion(f32[128,2048]{1,0:T(8,128)S(1)} %fusion.26, f32[128,2048]{1,0:T(8,128)S(1)} %convolution_add_fusion.1, bf16[512,2048]{1,0:T(8,128)(2,1)} %collective-permute-done.1, bf16[128,2048]{1,0:T(8,128)(2,1)S(1)} %fusion.12, s32[]{:T(128)S(6)} %select_n.14), kind=kOutput, calls=%fused_computation.5 | convolution fusion | flops 269221888 | bytes 4849668 | tf_op jit(solution)/shard_map/dot_general | solution.py:251
  (55 shorter events, 5.1 us)
Async XLA Ops:
  0.0 16.9 %copy-start.15 = (f32[7]{0:T(128)S(1)}, f32[7]{0:T(128)}, u32[]{:S(2)}) copy-start(f32[7]{0:T(128)} %constant.34) | copy-start | bytes 88
  0.0 93.7 %collective-permute-start.1 = (bf16[512,2048]{1,0:T(8,128)(2,1)}, bf16[512,2048]{1,0:T(8,128)(2,1)}, u32[]{:S(2)}, u32[]{:S(2)}) collective-permute-start(bf16[512,2048]{1,0:T(8,128)(2,1)} %param.16), channel_id=1, source_target_pairs={{0,2},{2,0},{1,3},{3,1},{4,6},{6,4},{5,7},{7,5},{8,10},{10,8},{9,1... | collective-permute-start | bytes 6291464 | tf_op jit(solution)/shard_map/ppermute | solution.py:188
  3.2 101.6 %collective-permute-start.2 = (bf16[512,2048]{1,0:T(8,128)(2,1)}, bf16[512,2048]{1,0:T(8,128)(2,1)}, u32[]{:S(2)}, u32[]{:S(2)}) collective-permute-start(bf16[512,2048]{1,0:T(8,128)(2,1)} %param.16), channel_id=1, source_target_pairs={{0,1},{1,0},{2,3},{3,2},{4,5},{5,4},{6,7},{7,6},{8,9},{9,8},{10,11... | collective-permute-start | bytes 6291464 | tf_op jit(solution)/shard_map/ppermute | solution.py:191
  8.3 11.7 %collective-permute-start = (bf16[6,2048]{1,0:T(8,128)(2,1)}, bf16[6,2048]{1,0:T(8,128)(2,1)}, u32[]{:S(2)}, u32[]{:S(2)}) collective-permute-start(bf16[6,2048]{1,0:T(8,128)(2,1)} %pad_maximum_fusion.1), channel_id=1, source_target_pairs={{0,4},{4,8},{8,12},{12,16},{16,20},{20,24},{24,28},{28,32},{32,36}... | collective-permute-start | bytes 73736 | tf_op jit(solution)/shard_map/ppermute | solution.py:19
  17.1 4.4 %copy-start.2 = (bf16[1,128,2048]{2,1,0:T(8,128)(2,1)S(1)}, bf16[1,128,2048]{2,1,0:T(8,128)(2,1)}, u32[]{:S(2)}) copy-start(bf16[1,128,2048]{2,1,0:T(8,128)(2,1)} %param.10) | copy-start | bytes 1572868
  18.4 3.3 %copy-start.3 = (bf16[1,128,2048]{2,1,0:T(8,128)(2,1)S(1)}, bf16[1,128,2048]{2,1,0:T(8,128)(2,1)}, u32[]{:S(2)}) copy-start(bf16[1,128,2048]{2,1,0:T(8,128)(2,1)} %param.11) | copy-start | bytes 1572868
  19.4 2.5 %copy-start.6 = (f32[1,1,2048]{2,1,0:T(1,128)S(1)}, f32[1,1,2048]{2,1,0:T(1,128)}, u32[]{:S(2)}) copy-start(f32[1,1,2048]{2,1,0:T(1,128)} %get-tuple-element.16) | copy-start | bytes 24580
  19.4 2.5 %copy-start.7 = (f32[1,1,2048]{2,1,0:T(1,128)S(1)}, f32[1,1,2048]{2,1,0:T(1,128)}, u32[]{:S(2)}) copy-start(f32[1,1,2048]{2,1,0:T(1,128)} %get-tuple-element.17) | copy-start | bytes 24580
  19.4 2.5 %copy-start.8 = (f32[1,1,2048]{2,1,0:T(1,128)S(1)}, f32[1,1,2048]{2,1,0:T(1,128)}, u32[]{:S(2)}) copy-start(f32[1,1,2048]{2,1,0:T(1,128)} %get-tuple-element.18) | copy-start | bytes 24580
  19.4 2.5 %copy-start.9 = (f32[1,1,2048]{2,1,0:T(1,128)S(1)}, f32[1,1,2048]{2,1,0:T(1,128)}, u32[]{:S(2)}) copy-start(f32[1,1,2048]{2,1,0:T(1,128)} %get-tuple-element.19) | copy-start | bytes 24580
  19.4 2.5 %copy-start.10 = (f32[1,1,2048]{2,1,0:T(1,128)S(1)}, f32[1,1,2048]{2,1,0:T(1,128)}, u32[]{:S(2)}) copy-start(f32[1,1,2048]{2,1,0:T(1,128)} %get-tuple-element.22) | copy-start | bytes 24580
  19.4 2.5 %copy-start.11 = (f32[1,1,2048]{2,1,0:T(1,128)S(1)}, f32[1,1,2048]{2,1,0:T(1,128)}, u32[]{:S(2)}) copy-start(f32[1,1,2048]{2,1,0:T(1,128)} %get-tuple-element.23) | copy-start | bytes 24580
  21.9 1.0 copy-start.13
  23.9 68.9 %copy-start.4 = (bf16[1,128,2048]{2,1,0:T(8,128)(2,1)S(1)}, bf16[1,128,2048]{2,1,0:T(8,128)(2,1)}, u32[]{:S(2)}) copy-start(bf16[1,128,2048]{2,1,0:T(8,128)(2,1)} %param.9) | copy-start | bytes 1572868
  24.2 76.1 %copy-start.14 = (f32[16]{0:T(128)S(1)}, f32[16]{0:T(128)}, u32[]{:S(2)}) copy-start(f32[16]{0:T(128)} %iota_multiply_fusion) | copy-start | bytes 196
  92.8 7.9 %copy-start = (f32[16,8,2048]{2,1,0:T(8,128)S(1)}, f32[16,8,2048]{2,1,0:T(8,128)}, u32[]{:S(2)}) copy-start(f32[16,8,2048]{2,1,0:T(8,128)} %multiply_exponential_fusion) | copy-start | bytes 3145732
  93.8 13.1 %collective-permute-start.3 = (bf16[512,2048]{1,0:T(8,128)(2,1)}, bf16[512,2048]{1,0:T(8,128)(2,1)S(1)}, u32[]{:S(2)}, u32[]{:S(2)}) collective-permute-start(bf16[512,2048]{1,0:T(8,128)(2,1)} %collective-permute-done.1), channel_id=1, source_target_pairs={{0,1},{1,0},{2,3},{3,2},{4,5},{5,4},{6,7},{7,6},{8,9},{9,8},{10,11... | collective-permute-start | bytes 6291464 | tf_op jit(solution)/shard_map/ppermute | solution.py:234
  102.0 0.7 copy-start.5
  102.1 0.7 copy-start.12
  102.8 1.6 %copy-start.1 = (bf16[512,2048]{1,0:T(8,128)(2,1)S(1)}, bf16[512,2048]{1,0:T(8,128)(2,1)}, u32[]{:S(2)}) copy-start(bf16[512,2048]{1,0:T(8,128)(2,1)} %param.16) | copy-start | bytes 6291460

commit v14 on v13

--- a/solution.py
+++ b/solution.py
@@ -217,24 +217,29 @@
     scale = residues * jnp.sqrt(-jnp.expm1(-2.0 * decay_rate))
     powers = jnp.exp(-decay_rate[:, :, None] * positions)
     kernel = jnp.einsum("gm,gmt->gt", scale, powers, precision=exact_precision)
-    closing = jnp.exp(-decay_rate[:, :, None] * (width - 1.0 - positions))
 
     taps = jnp.roll(kernel[:, ::-1], 1, axis=1)
     high = lax.reduce_precision(taps, exponent_bits=8, mantissa_bits=7)
     low = lax.reduce_precision(taps - high, exponent_bits=8, mantissa_bits=7)
-    ending = two_pass("gnj,jgc->ngc", closing, kv_grouped).reshape(-1, chans)
+    modes = decay_rate.shape[1]
+    rate_lanes = jnp.broadcast_to(jnp.transpose(decay_rate)[:, :, None], (modes, groups, GROUP))
+    fine_len = 8
+    rate_rows = rate_lanes.reshape(modes, 1, 1, chans)
+
+    late = jnp.exp(
+        -rate_rows * (fine_len * (width // fine_len - 1 - jnp.arange(width // fine_len, dtype=jnp.float32)))[None, :, None, None]
+    )
+    near = jnp.exp(-rate_rows * (fine_len - 1.0 - jnp.arange(fine_len, dtype=jnp.float32))[None, None, :, None])
+    kv_rows = kv_round.astype(jnp.float32).reshape(1, width // fine_len, fine_len, chans)
+    ending = jnp.sum(late * near * kv_rows, axis=(1, 2))
 
     first, later = scan_shifts(lax.axis_size("ctx"))
     spans = jnp.asarray([1] * (len(first) - 1) + later, jnp.float32)[:, None, None] * float(width)
-    modes = decay_rate.shape[1]
-    rate_lanes = jnp.broadcast_to(jnp.transpose(decay_rate)[:, :, None], (modes, groups, GROUP))
     decay = jnp.exp(-rate_lanes.reshape(1, modes, chans) * spans)
     entering, inner = scan_states(ending, decay, high, low, kv_round)
     entering, remote = lax.optimization_barrier((entering, remote))
     weight_blocks.append((other_chip + 1 - core, lax.ppermute(remote, "core", [(0, 1), (1, 0)])))
     scale_lanes = jnp.broadcast_to(jnp.transpose(scale)[:, :, None], (modes, groups, GROUP)).reshape(modes, 1, chans)
-    fine_len = 8
-    rate_rows = rate_lanes.reshape(modes, 1, 1, chans)
     coarse = jnp.exp(-rate_rows * (fine_len * jnp.arange(width // fine_len, dtype=jnp.float32))[None, :, None, None])
     fine = jnp.exp(-rate_rows * (jnp.arange(fine_len, dtype=jnp.float32) + 1.0)[None, None, :, None])
     weighted = (scale_lanes.reshape(modes, chans) * entering)[:, None, None, :]

time: 111 us -> 110 us (level)
  Pallas kernels: 68.6 us -> 64.8 us
  other arithmetic: 8.18 us -> 11.7 us
    pallas_call x1, Pallas kernels: 68.6 us -> 64.8 us  [scan_states(): pl.pallas_call(functools.partial(scan_kernel, count, parts), out_shape=(j...]
    reduce_sum x0 -> x1, other arithmetic: none -> 2.33 us  [local(): ending = jnp.sum(late * near * kv_rows, axis=(1, 2))]
    slice x1, local copies, waits for them, and re-layouts: 1.49 us -> 0.02 us  [local(): featured_q = featurize(query_rows, tails[0:keep], feature_taps[0])]
    convert_element_type x3, other arithmetic: 1.22 us -> 2.52 us  [featurize(): values = jnp.concatenate([tail, rows], axis=0).astype(jnp.float32)]
    another operation x1, local copies, waits for them, and re-layouts: 0.63 us -> 1.85 us  [local(): weighted = (scale_lanes.reshape(modes, chans) * entering)[:, None, None, :]]
    unnamed x32 -> x14, local copies, waits for them, and re-layouts: 1.73 us -> 2.79 us
  transfers between devices with their start and end apart: 4 -> 4, of which waited for: 0 -> 0; matrix products, arithmetic and copies ran while one was open for 18% -> 20% of each run, Pallas kernels for 62% -> 59%
where the time goes in v14:
time: 110 us; the launch traced here: 109 us
  Pallas kernels  64.8 us (59%)
  starting transfers between devices  15.8 us (14%)
  other arithmetic  11.7 us (11%)
  local copies, waits for them, and re-layouts  9.87 us (9%)
  matrix products  6.96 us (6%)
    pallas_call x1, Pallas kernels, scan_states(): pl.pallas_call(functools.partial(scan_kernel, count, parts), out_shape=(j...  64.8 us
    ppermute x1, starting transfers between devices, local(): lax.ppermute(remote, 'core', [(0, 1), (1, 0)])  6.66 us
    dot_general x4, matrix products, local(): term = jnp.dot(columns, weight, preferred_element_type=jnp.float32)  5.81 us
    ppermute x1, starting transfers between devices, shifted(): return lax.ppermute(shard, axis, pairs)  3.2 us
    ppermute x1, starting transfers between devices, local(): remote = lax.ppermute(out_weight, 'zlo', pair)  3.09 us
    ppermute x1, starting transfers between devices, local(): lax.ppermute(out_weight, 'core', pair)  2.87 us
    unnamed x14, local copies, waits for them, and re-layouts  2.79 us
    convert_element_type x3, other arithmetic, featurize(): values = jnp.concatenate([tail, rows], axis=0).astype(jnp.float32)  2.52 us
  transfers between devices with their start and end apart: 4, of which 0 were waited for; matrix products, arithmetic and copies ran while one was open for 20% of the time, Pallas kernels for 59%

profile of v14, /device:TPU:389, one launch (start us, length us, event | category | flops | bytes accessed | tf_op | source)
XLA Modules:
  0.0 109.4 jit_solution(7384112385147966091)
XLA Ops:
  0.0 3.1 %collective-permute-start.1 = (bf16[512,2048]{1,0:T(8,128)(2,1)}, bf16[512,2048]{1,0:T(8,128)(2,1)}, u32[]{:S(2)}, u32[]{:S(2)}) collective-permute-start(bf16[512,2048]{1,0:T(8,128)(2,1)} %param.16), channel_id=1, source_target_pairs={{0,2},{2,0},{1,3},{3,1},{4,6},{6,4},{5,7},{7,5},{8,10},{10,8},{9,1... | collective-permute-start | bytes 6291464 | tf_op jit(solution)/shard_map/ppermute | solution.py:188
  3.1 2.9 %collective-permute-start.2 = (bf16[512,2048]{1,0:T(8,128)(2,1)}, bf16[512,2048]{1,0:T(8,128)(2,1)}, u32[]{:S(2)}, u32[]{:S(2)}) collective-permute-start(bf16[512,2048]{1,0:T(8,128)(2,1)} %param.16), channel_id=1, source_target_pairs={{0,1},{1,0},{2,3},{3,2},{4,5},{5,4},{6,7},{7,6},{8,9},{9,8},{10,11... | collective-permute-start | bytes 6291464 | tf_op jit(solution)/shard_map/ppermute | solution.py:191
  6.0 0.8 slice_bitcast_fusion.2
  6.8 0.8 slice_bitcast_fusion
  7.6 3.2 %collective-permute-start = (bf16[6,2048]{1,0:T(8,128)(2,1)S(1)}, bf16[6,2048]{1,0:T(8,128)(2,1)S(1)}, u32[]{:S(2)}, u32[]{:S(2)}) collective-permute-start(bf16[6,2048]{1,0:T(8,128)(2,1)S(1)} %pad_maximum_fusion.1), channel_id=1, source_target_pairs={{0,4},{4,8},{8,12},{12,16},{16,20},{20,24},{24,28},{28,32},{32,36}... | collective-permute-start | bytes 73736 | tf_op jit(solution)/shard_map/ppermute | solution.py:19
  10.8 1.0 fusion.33
  11.8 0.7 fusion.27
  12.9 0.6 neg.31
  13.7 1.2 %fusion.15 = f32[128,1,128]{2,1,0:T(1,128)S(1)} fusion(f32[128,16,1]{1,2,0:T(1,128)S(1)} %copy.13, f32[128,16]{1,0:T(8,128)S(1)} %copy.12), kind=kOutput, calls=%fused_computation.34 | convolution fusion | flops 3407872 | bytes 81920 | tf_op jit(solution)/shard_map/gm,gmt->gt/dot_general | solution.py:219
  15.7 1.7 %multiply_exponential_fusion.1 = (f32[16,8,2048]{2,1,0:T(8,128)}, f32[16,8,2048]{2,1,0:T(8,128)}) fusion(f32[8]{0:T(128)S(1)} %get-tuple-element.35, f32[16,2048]{1,0:T(8,128)S(1)} %neg.31, f32[8]{0:T(128)S(1)} %get-tuple-element.36), kind=kLoop, calls=%fused_computation.33 | loop fusion | flops 524288 | bytes 2228288 | tf_op jit(solution)/shard_map/exp | solution.py:244
  18.0 1.3 %broadcast_in_dim.7 = f32[16,128,16]{2,1,0:T(8,128)} broadcast(f32[16,128]{1,0:T(8,128)S(1)} %get-tuple-element.29), dimensions={0,1} | broadcast | bytes 139264 | tf_op jit(solution)/shard_map/broadcast_in_dim | solution.py:242
  19.4 1.8 %reshape_reshape.3 = f32[16,2048]{1,0:T(8,128)S(1)} reshape(f32[16,128,16]{2,1,0:T(8,128)} %broadcast_in_dim.7) | data formatting | bytes 262144 | tf_op jit(solution)/shard_map/reshape;reshape | solution.py:245
  21.2 1.2 %maximum_convert_fusion.1 = f32[130,2048]{1,0:T(8,128)S(1)} fusion(bf16[128,2048]{1,0:T(8,128)(2,1)} %bitcast.40, bf16[2,2048]{1,0:T(2,128)(2,1)S(1)} %get-tuple-element.28), kind=kLoop, calls=%fused_computation.41 | loop fusion | flops 1064960 | bytes 1597440 | tf_op jit(solution)/shard_map/convert_element_type | solution.py:23
  22.4 1.2 %maximum_convert_fusion.2 = f32[130,2048]{1,0:T(8,128)S(1)} fusion(bf16[128,2048]{1,0:T(8,128)(2,1)} %bitcast.41, bf16[2,2048]{1,0:T(2,128)(2,1)S(1)} %get-tuple-element.27), kind=kLoop, calls=%fused_computation.42 | loop fusion | flops 1064960 | bytes 1597440 | tf_op jit(solution)/shard_map/convert_element_type | solution.py:23
  23.6 0.7 fusion.8.kv_ref
  24.4 1.1 %copy-done.1 = f32[16,8,2048]{2,1,0:T(8,128)S(1)} copy-done((f32[16,8,2048]{2,1,0:T(8,128)S(1)}, f32[16,8,2048]{2,1,0:T(8,128)}, u32[]{:S(2)}) %copy-start.1) | copy-done | bytes 1048600
  25.5 2.3 %multiply_reduce_fusion.1.ending_ref = f32[16,2048]{1,0:T(8,128)S(1)} fusion(f32[16,8,2048]{2,1,0:T(8,128)S(1)} %convert_bitcast_fusion, f32[16,8,2048]{2,1,0:T(8,128)S(1)} %copy-done.1, f32[16,16,2048]{2,1,0:T(8,128)S(1)} %multiply_exponential_fusion), kind=kLoop, calls=%fused_computation.1 | loop fusion | flops 12550144 | bytes 4325376 | tf_op jit(solution)/shard_map/reduce_sum | solution.py:234
  27.9 64.8 %shard_map.91 = (f32[16,2048]{1,0:T(8,128)S(1)}, f32[128,2048]{1,0:T(8,128)S(1)}) custom-call(f32[16,2048]{1,0:T(8,128)S(1)} %multiply_reduce_fusion.1.ending_ref, f32[7,16,2048]{2,1,0:T(8,128)S(1)} %multiply_exponential_fusion.3.decay_ref, f32[128,128]{1,0:T(8,128)S(1)} %get-tuple-element.16.high_ref, f32[128,128]{1,0:T(8,128)S(1)} %get-tuple-element.15.low_ref, ...), custom_call_target="tpu_custom_call" | custom-call | tf_op jit(solution)/shard_map/pallas_call | solution.py:162
  92.8 6.7 %collective-permute-start.3 = (bf16[512,2048]{1,0:T(8,128)(2,1)}, bf16[512,2048]{1,0:T(8,128)(2,1)S(1)}, u32[]{:S(2)}, u32[]{:S(2)}) collective-permute-start(bf16[512,2048]{1,0:T(8,128)(2,1)} %collective-permute-done.1), channel_id=1, source_target_pairs={{0,1},{1,0},{2,3},{3,2},{4,5},{5,4},{6,7},{7,6},{8,9},{9,8},{10,11... | collective-permute-start | bytes 6291464 | tf_op jit(solution)/shard_map/ppermute | solution.py:241
  99.9 1.4 %multiply_reduce_fusion = f32[16,8,2048]{2,1,0:T(8,128)S(1)} fusion(f32[16,8,2048]{2,1,0:T(8,128)S(1)} %copy-done, f32[16,16,2048]{2,1,0:T(8,128)S(1)} %exponential_multiply_fusion), kind=kLoop, calls=%fused_computation | loop fusion | flops 8126464 | bytes 4194304 | tf_op jit(solution)/shard_map/reduce_sum | solution.py:246
  101.4 0.6 copy-done.4
  102.5 1.1 copy-done.2
  104.0 2.0 %convolution_add_fusion.1 = f32[128,2048]{1,0:T(8,128)S(1)} fusion(f32[128,2048]{1,0:T(8,128)S(1)} %fusion.24, bf16[512,2048]{1,0:T(8,128)(2,1)} %collective-permute-done.2, bf16[128,2048]{1,0:T(8,128)(2,1)S(1)} %fusion.5, s32[]{:T(128)S(6)} %select_n.13), kind=kOutput, calls=%fused_computation.4 | convolution fusion | flops 268697600 | bytes 4325380 | tf_op jit(solution)/shard_map/dot_general | solution.py:256
  106.5 2.9 %fusion.2 = bf16[1,128,2048]{2,1,0:T(8,128)(2,1)} fusion(f32[128,2048]{1,0:T(8,128)S(1)} %fusion.20, f32[128,2048]{1,0:T(8,128)S(1)} %convolution_add_fusion.1, bf16[512,2048]{1,0:T(8,128)(2,1)} %collective-permute-done.1, bf16[128,2048]{1,0:T(8,128)(2,1)S(1)} %fusion.5, s32[]{:T(128)S(6)} %select_n.14), kind=kOutput, calls=%fused_computation.6 | convolution fusion | flops 269221888 | bytes 4849668 | tf_op jit(solution)/shard_map/dot_general | solution.py:256
  (36 shorter events, 4.1 us)
Async XLA Ops:
  0.0 92.8 %collective-permute-start.1 = (bf16[512,2048]{1,0:T(8,128)(2,1)}, bf16[512,2048]{1,0:T(8,128)(2,1)}, u32[]{:S(2)}, u32[]{:S(2)}) collective-permute-start(bf16[512,2048]{1,0:T(8,128)(2,1)} %param.16), channel_id=1, source_target_pairs={{0,2},{2,0},{1,3},{3,1},{4,6},{6,4},{5,7},{7,5},{8,10},{10,8},{9,1... | collective-permute-start | bytes 6291464 | tf_op jit(solution)/shard_map/ppermute | solution.py:188
  3.1 100.9 %collective-permute-start.2 = (bf16[512,2048]{1,0:T(8,128)(2,1)}, bf16[512,2048]{1,0:T(8,128)(2,1)}, u32[]{:S(2)}, u32[]{:S(2)}) collective-permute-start(bf16[512,2048]{1,0:T(8,128)(2,1)} %param.16), channel_id=1, source_target_pairs={{0,1},{1,0},{2,3},{3,2},{4,5},{5,4},{6,7},{7,6},{8,9},{9,8},{10,11... | collective-permute-start | bytes 6291464 | tf_op jit(solution)/shard_map/ppermute | solution.py:191
  7.6 13.6 %collective-permute-start = (bf16[6,2048]{1,0:T(8,128)(2,1)S(1)}, bf16[6,2048]{1,0:T(8,128)(2,1)S(1)}, u32[]{:S(2)}, u32[]{:S(2)}) collective-permute-start(bf16[6,2048]{1,0:T(8,128)(2,1)S(1)} %pad_maximum_fusion.1), channel_id=1, source_target_pairs={{0,4},{4,8},{8,12},{12,16},{16,20},{20,24},{24,28},{28,32},{32,36}... | collective-permute-start | bytes 73736 | tf_op jit(solution)/shard_map/ppermute | solution.py:19
  13.5 2.0 %copy-start.6 = (f32[7]{0:T(128)S(1)}, f32[7]{0:T(128)}, u32[]{:S(2)}) copy-start(f32[7]{0:T(128)} %constant.36) | copy-start | bytes 88
  24.3 1.2 %copy-start.1 = (f32[16,8,2048]{2,1,0:T(8,128)S(1)}, f32[16,8,2048]{2,1,0:T(8,128)}, u32[]{:S(2)}) copy-start(f32[16,8,2048]{2,1,0:T(8,128)} %get-tuple-element.14) | copy-start | bytes 3145732
  25.5 67.1 %copy-start.3 = (bf16[1,128,2048]{2,1,0:T(8,128)(2,1)S(1)}, bf16[1,128,2048]{2,1,0:T(8,128)(2,1)}, u32[]{:S(2)}) copy-start(bf16[1,128,2048]{2,1,0:T(8,128)(2,1)} %param.9) | copy-start | bytes 1572868
  27.9 71.7 %copy-start.5 = (f32[16]{0:T(128)S(1)}, f32[16]{0:T(128)}, u32[]{:S(2)}) copy-start(f32[16]{0:T(128)} %iota_multiply_fusion) | copy-start | bytes 196
  92.7 7.2 %copy-start = (f32[16,8,2048]{2,1,0:T(8,128)S(1)}, f32[16,8,2048]{2,1,0:T(8,128)}, u32[]{:S(2)}) copy-start(f32[16,8,2048]{2,1,0:T(8,128)} %get-tuple-element.13) | copy-start | bytes 3145732
  92.8 13.2 %collective-permute-start.3 = (bf16[512,2048]{1,0:T(8,128)(2,1)}, bf16[512,2048]{1,0:T(8,128)(2,1)S(1)}, u32[]{:S(2)}, u32[]{:S(2)}) collective-permute-start(bf16[512,2048]{1,0:T(8,128)(2,1)} %collective-permute-done.1), channel_id=1, source_target_pairs={{0,1},{1,0},{2,3},{3,2},{4,5},{5,4},{6,7},{7,6},{8,9},{9,8},{10,11... | collective-permute-start | bytes 6291464 | tf_op jit(solution)/shard_map/ppermute | solution.py:241
  101.3 0.7 copy-start.4
  102.0 1.6 %copy-start.2 = (bf16[512,2048]{1,0:T(8,128)(2,1)S(1)}, bf16[512,2048]{1,0:T(8,128)(2,1)}, u32[]{:S(2)}) copy-start(bf16[512,2048]{1,0:T(8,128)(2,1)} %param.16) | copy-start | bytes 6291460
